TPU v7x, 32 devices: a whole 2x2x4 slice. The times are simulated.
32 devices in a mesh: dp: 4 (over x, core), fsdp: 8 (over z, y).
Axes of the slice: x: 2, y: 2, z: 4, core: 2. Of those that a mesh axis runs over, the one named last changes fastest.
Arguments:
- x_short: bfloat16 [32, 256, 1152], P(('dp', 'fsdp')), may hold values from -6 to 6
- x_long: bfloat16 [8192, 1152], P(('dp', 'fsdp')), may hold values from -6 to 6
- short_cond: float32 [32, 1152], P(('dp', 'fsdp')), may hold values from -6 to 6
- long_cond: float32 [8, 1152], P('dp'), may hold values from -6 to 6
- short_heads: int32 [32, 16], P(('dp', 'fsdp')), may hold values 0 or 1
- long_heads: int32 [8, 16], P('dp'), may hold values 0 or 1
- short_groups: int32 [32, 36], P(('dp', 'fsdp')), may hold values 0 or 1
- long_groups: int32 [8, 36], P('dp'), may hold values 0 or 1
- short_keep: int32 [32, 256], P(('dp', 'fsdp')), may hold values 0 or 1
- long_keep: int32 [8192], P(('dp', 'fsdp')), may hold values 0 or 1
- w_ada: bfloat16 [1152, 6912], P('fsdp'), may hold values from -0.1875 to 0.1875
- b_ada: bfloat16 [6912], P('fsdp'), may hold values from -2 to 2
- w_head_router: bfloat16 [1152, 16], P('fsdp'), may hold values from -0.375 to 0.375
- w_group_router: bfloat16 [1152, 36], P('fsdp'), may hold values from -0.375 to 0.375
- w_qkv: bfloat16 [1152, 3456], P('fsdp'), may hold values from -0.1875 to 0.1875
- w_proj: bfloat16 [1152, 1152], P('fsdp'), may hold values from -1.5 to 1.5
- b_proj: bfloat16 [1152], P('fsdp'), may hold values from -2 to 2
- w_fc1: bfloat16 [1152, 4608], P('fsdp'), may hold values from -0.1875 to 0.1875
- b_fc1: bfloat16 [4608], P('fsdp'), may hold values from -2 to 2
- w_fc2: bfloat16 [4608, 1152], P('fsdp'), may hold values from -0.09375 to 0.09375
- b_fc2: bfloat16 [1152], P('fsdp'), may hold values from -2 to 2
- g_short: bfloat16 [32, 256, 1152], P(('dp', 'fsdp')), may hold values from -6 to 6
- g_long: bfloat16 [8192, 1152], P(('dp', 'fsdp')), may hold values from -6 to 6
Outputs:
- y_short: bfloat16 [32, 256, 1152], P(('dp', 'fsdp'))
- y_long: bfloat16 [8192, 1152], P(('dp', 'fsdp'))
- dx_short: bfloat16 [32, 256, 1152], P(('dp', 'fsdp'))
- dx_long: bfloat16 [8192, 1152], P(('dp', 'fsdp'))
- d_short_cond: float32 [32, 1152], P(('dp', 'fsdp'))
- d_long_cond: float32 [8, 1152], P('dp')
- g_w_ada: float32 [1152, 6912], P('fsdp')
- g_b_ada: float32 [6912], P('fsdp')
- g_w_head_router: float32 [1152, 16], P('fsdp')
- g_w_group_router: float32 [1152, 36], P('fsdp')
- g_w_qkv: float32 [1152, 3456], P('fsdp')
- g_w_proj: float32 [1152, 1152], P('fsdp')
- g_b_proj: float32 [1152], P('fsdp')
- g_w_fc1: float32 [1152, 4608], P('fsdp')
- g_b_fc1: float32 [4608], P('fsdp')
- g_w_fc2: float32 [4608, 1152], P('fsdp')
- g_b_fc2: float32 [1152], P('fsdp')
All inputs are finite; a program needn't handle non-finite values. No bound on the sum of `short_heads` or of `long_heads` or of `short_groups` or of `long_groups` or of `short_keep` or of `long_keep` on one device may be relied on, other than what follows from the above.
Results may differ from a plain program's by a relative error of at most 0.019.
Values may be sent and summed in bfloat16 or wider, within the bound.
A program may use at most 320 MiB of HBM per device.

v0:
```python
import jax
import jax.numpy as jnp
from jax import lax
from jax.sharding import PartitionSpec as P

CHAN = 128
SPLIT = 4


epsilon = 1e-06


def from_partner(value, axis, stride):
    mask = 2**stride
    pairs = [(source, source ^ mask) for source in range(lax.axis_size(axis))]
    return lax.ppermute(value, axis, pairs)


def shortened(value):

    def short(part):
        return part.astype(jnp.bfloat16) if part.dtype == jnp.float32 else part

    return jax.tree.map(short, value)


def product(left, right):
    return jnp.dot(left, right, preferred_element_type=jnp.float32)


def product_tn(left, right):
    return lax.dot_general(
        left, right, (((0,), (0,)), ((), ())), preferred_element_type=jnp.float32
    )


def product_nt(left, right):
    return lax.dot_general(
        left, right, (((1,), (1,)), ((), ())), preferred_element_type=jnp.float32
    )


def spread(per_slot, short_count, len_short, quarter_rows):
    width = per_slot.shape[1]
    short_part = jnp.broadcast_to(
        per_slot[:short_count, None, :], (short_count, len_short, width)
    ).reshape(short_count * len_short, width)
    long_part = jnp.broadcast_to(per_slot[short_count:], (quarter_rows, width))
    return jnp.concatenate([short_part, long_part], 0)


def slot_sum(values, short_count, len_short):
    short_rows = short_count * len_short
    short_part = jnp.sum(
        values[:short_rows].reshape((short_count, len_short) + values.shape[1:]), axis=1
    )
    long_part = jnp.sum(values[short_rows:], axis=0, keepdims=True)
    return jnp.concatenate([short_part, long_part], 0)


def norm_parts(values):
    average = jnp.mean(values, axis=-1, keepdims=True)
    centred = values - average
    variance = jnp.mean(centred * centred, axis=-1, keepdims=True)
    inverse = lax.rsqrt(variance + epsilon)
    return (centred * inverse, inverse)


def norm_back(gradient, normed, inverse):
    return inverse * (
        gradient
        - jnp.mean(gradient, axis=-1, keepdims=True)
        - normed * jnp.mean(gradient * normed, axis=-1, keepdims=True)
    )


def silu_grad(values):
    sigmoid_value = jax.nn.sigmoid(values)
    return sigmoid_value * (1.0 + values * (1.0 - sigmoid_value))


def attend(queries, key_rows, value_rows, scaling):
    scores = (
        jnp.einsum("nqhe,nkhe->nhqk", queries, key_rows, preferred_element_type=jnp.float32)
        * scaling
    )
    row_max = jnp.max(scores, axis=-1, keepdims=True)
    exponent = jnp.exp(scores - row_max)
    row_total = jnp.sum(exponent, axis=-1, keepdims=True)
    soft_weights = exponent / row_total
    head_out = jnp.einsum(
        "nhqk,nkhe->nqhe",
        soft_weights.astype(jnp.bfloat16),
        value_rows,
        preferred_element_type=jnp.float32,
    )
    return (head_out, row_max + jnp.log(row_total))


def attend_back(queries, key_rows, value_rows, log_total, d_out, scaling):
    scores = (
        jnp.einsum("nqhe,nkhe->nhqk", queries, key_rows, preferred_element_type=jnp.float32)
        * scaling
    )
    soft_weights = jnp.exp(scores - log_total)
    d_weights = jnp.einsum("nqhe,nkhe->nhqk", d_out, value_rows, preferred_element_type=jnp.float32)
    inner = jnp.sum(soft_weights * d_weights, axis=-1, keepdims=True)
    d_scores = (soft_weights * (d_weights - inner)).astype(jnp.bfloat16)
    d_queries = (
        jnp.einsum("nhqk,nkhe->nqhe", d_scores, key_rows, preferred_element_type=jnp.float32)
        * scaling
    )
    d_keys = (
        jnp.einsum("nhqk,nqhe->nkhe", d_scores, queries, preferred_element_type=jnp.float32)
        * scaling
    )
    d_values = jnp.einsum(
        "nhqk,nqhe->nkhe",
        soft_weights.astype(jnp.bfloat16),
        d_out,
        preferred_element_type=jnp.float32,
    )
    return (d_queries, d_keys, d_values)


def gelu_tanh(values):
    return jax.nn.gelu(values, approximate=True)


def per_device(
    x_short,
    x_long,
    short_cond,
    long_cond,
    short_heads,
    long_heads,
    short_groups,
    long_groups,
    short_keep,
    long_keep,
    w_ada,
    b_ada,
    w_head_router,
    w_group_router,
    w_qkv,
    w_proj,
    b_proj,
    w_fc1,
    b_fc1,
    w_fc2,
    b_fc2,
    g_short,
    g_long,
):
    short_count, len_short, model_width = x_short.shape
    quarter_rows = x_long.shape[0]
    head_count = w_head_router.shape[1]
    head_width = model_width // head_count
    group_count = w_group_router.shape[1]
    slot_count = short_count + 1
    short_rows = short_count * len_short
    row_count = short_rows + quarter_rows
    scaling = head_width ** (-0.5)
    fsdp_index = lax.axis_index("fsdp")
    fsdp_count = lax.axis_size("fsdp")
    group_row = fsdp_index // SPLIT
    first_member = (fsdp_index % SPLIT == 0).astype(jnp.bfloat16)
    group_total = fsdp_count // SPLIT
    first_set = (w_ada, b_ada, w_head_router, w_group_router, w_qkv, w_proj, b_proj)
    second_set = (w_fc1, b_fc1, w_fc2, b_fc2)
    ada_full, ada_bias, head_router, group_router, qkv_full, proj_full, proj_bias = (
        lax.all_gather(first_set[0], "fsdp", axis=0, tiled=True),
        lax.all_gather(first_set[1], "fsdp", axis=0, tiled=True),
        lax.all_gather(first_set[2], "fsdp", axis=0, tiled=True),
        lax.all_gather(first_set[3], "fsdp", axis=0, tiled=True),
        lax.all_gather(first_set[4], "fsdp", axis=0, tiled=True),
        lax.all_gather(first_set[5], "fsdp", axis=0, tiled=True),
        lax.all_gather(first_set[6], "fsdp", axis=0, tiled=True),
    )
    condition = jnp.concatenate(
        [short_cond, lax.dynamic_slice_in_dim(long_cond, group_row, 1, 0)], 0
    )
    head_mask = jnp.concatenate(
        [short_heads, lax.dynamic_slice_in_dim(long_heads, group_row, 1, 0)], 0
    ).astype(jnp.float32)
    group_mask = jnp.concatenate(
        [short_groups, lax.dynamic_slice_in_dim(long_groups, group_row, 1, 0)], 0
    ).astype(jnp.float32)
    silu_act = jax.nn.silu(condition).astype(jnp.bfloat16)
    modulation = product(silu_act, ada_full) + ada_bias.astype(jnp.float32)
    head_sigmoid = jax.nn.sigmoid(product(silu_act, head_router))
    group_sigmoid = jax.nn.sigmoid(product(silu_act, group_router))
    head_gate = head_mask * 2.0 * head_sigmoid
    group_gate = group_mask * 2.0 * group_sigmoid
    shift1, scale1, gate1, shift2, scale2, gate2 = jnp.split(
        spread(modulation, short_count, len_short, quarter_rows), 6, axis=1
    )
    x_rows = jnp.concatenate([x_short.reshape(short_rows, model_width), x_long], 0).astype(
        jnp.float32
    )
    keep_rows = jnp.concatenate([short_keep.reshape(short_rows), long_keep], 0).astype(jnp.float32)[
        :, None
    ]
    normed1, inverse1 = norm_parts(x_rows)
    hidden1 = (normed1 * (1.0 + scale1) + shift1).astype(jnp.bfloat16)
    qkv_rows = product(hidden1, qkv_full).astype(jnp.bfloat16)
    short_qkv = qkv_rows[:short_rows].reshape(short_count, len_short, 3, head_count, head_width)
    short_out, short_log = attend(
        short_qkv[:, :, 0], short_qkv[:, :, 1], short_qkv[:, :, 2], scaling
    )
    long_qkv = qkv_rows[short_rows:]
    own_kv = long_qkv[:, model_width:]
    partner_kv = from_partner(own_kv, "fsdp", 0)
    near_rows = jnp.concatenate([own_kv, partner_kv], 0)
    far_rows = from_partner(near_rows, "fsdp", 1)
    group_kv = jnp.concatenate([near_rows, far_rows], 0)
    long_queries = long_qkv[:, :model_width].reshape(1, quarter_rows, head_count, head_width)
    long_keys = group_kv[:, :model_width].reshape(1, SPLIT * quarter_rows, head_count, head_width)
    long_values = group_kv[:, model_width:].reshape(1, SPLIT * quarter_rows, head_count, head_width)
    long_out, long_log = attend(long_queries, long_keys, long_values, scaling)
    head_rows = jnp.concatenate(
        [
            short_out.reshape(short_rows, head_count, head_width),
            long_out.reshape(quarter_rows, head_count, head_width),
        ],
        0,
    )
    head_gate_rows = spread(head_gate, short_count, len_short, quarter_rows)[:, :, None]
    attention = (head_rows * head_gate_rows).reshape(row_count, model_width).astype(jnp.bfloat16)
    projected = product(attention, proj_full) + proj_bias.astype(jnp.float32)
    mixed = x_rows + gate1 * projected
    fc1_full, fc1_bias, fc2_full, fc2_bias = (
        lax.all_gather(second_set[0], "fsdp", axis=0, tiled=True),
        lax.all_gather(second_set[1], "fsdp", axis=0, tiled=True),
        lax.all_gather(second_set[2], "fsdp", axis=0, tiled=True),
        lax.all_gather(second_set[3], "fsdp", axis=0, tiled=True),
    )
    normed2, inverse2 = norm_parts(mixed)
    hidden2 = (normed2 * (1.0 + scale2) + shift2).astype(jnp.bfloat16)
    up_rows = product(hidden2, fc1_full) + fc1_bias.astype(jnp.float32)
    gelu_value, gelu_pull = jax.vjp(gelu_tanh, up_rows)
    channel_gate = spread(
        jnp.repeat(group_gate, CHAN, axis=1), short_count, len_short, quarter_rows
    )
    activated = (gelu_value * channel_gate).astype(jnp.bfloat16)
    down_rows = product(activated, fc2_full) + fc2_bias.astype(jnp.float32)
    out_rows = mixed + gate2 * keep_rows * down_rows
    y_short = out_rows[:short_rows].reshape(x_short.shape).astype(jnp.bfloat16)
    y_long = out_rows[short_rows:].astype(jnp.bfloat16)
    fc1_back, fc1_unused, fc2_back, fc2_unused = (
        lax.all_gather(second_set[0], "fsdp", axis=0, tiled=True),
        lax.all_gather(second_set[1], "fsdp", axis=0, tiled=True),
        lax.all_gather(second_set[2], "fsdp", axis=0, tiled=True),
        lax.all_gather(second_set[3], "fsdp", axis=0, tiled=True),
    )
    ada_back, ada_unused, head_back, group_back, qkv_back, proj_back, proj_unused = (
        lax.all_gather(first_set[0], "fsdp", axis=0, tiled=True),
        lax.all_gather(first_set[1], "fsdp", axis=0, tiled=True),
        lax.all_gather(first_set[2], "fsdp", axis=0, tiled=True),
        lax.all_gather(first_set[3], "fsdp", axis=0, tiled=True),
        lax.all_gather(first_set[4], "fsdp", axis=0, tiled=True),
        lax.all_gather(first_set[5], "fsdp", axis=0, tiled=True),
        lax.all_gather(first_set[6], "fsdp", axis=0, tiled=True),
    )
    gradient = jnp.concatenate([g_short.reshape(short_rows, model_width), g_long], 0).astype(
        jnp.float32
    )
    d_down = (gradient * gate2 * keep_rows).astype(jnp.bfloat16)
    slot_gate2 = slot_sum(gradient * keep_rows * down_rows, short_count, len_short)
    grad_fc2 = product_tn(activated, d_down)
    grad_fc2_bias = jnp.sum(d_down, axis=0, dtype=jnp.float32)
    d_activated = product_nt(d_down, fc2_back)
    d_channel = slot_sum(d_activated * gelu_value, short_count, len_short)
    d_group = jnp.sum(d_channel.reshape(slot_count, group_count, CHAN), axis=-1)
    d_up = gelu_pull(d_activated * channel_gate)[0].astype(jnp.bfloat16)
    grad_fc1 = product_tn(hidden2, d_up)
    grad_fc1_bias = jnp.sum(d_up, axis=0, dtype=jnp.float32)
    d_hidden2 = product_nt(d_up, fc1_back)
    slot_shift2 = slot_sum(d_hidden2, short_count, len_short)
    slot_scale2 = slot_sum(d_hidden2 * normed2, short_count, len_short)
    d_mixed = gradient + norm_back(d_hidden2 * (1.0 + scale2), normed2, inverse2)
    mlp_shards = (
        lax.psum_scatter(
            grad_fc1.astype(jnp.bfloat16), "fsdp", scatter_dimension=0, tiled=True
        ).astype(jnp.float32),
        lax.psum_scatter(
            grad_fc1_bias.astype(jnp.bfloat16), "fsdp", scatter_dimension=0, tiled=True
        ).astype(jnp.float32),
        lax.psum_scatter(
            grad_fc2.astype(jnp.bfloat16), "fsdp", scatter_dimension=0, tiled=True
        ).astype(jnp.float32),
        lax.psum_scatter(
            grad_fc2_bias.astype(jnp.bfloat16), "fsdp", scatter_dimension=0, tiled=True
        ).astype(jnp.float32),
    )
    d_projected = (d_mixed * gate1).astype(jnp.bfloat16)
    slot_gate1 = slot_sum(d_mixed * projected, short_count, len_short)
    grad_proj = product_tn(attention, d_projected)
    grad_proj_bias = jnp.sum(d_projected, axis=0, dtype=jnp.float32)
    d_attention = product_nt(d_projected, proj_back).reshape(row_count, head_count, head_width)
    d_head = slot_sum(jnp.sum(d_attention * head_rows, axis=-1), short_count, len_short)
    d_heads = (d_attention * head_gate_rows).astype(jnp.bfloat16)
    short_dq, short_dk, short_dv = attend_back(
        short_qkv[:, :, 0],
        short_qkv[:, :, 1],
        short_qkv[:, :, 2],
        short_log,
        d_heads[:short_rows].reshape(short_count, len_short, head_count, head_width),
        scaling,
    )
    long_dq, long_dk, long_dv = attend_back(
        long_queries,
        long_keys,
        long_values,
        long_log,
        d_heads[short_rows:].reshape(1, quarter_rows, head_count, head_width),
        scaling,
    )
    kv_grad = jnp.concatenate(
        [
            long_dk.reshape(SPLIT * quarter_rows, model_width),
            long_dv.reshape(SPLIT * quarter_rows, model_width),
        ],
        1,
    )
    returned_far = from_partner(kv_grad[2 * quarter_rows :].astype(jnp.bfloat16), "fsdp", 1).astype(
        jnp.float32
    )
    near_grad = kv_grad[: 2 * quarter_rows] + returned_far
    returned_pair = from_partner(shortened(near_grad[quarter_rows:]), "fsdp", 0)
    own_kv_grad = near_grad[:quarter_rows] + returned_pair
    short_dqkv = jnp.concatenate(
        [
            short_dq.reshape(short_rows, model_width),
            short_dk.reshape(short_rows, model_width),
            short_dv.reshape(short_rows, model_width),
        ],
        1,
    )
    long_dqkv = jnp.concatenate([long_dq.reshape(quarter_rows, model_width), own_kv_grad], 1)
    d_qkv = jnp.concatenate([short_dqkv, long_dqkv], 0).astype(jnp.bfloat16)
    grad_qkv = product_tn(hidden1, d_qkv)
    d_hidden1 = product_nt(d_qkv, qkv_back)
    slot_shift1 = slot_sum(d_hidden1, short_count, len_short)
    slot_scale1 = slot_sum(d_hidden1 * normed1, short_count, len_short)
    d_rows = d_mixed + norm_back(d_hidden1 * (1.0 + scale1), normed1, inverse1)
    dx_short = d_rows[:short_rows].reshape(x_short.shape).astype(jnp.bfloat16)
    dx_long = d_rows[short_rows:].astype(jnp.bfloat16)
    d_modulation = jnp.concatenate(
        [slot_shift1, slot_scale1, slot_gate1, slot_shift2, slot_scale2, slot_gate2], 1
    )
    d_head_logit = d_head * head_mask * 2.0 * head_sigmoid * (1.0 - head_sigmoid)
    d_group_logit = d_group * group_mask * 2.0 * group_sigmoid * (1.0 - group_sigmoid)
    placement = (jnp.arange(group_total) == group_row).astype(jnp.float32)[:, None]
    long_mod_sum, long_head_sum, long_group_sum = (
        lax.psum((placement * d_modulation[short_count:]).astype(jnp.bfloat16), "fsdp").astype(
            jnp.float32
        ),
        lax.psum((placement * d_head_logit[short_count:]).astype(jnp.bfloat16), "fsdp").astype(
            jnp.float32
        ),
        lax.psum((placement * d_group_logit[short_count:]).astype(jnp.bfloat16), "fsdp").astype(
            jnp.float32
        ),
    )
    long_mod_low = long_mod_sum.astype(jnp.bfloat16)
    long_head_low = long_head_sum.astype(jnp.bfloat16)
    long_group_low = long_group_sum.astype(jnp.bfloat16)
    short_mod_low = d_modulation[:short_count].astype(jnp.bfloat16)
    short_head_low = d_head_logit[:short_count].astype(jnp.bfloat16)
    short_group_low = d_group_logit[:short_count].astype(jnp.bfloat16)
    d_silu_short = (
        product_nt(short_mod_low, ada_back)
        + product_nt(short_head_low, head_back)
        + product_nt(short_group_low, group_back)
    )
    d_short_cond = d_silu_short * silu_grad(short_cond)
    d_silu_long = (
        product_nt(long_mod_low, ada_back)
        + product_nt(long_head_low, head_back)
        + product_nt(long_group_low, group_back)
    )
    d_long_cond = d_silu_long * silu_grad(long_cond)
    factor_mod = jnp.concatenate(
        [short_mod_low, lax.dynamic_slice_in_dim(long_mod_low, group_row, 1, 0) * first_member], 0
    )
    factor_head = jnp.concatenate(
        [short_head_low, lax.dynamic_slice_in_dim(long_head_low, group_row, 1, 0) * first_member], 0
    )
    factor_group = jnp.concatenate(
        [short_group_low, lax.dynamic_slice_in_dim(long_group_low, group_row, 1, 0) * first_member],
        0,
    )
    attention_terms = (grad_qkv, grad_proj, grad_proj_bias)
    attention_terms = attention_terms + (
        product_tn(silu_act, factor_mod),
        jnp.sum(factor_mod, axis=0, dtype=jnp.float32),
        product_tn(silu_act, factor_head),
        product_tn(silu_act, factor_group),
    )
    attention_shards = jax.tree.map(
        lambda part: part.astype(jnp.float32),
        lax.psum_scatter(shortened(attention_terms), "fsdp", scatter_dimension=0, tiled=True),
    )
    summed = jax.tree.map(
        lambda part: part.astype(jnp.float32),
        lax.psum(shortened(attention_shards + mlp_shards), "dp"),
    )
    g_w_qkv, g_w_proj, g_b_proj = (summed[0], summed[1], summed[2])
    g_w_fc1, g_b_fc1, g_w_fc2, g_b_fc2 = (summed[-4], summed[-3], summed[-2], summed[-1])
    g_w_ada, g_b_ada, g_w_head_router, g_w_group_router = (
        summed[3],
        summed[4],
        summed[5],
        summed[6],
    )
    return (
        y_short,
        y_long,
        dx_short,
        dx_long,
        d_short_cond,
        d_long_cond,
        g_w_ada,
        g_b_ada,
        g_w_head_router,
        g_w_group_router,
        g_w_qkv,
        g_w_proj,
        g_b_proj,
        g_w_fc1,
        g_b_fc1,
        g_w_fc2,
        g_b_fc2,
    )


def solution(mesh):
    return jax.shard_map(
        per_device,
        mesh=mesh,
        in_specs=(
            P(("dp", "fsdp"), None, None),
            P(("dp", "fsdp"), None),
            P(("dp", "fsdp"), None),
            P("dp", None),
            P(("dp", "fsdp"), None),
            P("dp", None),
            P(("dp", "fsdp"), None),
            P("dp", None),
            P(("dp", "fsdp"), None),
            P(("dp", "fsdp")),
            P("fsdp", None),
            P("fsdp"),
            P("fsdp", None),
            P("fsdp", None),
            P("fsdp", None),
            P("fsdp", None),
            P("fsdp"),
            P("fsdp", None),
            P("fsdp"),
            P("fsdp", None),
            P("fsdp"),
            P(("dp", "fsdp"), None, None),
            P(("dp", "fsdp"), None),
        ),
        out_specs=(
            P(("dp", "fsdp"), None, None),
            P(("dp", "fsdp"), None),
            P(("dp", "fsdp"), None, None),
            P(("dp", "fsdp"), None),
            P(("dp", "fsdp"), None),
            P("dp", None),
            P("fsdp", None),
            P("fsdp"),
            P("fsdp", None),
            P("fsdp", None),
            P("fsdp", None),
            P("fsdp", None),
            P("fsdp"),
            P("fsdp", None),
            P("fsdp"),
            P("fsdp", None),
            P("fsdp"),
        ),
        check_vma=False,
    )
```

profile of v0, /device:TPU:0, one launch (start us, length us, event | category | flops | bytes accessed | tf_op | source)
XLA Modules:
  0.0 2054.6 jit_solution(11012720955627643343)
XLA Ops:
  14.4 40.8 %all-reduce.9 = (bf16[6912]{0:T(1024)(128)(2,1)S(1)}, bf16[1152]{0:T(1024)(128)(2,1)S(1)}, bf16[1152]{0:T(1024)(128)(2,1)S(1)}, bf16[4608]{0:T(1024)(128)(2,1)S(1)}) all-reduce(bf16[6912]{0:T(1024)(128)(2,1)S(1)} %dynamic-update-slice, bf16[1152]{0:T(1024)(128)(2,1)S(1)} %dynamic-update-slice.1, ...), channel_id=1, replica_groups=mesh['dp'=4,'fsdp'=8] {'fsdp'}, use_global_device_ids=true, to_apply=%add | all-reduce | flops 13824 | bytes 55296
  56.0 174.3 %all-gather.8.cloned.1.call-done = bf16[1152,6912]{1,0:T(8,128)(2,1)} async-done(((bf16[144,6912]{1,0:T(8,128)(2,1)}), bf16[1152,6912]{1,0:T(8,128)(2,1)}) %all-gather.8.cloned.1.call-update) | async-done | bytes 15925264 | tf_op jit(solution)/shard_map/all_gather | solution.py:172
  230.4 7.7 convolution_add_fusion
  238.2 111.7 %all-gather.10.cloned.1.call-done = bf16[1152,3456]{1,0:T(8,128)(2,1)} async-done(((bf16[144,3456]{1,0:T(8,128)(2,1)}), bf16[1152,3456]{1,0:T(8,128)(2,1)}) %all-gather.10.cloned.1.call-update) | async-done | bytes 7962640 | tf_op jit(solution)/shard_map/all_gather | solution.py:176
  353.2 12.5 convolution_convert_fusion.5
  366.5 40.6 %collective-permute-done = bf16[256,2304]{1,0:T(8,128)(2,1)S(1)} collective-permute-done((bf16[256,2304]{1,0:T(8,128)(2,1)S(1)}, bf16[256,2304]{1,0:T(8,128)(2,1)S(1)}, u32[]{:S(2)}, u32[]{:S(2)}) %collective-permute-start) | collective-permute-done | bytes 1179680 | tf_op jit(solution)/shard_map/ppermute | solution.py:16
  410.6 120.2 %all-gather = bf16[8,144,16]{1,2,0:T(8,128)(2,1)S(1)} all-gather(bf16[1,144,16]{1,2,0:T(8,128)(2,1)S(1)} %bitcast.215), channel_id=1, replica_groups=mesh['dp'=4,'fsdp'=8] {'fsdp'}, dimensions={0}, use_global_device_ids=true | all-gather | bytes 41472 | tf_op jit(solution)/shard_map/all_gather | solution.py:174
  531.0 32.7 %all-gather.1 = bf16[8,144,36]{1,2,0:T(8,128)(2,1)S(1)} all-gather(bf16[1,144,36]{1,2,0:T(8,128)(2,1)S(1)} %bitcast.214), channel_id=1, replica_groups=mesh['dp'=4,'fsdp'=8] {'fsdp'}, dimensions={0}, use_global_device_ids=true | all-gather | bytes 93312 | tf_op jit(solution)/shard_map/all_gather | solution.py:175
  570.8 2.8 copy.76
  581.8 2.8 copy.80
  584.6 4.7 copy.78
  591.9 3.6 fusion
  598.3 6.2 fusion.16
  606.1 6.4 fusion.129
  613.3 14.4 fusion.112
  627.7 131.0 %all-gather.16.cloned.1.call-done = bf16[4608,1152]{1,0:T(8,128)(2,1)} async-done(((bf16[576,1152]{1,0:T(8,128)(2,1)}), bf16[4608,1152]{1,0:T(8,128)(2,1)}) %all-gather.16.cloned.1.call-update) | async-done | bytes 10616848 | tf_op jit(solution)/shard_map/all_gather | solution.py:235
  758.7 16.4 fusion.21
  775.1 4.3 slice_reduce_fusion.1
  787.6 11.9 fusion.122
  799.5 18.5 convolution_add_fusion.1
  818.1 16.1 fusion.109
  834.2 8.2 fusion.124
  846.6 4.6 fusion.12
  851.2 14.4 multiply_reduce_fusion
  865.6 11.9 multiply_convert_fusion
  884.2 3.2 convolution_convert_fusion.4
  888.9 3.6 multiply_reduce_fusion.2
  894.5 63.4 %collective-permute-done.2 = bf16[512,2304]{0,1:T(8,128)(2,1)} collective-permute-done((bf16[512,2304]{0,1:T(8,128)(2,1)}, bf16[512,2304]{0,1:T(8,128)(2,1)}, u32[]{:S(2)}, u32[]{:S(2)}) %collective-permute-start.2) | collective-permute-done | bytes 2359328 | tf_op jit(solution)/shard_map/ppermute | solution.py:16
  957.9 4.6 fusion.18
  970.7 20.2 collective-permute-done.3
  993.7 20.2 convolution_convert_fusion.3
  1015.1 16.4 convolution_convert_fusion.1
  1033.2 12.2 convolution_convert_fusion.2
  1049.5 13.7 fusion.110
  1063.8 5.1 fusion.24
  1071.6 37.3 %psum.98 = bf16[2,6912]{1,0:T(2,128)(2,1)S(1)} all-reduce(bf16[2,6912]{1,0:T(2,128)(2,1)S(1)} %multiply_convert_fusion.4), channel_id=1, replica_groups=mesh['dp'=4,'fsdp'=8] {'fsdp'}, use_global_device_ids=true, to_apply=%region_32.33 | all-reduce | flops 13824 | bytes 55296 | tf_op jit(solution)/shard_map/psum | solution.py:356
  1109.1 7.8 convolution_convert_fusion
  1120.5 36.3 %all-reduce.8 = (bf16[2,16]{1,0:T(2,128)(2,1)S(1)}, bf16[2,36]{1,0:T(2,128)(2,1)S(1)}, bf16[6912]{0:T(1024)(128)(2,1)S(1)}, bf16[1152]{0:T(1024)(128)(2,1)S(1)},...) all-reduce(bf16[2,16]{1,0:T(2,128)(2,1)S(1)} %multiply_convert_fusi, ...), channel_id=1, replica_groups=mesh['dp'=4,'fsdp'=8] {'fsdp'}, use_global_device_ids=true, to_apply=%region_33.34 | all-reduce | flops 13928 | bytes 55712 | tf_op jit(solution)/shard_map/psum | solution.py:359
  1160.1 181.1 %reduce-scatter.20.cloned.1.call-done = bf16[576,1152]{1,0:T(8,128)(2,1)} async-done(((bf16[4608,1152]{1,0:T(8,128)(2,1)}), bf16[576,1152]{1,0:T(8,128)(2,1)}) %reduce-scatter.20.cloned.1.call-update) | async-done | bytes 1327120 | tf_op jit(solution)/shard_map/reduce_scatter | solution.py:289
  1341.2 182.8 %reduce-scatter.18.cloned.1.call-done = bf16[144,4608]{1,0:T(8,128)(2,1)} async-done(((bf16[1152,4608]{1,0:T(8,128)(2,1)}), bf16[144,4608]{1,0:T(8,128)(2,1)}) %reduce-scatter.18.cloned.1.call-update) | async-done | bytes 1327120 | tf_op jit(solution)/shard_map/reduce_scatter | solution.py:283
  1523.9 271.5 %reduce-scatter.12.cloned.1.call-done = bf16[144,6912]{1,0:T(8,128)(2,1)} async-done(((bf16[1152,6912]{1,0:T(8,128)(2,1)}), bf16[144,6912]{1,0:T(8,128)(2,1)}) %reduce-scatter.12.cloned.1.call-update) | async-done | bytes 1990672 | tf_op jit(solution)/shard_map/reduce_scatter | solution.py:403
  1795.4 9.8 convolution_reduce_fusion.1
  1805.2 9.8 fusion.136
  1817.7 40.2 %reduce-scatter.22.cloned.1.call-done = bf16[144,16]{1,0:T(8,128)(2,1)} async-done(((bf16[1152,16]{1,0:T(8,128)(2,1)}), bf16[144,16]{1,0:T(8,128)(2,1)}) %reduce-scatter.22.cloned.1.call-update) | async-done | bytes 4624
  1858.7 61.4 %reduce-scatter.24.cloned.1.call-done = bf16[144,36]{1,0:T(8,128)(2,1)} async-done(((bf16[1152,36]{1,0:T(8,128)(2,1)}), bf16[144,36]{1,0:T(8,128)(2,1)}) %reduce-scatter.24.cloned.1.call-update) | async-done | bytes 10384
  1921.0 11.3 all-reduce.10
  1935.9 100.9 %all-reduce.14.cloned.1.call-done = (bf16[144,6912]{1,0:T(8,128)(2,1)}, bf16[144,3456]{1,0:T(8,128)(2,1)}, bf16[144,1152]{1,0:T(8,128)(2,1)}, bf16[144,4608]{1,0:T(8,128)(2,1)}, bf16[576,1152]{1,0:T(8,128)(2,1)}) async-done(((bf16[144,6912]{1,0:T(8,128)(2,1)}, bf16[144,3456]{1,0:T(8,128)(2,1)}, bf16[144,1152]{1,0:T(8,128)(2,1)}, bf16[144,4608]{1,0:T(8,128)(2,1)}, bf16[576,1152]{1,0:T(8,128)(2,1)}), ...) | async-done | bytes 5971984 | tf_op jit(solution)/shard_map/psum | solution.py:407
  2038.6 3.8 convert_element_type.251
  (435 shorter events, 99.5 us)
Async XLA Ops:
  7.2 557.4 %copy-start = (s32[2,36]{1,0:T(2,128)S(1)}, s32[2,36]{1,0:T(2,128)}, u32[]{:S(2)}) copy-start(s32[2,36]{1,0:T(2,128)} %param.30) | copy-start | bytes 868
  7.2 223.1 %all-gather.8.cloned.1.call-start = ((), (), s32[]{:S(2)}) async-start(), calls=%async_computation.7 | async-start | bytes 17915904 | tf_op jit(solution)/shard_map/all_gather | solution.py:172
  8.0 47.2 %copy-start.23 = (bf16[256,1152]{1,0:T(8,128)(2,1)S(1)}, bf16[256,1152]{1,0:T(8,128)(2,1)}, u32[]{:S(2)}) copy-start(bf16[256,1152]{1,0:T(8,128)(2,1)} %param.24) | copy-start | bytes 1769476
  8.0 47.2 %copy-start.26 = (bf16[1,256,1152]{2,1,0:T(8,128)(2,1)S(1)}, bf16[1,256,1152]{2,1,0:T(8,128)(2,1)}, u32[]{:S(2)}) copy-start(bf16[1,256,1152]{2,1,0:T(8,128)(2,1)} %param.23) | copy-start | bytes 1769476
  8.0 341.9 %all-gather.10.cloned.1.call-start = ((), (), s32[]{:S(2)}) async-start(), calls=%async_computation.8 | async-start | bytes 8957952 | tf_op jit(solution)/shard_map/all_gather | solution.py:176
  8.8 597.2 %all-gather.12.cloned.1.call-start = ((), (), s32[]{:S(2)}) async-start(), calls=%async_computation.9 | async-start | bytes 2985984 | tf_op jit(solution)/shard_map/all_gather | solution.py:177
  9.5 46.4 %copy-start.90 = (f32[2,1152]{1,0:T(2,128)S(1)}, f32[2,1152]{1,0:T(2,128)}, u32[]{:S(2)}) copy-start(f32[2,1152]{1,0:T(2,128)} %param.26) | copy-start | bytes 27652
  9.5 46.5 %copy-start.78 = (f32[1,1152]{1,0:T(1,128)S(1)}, f32[1,1152]{1,0:T(1,128)}, u32[]{:S(2)}) copy-start(f32[1,1152]{1,0:T(1,128)} %param.25) | copy-start | bytes 13828
  9.5 603.7 %all-gather.14.cloned.1.call-start = ((), (), s32[]{:S(2)}) async-start(), calls=%async_computation.10 | async-start | bytes 11943936 | tf_op jit(solution)/shard_map/all_gather | solution.py:233
  10.1 748.6 %all-gather.16.cloned.1.call-start = ((), (), s32[]{:S(2)}) async-start(), calls=%async_computation.11 | async-start | bytes 11943936 | tf_op jit(solution)/shard_map/all_gather | solution.py:235
  10.7 1149.4 %reduce-scatter.16.cloned.1.call-start = ((), (), s32[]{:S(2)}) async-start(), calls=%async_computation.14 | async-start | bytes 2985984 | tf_op jit(solution)/shard_map/reduce_scatter | solution.py:403
  55.5 295.4 %copy-start.76 = (f32[512]{0:T(512)}, f32[512]{0:T(512)S(1)}, u32[]{:S(2)}) copy-start(f32[512]{0:T(512)S(1)} %broadcast_multiply_fusion.6) | copy-start | bytes 6148
  55.9 294.9 %copy-start.83 = (f32[512]{0:T(512)}, f32[512]{0:T(512)S(1)}, u32[]{:S(2)}) copy-start(f32[512]{0:T(512)S(1)} %add_rsqrt_fusion.1) | copy-start | bytes 6148
  56.0 723.7 %copy-start.69 = (bf16[2,1152]{1,0:T(2,128)(2,1)}, bf16[2,1152]{1,0:T(2,128)(2,1)S(1)}, u32[]{:S(2)}) copy-start(bf16[2,1152]{1,0:T(2,128)(2,1)S(1)} %fusion.84) | copy-start | bytes 13828
  365.8 42.9 %copy-start.38 = (bf16[512,3456]{1,0:T(8,128)(2,1)}, bf16[512,3456]{1,0:T(8,128)(2,1)S(1)}, u32[]{:S(2)}) copy-start(bf16[512,3456]{1,0:T(8,128)(2,1)S(1)} %convolution_convert_fusion.5) | copy-start | bytes 10616836
  365.9 44.8 %copy-start.86 = (bf16[144,16]{0,1:T(8,128)(2,1)S(1)}, bf16[144,16]{0,1:T(8,128)(2,1)}, u32[]{:S(2)}) copy-start(bf16[144,16]{0,1:T(8,128)(2,1)} %param.35) | copy-start | bytes 13828
  365.9 165.1 %copy-start.75 = (bf16[144,36]{0,1:T(8,128)(2,1)S(1)}, bf16[144,36]{0,1:T(8,128)(2,1)}, u32[]{:S(2)}) copy-start(bf16[144,36]{0,1:T(8,128)(2,1)} %param.36) | copy-start | bytes 31108
  365.9 198.7 %copy-start.104 = (s32[2,16]{1,0:T(2,128)S(1)}, s32[2,16]{1,0:T(2,128)}, u32[]{:S(2)}) copy-start(s32[2,16]{1,0:T(2,128)} %param.28) | copy-start | bytes 388
  365.9 199.2 %copy-start.96 = (s32[256]{0:T(256)S(1)}, s32[256]{0:T(256)}, u32[]{:S(2)}) copy-start(s32[256]{0:T(256)} %param.32) | copy-start | bytes 3076
  365.9 199.2 %copy-start.97 = (s32[1,256]{1,0:T(1,128)S(1)}, s32[1,256]{1,0:T(1,128)}, u32[]{:S(2)}) copy-start(s32[1,256]{1,0:T(1,128)} %param.31) | copy-start | bytes 3076
  365.9 199.2 %copy-start.100 = (s32[1,16]{1,0:T(1,128)S(1)}, s32[1,16]{1,0:T(1,128)}, u32[]{:S(2)}) copy-start(s32[1,16]{1,0:T(1,128)} %param.27) | copy-start | bytes 196
  365.9 41.1 %collective-permute-start = (bf16[256,2304]{1,0:T(8,128)(2,1)S(1)}, bf16[256,2304]{1,0:T(8,128)(2,1)S(1)}, u32[]{:S(2)}, u32[]{:S(2)}) collective-permute-start(bf16[256,2304]{1,0:T(8,128)(2,1)S(1)} %slice.215), channel_id=1, source_target_pairs={{0,1},{1,0},{2,3},{3,2},{4,5},{5,4},{6,7},{7,6},{8,9},{9,8},{10,11... | collective-permute-start | bytes 3538952 | tf_op jit(solution)/shard_map/ppermute | solution.py:16
  408.8 168.4 %collective-permute-start.1 = (bf16[512,2304]{1,0:T(8,128)(2,1)}, bf16[512,2304]{1,0:T(8,128)(2,1)}, u32[]{:S(2)}, u32[]{:S(2)}) collective-permute-start(bf16[512,2304]{1,0:T(8,128)(2,1)} %pad_maximum_fusion.4), channel_id=1, source_target_pairs={{0,2},{1,3},{2,0},{3,1},{4,6},{5,7},{6,4},{7,5},{8,10},{9,11},{10,... | collective-permute-start | bytes 7077896 | tf_op jit(solution)/shard_map/ppermute | solution.py:16
  531.0 35.0 %copy-start.61 = (bf16[1152,16]{0,1:T(8,128)(2,1)}, bf16[1152,16]{0,1:T(8,128)(2,1)S(1)}, u32[]{:S(2)}) copy-start(bf16[1152,16]{0,1:T(8,128)(2,1)S(1)} %reshape.423) | copy-start | bytes 110596
  612.5 221.7 %copy-start.11 = (f32[512,1152]{1,0:T(8,128)}, f32[512,1152]{1,0:T(8,128)S(1)}, u32[]{:S(2)}) copy-start(f32[512,1152]{1,0:T(8,128)S(1)} %get-tuple-element.72) | copy-start | bytes 7077892
  613.2 221.0 %copy-start.88 = (f32[512]{0:T(512)}, f32[512]{0:T(512)S(1)}, u32[]{:S(2)}) copy-start(f32[512]{0:T(512)S(1)} %add_rsqrt_fusion) | copy-start | bytes 6148
  613.2 145.5 %copy-start.41 = (bf16[256,1152]{1,0:T(8,128)(2,1)S(1)}, bf16[256,1152]{1,0:T(8,128)(2,1)}, u32[]{:S(2)}) copy-start(bf16[256,1152]{1,0:T(8,128)(2,1)} %param.45) | copy-start | bytes 1769476
  613.2 145.5 %copy-start.53 = (f32[4608]{0:T(1024)S(1)}, f32[4608]{0:T(1024)}, u32[]{:S(2)}) copy-start(f32[4608]{0:T(1024)} %convert_element_type.228) | copy-start | bytes 55300
  884.0 73.9 %collective-permute-start.2 = (bf16[512,2304]{0,1:T(8,128)(2,1)}, bf16[512,2304]{0,1:T(8,128)(2,1)}, u32[]{:S(2)}, u32[]{:S(2)}) collective-permute-start(bf16[512,2304]{0,1:T(8,128)(2,1)} %fusion.19), channel_id=1, source_target_pairs={{0,2},{1,3},{2,0},{3,1},{4,6},{5,7},{6,4},{7,5},{8,10},{9,11},{10,... | collective-permute-start | bytes 7077896 | tf_op jit(solution)/shard_map/ppermute | solution.py:16
  887.5 272.6 %reduce-scatter.14.cloned.1.call-start = ((), (), s32[]{:S(2)}) async-start(), calls=%async_computation.13 | async-start | bytes 8957952 | tf_op jit(solution)/shard_map/reduce_scatter | solution.py:403
  892.5 65.4 %slice-start.10 = ((s8[4718592]{0:T(1024)(128)(4,1)}), s8[4194304]{0:T(1024)(128)(4,1)S(1)}, s32[]{:S(2)}) async-start(s8[4718592]{0:T(1024)(128)(4,1)} %bitcast.170), calls=%async_computation.30 | async-start | bytes 8388608
  892.5 65.4 %slice-start.12 = ((s8[4718592]{0:T(1024)(128)(4,1)}), s8[4194304]{0:T(1024)(128)(4,1)S(1)}, s32[]{:S(2)}) async-start(s8[4718592]{0:T(1024)(128)(4,1)} %bitcast.174), calls=%async_computation.32 | async-start | bytes 8388608
  892.5 65.4 %slice-start.11 = ((s8[4718592]{0:T(1024)(128)(4,1)}), s8[524288]{0:T(1024)(128)(4,1)S(1)}, s32[]{:S(2)}) async-start(s8[4718592]{0:T(1024)(128)(4,1)} %bitcast.170), calls=%async_computation.31 | async-start | bytes 1048576
  892.5 65.4 %slice-start.13 = ((s8[4718592]{0:T(1024)(128)(4,1)}), s8[524288]{0:T(1024)(128)(4,1)S(1)}, s32[]{:S(2)}) async-start(s8[4718592]{0:T(1024)(128)(4,1)} %bitcast.174), calls=%async_computation.33 | async-start | bytes 1048576
  893.7 73.4 %slice-start.8 = ((s8[8388608]{0:T(1024)(128)(4,1)}), s8[4194304]{0:T(1024)(128)(4,1)S(1)}, s32[]{:S(2)}) async-start(s8[8388608]{0:T(1024)(128)(4,1)} %bitcast.167), calls=%async_computation.28 | async-start | bytes 8388608
  894.5 98.1 %copy-start.56 = (bf16[16,72,256]{2,1,0:T(8,128)(2,1)}, bf16[16,72,256]{2,1,0:T(8,128)(2,1)S(1)}, u32[]{:S(2)}) copy-start(bf16[16,72,256]{2,1,0:T(8,128)(2,1)S(1)} %fusion.61) | copy-start | bytes 1769476
  894.5 72.6 %slice-start.9 = ((s8[8388608]{0:T(1024)(128)(4,1)}), s8[4194304]{0:T(1024)(128)(4,1)S(1)}, s32[]{:S(2)}) async-start(s8[8388608]{0:T(1024)(128)(4,1)} %bitcast.167), calls=%async_computation.29 | async-start | bytes 8388608
  964.3 26.6 %collective-permute-start.3 = (bf16[256,2304]{0,1:T(8,128)(2,1)S(1)}, bf16[256,2304]{0,1:T(8,128)(2,1)}, u32[]{:S(2)}, u32[]{:S(2)}) collective-permute-start(bf16[256,2304]{0,1:T(8,128)(2,1)S(1)} %slice.317), channel_id=1, source_target_pairs={{0,1},{1,0},{2,3},{3,2},{4,5},{5,4},{6,7},{7,6},{8,9},{9,8},{10,11... | collective-permute-start | bytes 3538952 | tf_op jit(solution)/shard_map/ppermute | solution.py:16
  1013.9 327.3 %reduce-scatter.20.cloned.1.call-start = ((), (), s32[]{:S(2)}) async-start(), calls=%async_computation.16 | async-start | bytes 11943936 | tf_op jit(solution)/shard_map/reduce_scatter | solution.py:289
  1031.5 492.4 %reduce-scatter.18.cloned.1.call-start = ((), (), s32[]{:S(2)}) async-start(), calls=%async_computation.15 | async-start | bytes 11943936 | tf_op jit(solution)/shard_map/reduce_scatter | solution.py:283
  1045.4 750.0 %reduce-scatter.12.cloned.1.call-start = ((), (), s32[]{:S(2)}) async-start(), calls=%async_computation.12 | async-start | bytes 17915904 | tf_op jit(solution)/shard_map/reduce_scatter | solution.py:403
  1070.7 38.4 %copy-start.70 = (bf16[2,1152]{1,0:T(2,128)(2,1)S(1)}, bf16[2,1152]{1,0:T(2,128)(2,1)}, u32[]{:S(2)}) copy-start(bf16[2,1152]{1,0:T(2,128)(2,1)} %copy-done.69) | copy-start | bytes 13828
  1117.0 41.0 %copy-start.92 = (bf16[2,36]{1,0:T(2,128)(2,1)S(1)}, bf16[2,36]{1,0:T(2,128)(2,1)}, u32[]{:S(2)}) copy-start(bf16[2,36]{1,0:T(2,128)(2,1)} %get-tuple-element.69) | copy-start | bytes 436
  1117.0 42.5 %copy-start.62 = (bf16[1152,16]{0,1:T(8,128)(2,1)S(1)}, bf16[1152,16]{0,1:T(8,128)(2,1)}, u32[]{:S(2)}) copy-start(bf16[1152,16]{0,1:T(8,128)(2,1)} %copy-done.61) | copy-start | bytes 110596
  1117.0 42.6 %copy-start.60 = (bf16[1152,36]{0,1:T(8,128)(2,1)S(1)}, bf16[1152,36]{0,1:T(8,128)(2,1)}, u32[]{:S(2)}) copy-start(bf16[1152,36]{0,1:T(8,128)(2,1)} %reshape.425) | copy-start | bytes 248836
  1117.0 740.9 %reduce-scatter.22.cloned.1.call-start = ((), (), s32[]{:S(2)}) async-start(), calls=%async_computation.17 | async-start | bytes 331776
  1158.0 762.2 %reduce-scatter.24.cloned.1.call-start = ((), (), s32[]{:S(2)}) async-start(), calls=%async_computation.18 | async-start | bytes 331776
  1159.2 877.6 %all-reduce.14.cloned.1.call-start = ((), (), s32[]{:S(2)}) async-start(), calls=%async_computation.19 | async-start | bytes 11943936 | tf_op jit(solution)/shard_map/psum | solution.py:407
  (95 other events, 688.3 us)
Sparse Core Ops, SparseCore 0:
  10.2 220.1 all-gather.7
  232.5 117.2 all-gather.9
  352.0 69.7 all-gather.11
  423.8 182.3 all-gather.13
  608.3 150.3 all-gather.15
  887.6 88.8 reduce-scatter.15
  1014.0 144.2 reduce-scatter.13
  1161.9 179.2 reduce-scatter.19
  1344.8 179.1 reduce-scatter.17
  1527.6 267.6 reduce-scatter.11
  1799.3 58.6 reduce-scatter.21
  1861.6 58.4 reduce-scatter.23
  1922.9 113.8 all-reduce.13
where the time goes:
time: 2060 us; the launch traced here: 2050 us
  waiting for transfers between devices  1380 us (67%)
  blocking collectives  279 us (14%)
  matrix products  231 us (11%)
  other arithmetic  84.8 us (4%)
  local copies, waits for them, and re-layouts  55.8 us (3%)
    reduce_scatter x3, waiting for transfers between devices, per_device(): lax.psum_scatter(shortened(attention_terms), 'fsdp', scatter_dimension=0,...  271 us
    reduce_scatter x1, waiting for transfers between devices, per_device(): lax.psum_scatter(grad_fc1.astype(jnp.bfloat16), 'fsdp', scatter_dimension...  183 us
    reduce_scatter x1, waiting for transfers between devices, per_device(): lax.psum_scatter(grad_fc2.astype(jnp.bfloat16), 'fsdp', scatter_dimension...  181 us
    all_gather x1, waiting for transfers between devices, per_device(): lax.all_gather(first_set[0], 'fsdp', axis=0, tiled=True)  174 us
    all_gather x1, waiting for transfers between devices, per_device(): lax.all_gather(second_set[2], 'fsdp', axis=0, tiled=True)  131 us
    ppermute x4, waiting for transfers between devices, from_partner(): return lax.ppermute(value, axis, pairs)  124 us
    all_gather x1, blocking collectives, per_device(): lax.all_gather(first_set[2], 'fsdp', axis=0, tiled=True)  120 us
    all_gather x1, waiting for transfers between devices, per_device(): lax.all_gather(first_set[4], 'fsdp', axis=0, tiled=True)  112 us
  transfers between devices with their start and end apart: 17, of which 12 were waited for; matrix products, arithmetic and copies ran while one was open for 11% of the time, Pallas kernels for 0%

commit v1 on v0

v1 whole, which is shorter than its diff:
```python
import jax
import jax.numpy as jnp
from jax import lax
from jax.sharding import PartitionSpec as P

CHAN = 128
SPLIT = 4


epsilon = 1e-06


def swap(value, axis, mask):
    pairs = [(source, source ^ mask) for source in range(lax.axis_size(axis))]
    return lax.ppermute(value, axis, pairs)


def place(buffer, block, *where):
    return lax.dynamic_update_slice(buffer, block, where)


def gather_small(rows, axis):
    mask = 1
    while mask < lax.axis_size(axis):
        rows = jnp.concatenate([rows, swap(rows, axis, mask)], 0)
        mask *= 2
    return rows


def gather_blocks(block, y_first):
    half = lax.axis_size("fsdp") // 2
    position = lax.axis_index("fsdp") // 2
    line = jnp.zeros((half,) + block.shape, block.dtype)
    line = place(line, block[None], position, 0, 0)
    for step in range(1, half):
        line = place(line, swap(block, "fsdp", 2 * step)[None], position ^ step, 0, 0)
    held = {(0, 0): line}
    if y_first:
        held[0, 1] = swap(line, "fsdp", 1)
        held[2, 0] = swap(line, "dp", 2)
        held[2, 1] = swap(held[0, 1], "dp", 2)
    else:
        held[2, 0] = swap(line, "dp", 2)
        held[0, 1] = swap(line, "fsdp", 1)
        held[2, 1] = swap(held[2, 0], "fsdp", 1)
    for role, side in list(held):
        held[role ^ 1, side] = swap(held[role, side], "dp", 1)
    return held


def stack_roles(parts, rows):
    role, side = lax.axis_index("dp"), lax.axis_index("fsdp") % 2
    half = lax.axis_size("fsdp") // 2
    width = sum(part[0, 0].shape[2] for part in parts)
    whole = jnp.zeros((4, half, 2, rows, width), jnp.bfloat16)
    offset = 0
    for part in parts:
        for (role_xor, side_xor), line in part.items():
            whole = place(
                whole, line[None, :, None], role ^ role_xor, 0, side ^ side_xor, 0, offset
            )
        offset += part[0, 0].shape[2]
    return whole.reshape(4, half * 2 * rows, width)


def stack_rows(part, rows):
    role, side = lax.axis_index("dp"), lax.axis_index("fsdp") % 2
    half = lax.axis_size("fsdp") // 2
    width = part[0, 0].shape[2]
    whole = jnp.zeros((half, 2, 4, rows, width), jnp.bfloat16)
    for (role_xor, side_xor), line in part.items():
        whole = place(whole, line[:, None, None], 0, side ^ side_xor, role ^ role_xor, 0, 0)
    return whole.reshape(half * 8 * rows, width)


def low(value):
    return value.astype(jnp.bfloat16)


def scatter_blocks(terms, y_first):
    half = lax.axis_size("fsdp") // 2
    position = lax.axis_index("fsdp") // 2
    side = lax.axis_index("fsdp") % 2

    def on_side(value, which):
        return lax.dynamic_index_in_dim(value, which, 1, keepdims=False)

    far = terms[2] + swap(low(terms[3]), "dp", 1).astype(jnp.float32)
    near = terms[0] + swap(low(terms[1]), "dp", 1).astype(jnp.float32)
    if y_first:
        far = on_side(far, side) + swap(low(on_side(far, side ^ 1)), "fsdp", 1)
        near = on_side(near, side) + swap(low(on_side(near, side ^ 1)), "fsdp", 1)
        near = near + swap(low(far), "dp", 2)
    else:
        near = near + swap(low(far), "dp", 2)
        near = on_side(near, side) + swap(low(on_side(near, side ^ 1)), "fsdp", 1)

    def at(index):
        return lax.dynamic_index_in_dim(near, index, 0, keepdims=False)

    total = at(position)
    for step in range(1, half):
        total = total + swap(low(at(position ^ step)), "fsdp", 2 * step)
    return low(total)


def share_roles(block):
    role = lax.axis_index("dp")
    whole = jnp.zeros((4,) + block.shape, jnp.float32)
    whole = place(whole, block[None].astype(jnp.float32), role, 0, 0)
    for step in range(1, 4):
        whole = place(whole, swap(block, "dp", step)[None].astype(jnp.float32), role ^ step, 0, 0)
    return whole


def product(left, right):
    return jnp.dot(left, right, preferred_element_type=jnp.float32)


def product_tn(left, right):
    return lax.dot_general(
        left, right, (((0,), (0,)), ((), ())), preferred_element_type=jnp.float32
    )


def product_nt(left, right):
    return lax.dot_general(
        left, right, (((1,), (1,)), ((), ())), preferred_element_type=jnp.float32
    )


def spread(per_slot, short_count, len_short, quarter_rows):
    width = per_slot.shape[1]
    short_part = jnp.broadcast_to(
        per_slot[:short_count, None, :], (short_count, len_short, width)
    ).reshape(short_count * len_short, width)
    long_part = jnp.broadcast_to(per_slot[short_count:], (quarter_rows, width))
    return jnp.concatenate([short_part, long_part], 0)


def slot_sum(values, short_count, len_short):
    short_rows = short_count * len_short
    short_part = jnp.sum(
        values[:short_rows].reshape((short_count, len_short) + values.shape[1:]), axis=1
    )
    long_part = jnp.sum(values[short_rows:], axis=0, keepdims=True)
    return jnp.concatenate([short_part, long_part], 0)


def norm_parts(values):
    average = jnp.mean(values, axis=-1, keepdims=True)
    centred = values - average
    variance = jnp.mean(centred * centred, axis=-1, keepdims=True)
    inverse = lax.rsqrt(variance + epsilon)
    return (centred * inverse, inverse)


def norm_back(gradient, normed, inverse):
    return inverse * (
        gradient
        - jnp.mean(gradient, axis=-1, keepdims=True)
        - normed * jnp.mean(gradient * normed, axis=-1, keepdims=True)
    )


def silu_grad(values):
    sigmoid_value = jax.nn.sigmoid(values)
    return sigmoid_value * (1.0 + values * (1.0 - sigmoid_value))


def attend(queries, key_rows, value_rows, scaling):
    scores = (
        jnp.einsum("nqhe,nkhe->nhqk", queries, key_rows, preferred_element_type=jnp.float32)
        * scaling
    )
    row_max = jnp.max(scores, axis=-1, keepdims=True)
    exponent = jnp.exp(scores - row_max)
    row_total = jnp.sum(exponent, axis=-1, keepdims=True)
    soft_weights = exponent / row_total
    head_out = jnp.einsum(
        "nhqk,nkhe->nqhe",
        soft_weights.astype(jnp.bfloat16),
        value_rows,
        preferred_element_type=jnp.float32,
    )
    return (head_out, row_max + jnp.log(row_total))


def attend_back(queries, key_rows, value_rows, log_total, d_out, scaling):
    scores = (
        jnp.einsum("nqhe,nkhe->nhqk", queries, key_rows, preferred_element_type=jnp.float32)
        * scaling
    )
    soft_weights = jnp.exp(scores - log_total)
    d_weights = jnp.einsum("nqhe,nkhe->nhqk", d_out, value_rows, preferred_element_type=jnp.float32)
    inner = jnp.sum(soft_weights * d_weights, axis=-1, keepdims=True)
    d_scores = (soft_weights * (d_weights - inner)).astype(jnp.bfloat16)
    d_queries = (
        jnp.einsum("nhqk,nkhe->nqhe", d_scores, key_rows, preferred_element_type=jnp.float32)
        * scaling
    )
    d_keys = (
        jnp.einsum("nhqk,nqhe->nkhe", d_scores, queries, preferred_element_type=jnp.float32)
        * scaling
    )
    d_values = jnp.einsum(
        "nhqk,nqhe->nkhe",
        soft_weights.astype(jnp.bfloat16),
        d_out,
        preferred_element_type=jnp.float32,
    )
    return (d_queries, d_keys, d_values)


def gelu_tanh(values):
    return jax.nn.gelu(values, approximate=True)


def per_device(
    x_short,
    x_long,
    short_cond,
    long_cond,
    short_heads,
    long_heads,
    short_groups,
    long_groups,
    short_keep,
    long_keep,
    w_ada,
    b_ada,
    w_head_router,
    w_group_router,
    w_qkv,
    w_proj,
    b_proj,
    w_fc1,
    b_fc1,
    w_fc2,
    b_fc2,
    g_short,
    g_long,
):
    short_count, len_short, model_width = x_short.shape
    quarter_rows = x_long.shape[0]
    head_count = w_head_router.shape[1]
    head_width = model_width // head_count
    group_count = w_group_router.shape[1]
    slot_count = short_count + 1
    short_rows = short_count * len_short
    row_count = short_rows + quarter_rows
    scaling = head_width ** (-0.5)
    fsdp_index = lax.axis_index("fsdp")
    fsdp_count = lax.axis_size("fsdp")
    role = lax.axis_index("dp")
    group_row = fsdp_index // SPLIT
    first_member = (fsdp_index % SPLIT == 0).astype(jnp.float32)
    group_total = fsdp_count // SPLIT
    half = fsdp_count // 2
    shard_rows = w_qkv.shape[0]
    unit_rows = w_fc2.shape[0] // 4
    first_columns = (model_width // 256 + 1) * 128

    def block_of(matrix, start, width):
        return lax.dynamic_slice_in_dim(matrix, start, width, 1)

    mixed_shard = jnp.concatenate([w_qkv, w_proj], 1)
    first_part = gather_blocks(block_of(mixed_shard, role * model_width, first_columns), True)
    second_part = gather_blocks(
        block_of(mixed_shard, role * model_width + first_columns, model_width - first_columns), False
    )
    attention_full = stack_roles([first_part, second_part], shard_rows)
    fc1_part = gather_blocks(block_of(w_fc1, role * model_width, model_width), True)
    fc2_part = gather_blocks(lax.dynamic_slice_in_dim(w_fc2, role * unit_rows, unit_rows, 0), False)
    short_act = low(jax.nn.silu(short_cond))
    long_act = low(jax.nn.silu(long_cond))
    message = jnp.concatenate([short_act, b_proj[None], b_fc1[None], b_fc2[None]], 1)
    message = gather_small(message, "fsdp")
    members = jnp.arange(fsdp_count) ^ fsdp_index
    act_rows = message[:, :model_width]
    biases = jnp.take(message[:, model_width:], members, axis=0).astype(jnp.float32)
    proj_bias = biases[:, :shard_rows].reshape(-1)
    fc1_bias = biases[:, shard_rows : shard_rows + 4 * shard_rows].reshape(-1)
    fc2_bias = biases[:, 5 * shard_rows :].reshape(-1)
    groups = jnp.arange(group_total) ^ group_row
    item_act = jnp.concatenate([act_rows, jnp.take(long_act, groups, axis=0)], 0)

    def own_columns(rows):
        return lax.dynamic_slice_in_dim(rows, fsdp_index * shard_rows, shard_rows, 1)

    item_columns = own_columns(item_act)
    bias_row = lax.dynamic_update_slice_in_dim(
        jnp.zeros((fsdp_count * b_ada.shape[0],), jnp.float32),
        b_ada.astype(jnp.float32),
        fsdp_index * b_ada.shape[0],
        0,
    )
    partial = jnp.concatenate(
        [
            product(item_columns, w_ada) + bias_row,
            product(item_columns, w_head_router),
            product(item_columns, w_group_router),
        ],
        1,
    )
    short_part, long_part = partial[:fsdp_count], partial[fsdp_count:]
    mask = fsdp_count // 2
    while mask:
        if mask >= SPLIT:
            step = mask // SPLIT
            taken = swap(jnp.concatenate([short_part[mask:], long_part[step:]], 0), "fsdp", mask)
            long_part = long_part[:step] + taken[mask:]
        else:
            taken = swap(jnp.concatenate([short_part[mask:], long_part], 0), "fsdp", mask)
            long_part = long_part + taken[mask:]
        short_part = short_part[:mask] + taken[:mask]
        mask //= 2
    conditioned = jnp.concatenate([short_part, long_part], 0)
    mod_width = 6 * model_width
    modulation = conditioned[:, :mod_width]
    head_sigmoid = jax.nn.sigmoid(conditioned[:, mod_width : mod_width + head_count])
    group_sigmoid = jax.nn.sigmoid(conditioned[:, mod_width + head_count :])
    head_mask = jnp.concatenate(
        [short_heads, lax.dynamic_slice_in_dim(long_heads, group_row, 1, 0)], 0
    ).astype(jnp.float32)
    group_mask = jnp.concatenate(
        [short_groups, lax.dynamic_slice_in_dim(long_groups, group_row, 1, 0)], 0
    ).astype(jnp.float32)
    head_gate = head_mask * 2.0 * head_sigmoid
    group_gate = group_mask * 2.0 * group_sigmoid
    shift1, scale1, gate1, shift2, scale2, gate2 = jnp.split(
        spread(modulation, short_count, len_short, quarter_rows), 6, axis=1
    )
    x_rows = jnp.concatenate([x_short.reshape(short_rows, model_width), x_long], 0).astype(
        jnp.float32
    )
    keep_rows = jnp.concatenate([short_keep.reshape(short_rows), long_keep], 0).astype(jnp.float32)[
        :, None
    ]
    normed1, inverse1 = norm_parts(x_rows)
    hidden1 = low(normed1 * (1.0 + scale1) + shift1)
    q_rows, k_rows, v_rows = (low(product(hidden1, attention_full[part])) for part in range(3))

    def split_heads(rows, count):
        return rows.reshape(count, -1, head_count, head_width)

    own_k, own_v = k_rows[short_rows:], v_rows[short_rows:]
    k_y = swap(own_k, "fsdp", 1)
    v_z = swap(own_v, "fsdp", 2)
    k_far = swap(jnp.concatenate([own_k, k_y], 0), "fsdp", 2)
    v_far = swap(jnp.concatenate([own_v, v_z], 0), "fsdp", 1)
    long_keys = split_heads(jnp.concatenate([own_k, k_y, k_far], 0), 1)
    long_values = split_heads(
        jnp.concatenate([own_v, v_far[:quarter_rows], v_z, v_far[quarter_rows:]], 0), 1
    )
    short_q, short_k, short_v = (
        split_heads(rows[:short_rows], short_count) for rows in (q_rows, k_rows, v_rows)
    )
    short_out, short_log = attend(short_q, short_k, short_v, scaling)
    long_queries = split_heads(q_rows[short_rows:], 1)
    long_out, long_log = attend(long_queries, long_keys, long_values, scaling)
    head_rows = jnp.concatenate(
        [
            short_out.reshape(short_rows, head_count, head_width),
            long_out.reshape(quarter_rows, head_count, head_width),
        ],
        0,
    )
    head_gate_rows = spread(head_gate, short_count, len_short, quarter_rows)[:, :, None]
    attention = low((head_rows * head_gate_rows).reshape(row_count, model_width))
    projected = product(attention, attention_full[3]) + proj_bias
    mixed = x_rows + gate1 * projected
    fc1_full = stack_roles([fc1_part], shard_rows)
    fc2_full = stack_rows(fc2_part, unit_rows)
    fc2_full = fc2_full.reshape(4, -1, model_width)
    normed2, inverse2 = norm_parts(mixed)
    hidden2 = low(normed2 * (1.0 + scale2) + shift2)
    channel_gate = spread(
        jnp.repeat(group_gate, CHAN, axis=1), short_count, len_short, quarter_rows
    )
    gates = jnp.split(channel_gate, 4, axis=1)
    gelus, pulls, activated = [], [], []
    down_rows = fc2_bias
    for part in range(4):
        up_rows = product(hidden2, fc1_full[part]) + fc1_bias.reshape(4, -1)[part]
        gelu_value, gelu_pull = jax.vjp(gelu_tanh, up_rows)
        gelus.append(gelu_value)
        pulls.append(gelu_pull)
        activated.append(low(gelu_value * gates[part]))
        down_rows = down_rows + product(activated[part], fc2_full[part])
    out_rows = mixed + gate2 * keep_rows * down_rows
    y_short = low(out_rows[:short_rows].reshape(x_short.shape))
    y_long = low(out_rows[short_rows:])
    gradient = jnp.concatenate([g_short.reshape(short_rows, model_width), g_long], 0).astype(
        jnp.float32
    )
    d_down = low(gradient * gate2 * keep_rows)
    slot_gate2 = slot_sum(gradient * keep_rows * down_rows, short_count, len_short)
    grad_fc2 = jnp.concatenate([low(product_tn(part, d_down)) for part in activated], 0)
    grad_fc2 = grad_fc2.reshape(half, 2, 4, unit_rows, model_width)
    fc2_terms = [
        lax.dynamic_index_in_dim(grad_fc2, role ^ step, 2, keepdims=False) for step in range(4)
    ]
    fc2_block = scatter_blocks(fc2_terms, False)
    g_w_fc2 = share_roles(fc2_block).reshape(4 * unit_rows, model_width)
    d_ups, d_groups = [], []
    d_hidden2 = 0.0
    for part in range(4):
        d_activated = product_nt(d_down, fc2_full[part])
        d_channel = slot_sum(d_activated * gelus[part], short_count, len_short)
        d_groups.append(jnp.sum(d_channel.reshape(slot_count, -1, CHAN), axis=-1))
        d_ups.append(low(pulls[part](d_activated * gates[part])[0]))
        d_hidden2 = d_hidden2 + product_nt(d_ups[part], fc1_full[part])
    d_group = jnp.concatenate(d_groups, 1)
    up_stack = jnp.stack(d_ups)

    def role_term(left, right):
        return product_tn(left, right).reshape(half, 2, shard_rows, -1)

    fc1_terms = [
        role_term(hidden2, lax.dynamic_index_in_dim(up_stack, role ^ step, 0, keepdims=False))
        for step in range(4)
    ]
    fc1_block = scatter_blocks(fc1_terms, True)
    g_w_fc1 = share_roles(fc1_block).transpose(1, 0, 2).reshape(shard_rows, -1)
    slot_shift2 = slot_sum(d_hidden2, short_count, len_short)
    slot_scale2 = slot_sum(d_hidden2 * normed2, short_count, len_short)
    d_mixed = gradient + norm_back(d_hidden2 * (1.0 + scale2), normed2, inverse2)
    d_projected = low(d_mixed * gate1)
    slot_gate1 = slot_sum(d_mixed * projected, short_count, len_short)
    d_attention = product_nt(d_projected, attention_full[3]).reshape(
        row_count, head_count, head_width
    )
    d_head = slot_sum(jnp.sum(d_attention * head_rows, axis=-1), short_count, len_short)
    d_heads = low(d_attention * head_gate_rows)
    bias_grad = jnp.concatenate(
        [jnp.sum(d_projected, axis=0, dtype=jnp.float32)]
        + [jnp.sum(d_up, axis=0, dtype=jnp.float32) for d_up in d_ups]
        + [jnp.sum(d_down, axis=0, dtype=jnp.float32)]
    )[None]
    for axis in ("fsdp", "dp"):
        mask = 1
        while mask < lax.axis_size(axis):
            bias_grad = bias_grad + swap(bias_grad, axis, mask)
            mask *= 2
    bias_grad = bias_grad[0]

    def own_bias(start, count):
        return lax.dynamic_slice_in_dim(bias_grad, start + fsdp_index * count, count, 0)

    g_b_proj = own_bias(0, shard_rows)
    g_b_fc1 = own_bias(model_width, 4 * shard_rows)
    g_b_fc2 = own_bias(5 * model_width, shard_rows)
    long_dq, long_dk, long_dv = attend_back(
        long_queries, long_keys, long_values, long_log, split_heads(d_heads[short_rows:], 1), scaling
    )
    dk = long_dk.reshape(SPLIT, quarter_rows, model_width)
    dv = long_dv.reshape(SPLIT, quarter_rows, model_width)
    dk_near = dk[:2] + swap(low(dk[2:]), "fsdp", 2)
    own_dk = dk_near[0] + swap(low(dk_near[1]), "fsdp", 1)
    dv_sent = swap(low(jnp.stack([dv[1], dv[3]])), "fsdp", 1)
    dv_near = jnp.stack([dv[0], dv[2]]) + dv_sent
    own_dv = dv_near[0] + swap(low(dv_near[1]), "fsdp", 2)
    short_dq, short_dk, short_dv = attend_back(
        short_q, short_k, short_v, short_log, split_heads(d_heads[:short_rows], short_count), scaling
    )

    def join(short_rows_part, long_rows_part):
        return low(
            jnp.concatenate(
                [
                    short_rows_part.reshape(short_rows, model_width),
                    long_rows_part.reshape(quarter_rows, model_width),
                ],
                0,
            )
        )

    dq_rows, dk_rows, dv_rows = join(short_dq, long_dq), join(short_dk, own_dk), join(short_dv, own_dv)
    right_stack = jnp.stack([dq_rows, dk_rows, dv_rows, d_projected])
    left_stack = jnp.stack([hidden1, attention])
    attention_terms = []
    for step in range(4):
        which = role ^ step
        right = lax.dynamic_index_in_dim(right_stack, which, 0, keepdims=False)
        left = lax.dynamic_index_in_dim(left_stack, which // 3, 0, keepdims=False)
        attention_terms.append(role_term(left, right))
    attention_block = jnp.concatenate(
        [
            scatter_blocks([term[..., :first_columns] for term in attention_terms], True),
            scatter_blocks([term[..., first_columns:] for term in attention_terms], False),
        ],
        1,
    )
    attention_grad = share_roles(attention_block)
    g_w_qkv = attention_grad[:3].transpose(1, 0, 2).reshape(shard_rows, -1)
    g_w_proj = attention_grad[3]
    d_hidden1 = (
        product_nt(dq_rows, attention_full[0])
        + product_nt(dk_rows, attention_full[1])
        + product_nt(dv_rows, attention_full[2])
    )
    slot_shift1 = slot_sum(d_hidden1, short_count, len_short)
    slot_scale1 = slot_sum(d_hidden1 * normed1, short_count, len_short)
    d_rows = d_mixed + norm_back(d_hidden1 * (1.0 + scale1), normed1, inverse1)
    dx_short = low(d_rows[:short_rows].reshape(x_short.shape))
    dx_long = low(d_rows[short_rows:])
    d_head_logit = d_head * head_mask * 2.0 * head_sigmoid * (1.0 - head_sigmoid)
    d_group_logit = d_group * group_mask * 2.0 * group_sigmoid * (1.0 - group_sigmoid)
    d_conditioned = jnp.concatenate(
        [
            slot_shift1,
            slot_scale1,
            slot_gate1,
            slot_shift2,
            slot_scale2,
            slot_gate2,
            d_head_logit,
            d_group_logit,
        ],
        1,
    )
    long_sum = d_conditioned[short_count:]
    for mask in (1, 2):
        long_sum = long_sum + swap(long_sum, "fsdp", mask)
    own_rows = low(jnp.concatenate([d_conditioned[:short_count], long_sum], 0))[None]
    member_rows = gather_small(own_rows, "fsdp")
    ordered = jnp.take(member_rows, members, axis=0)
    d_items = jnp.concatenate([ordered[:, 0], ordered[::SPLIT, 1]], 0)
    d_silu = (
        product_nt(d_items[:, :mod_width], w_ada)
        + product_nt(d_items[:, mod_width : mod_width + head_count], w_head_router)
        + product_nt(d_items[:, mod_width + head_count :], w_group_router)
    )
    d_silu = jnp.take(gather_small(d_silu[None], "fsdp"), members, axis=0)
    d_silu = d_silu.transpose(1, 0, 2).reshape(-1, model_width)
    d_short_cond = lax.dynamic_slice_in_dim(d_silu, fsdp_index, 1, 0) * silu_grad(short_cond)
    d_long_cond = d_silu[fsdp_count:] * silu_grad(long_cond)
    replicas = jnp.arange(lax.axis_size("dp")) ^ role
    factors = jnp.take(gather_small(d_items[None], "dp"), replicas, axis=0)
    factors = factors.reshape(-1, factors.shape[2])
    ordered_act = jnp.concatenate([jnp.take(act_rows, members, axis=0), long_act], 0)
    act_factors = jnp.take(gather_small(own_columns(ordered_act)[None], "dp"), replicas, axis=0)
    act_factors = act_factors.reshape(-1, shard_rows)
    g_w_ada = product_tn(act_factors, factors[:, :mod_width])
    g_w_head_router = product_tn(act_factors, factors[:, mod_width : mod_width + head_count])
    g_w_group_router = product_tn(act_factors, factors[:, mod_width + head_count :])
    g_b_ada = lax.dynamic_slice_in_dim(
        jnp.sum(factors[:, :mod_width].astype(jnp.float32), axis=0),
        fsdp_index * b_ada.shape[0],
        b_ada.shape[0],
        0,
    )
    return (
        y_short,
        y_long,
        dx_short,
        dx_long,
        d_short_cond,
        d_long_cond,
        g_w_ada,
        g_b_ada,
        g_w_head_router,
        g_w_group_router,
        g_w_qkv,
        g_w_proj,
        g_b_proj,
        g_w_fc1,
        g_b_fc1,
        g_w_fc2,
        g_b_fc2,
    )


def solution(mesh):
    return jax.shard_map(
        per_device,
        mesh=mesh,
        in_specs=(
            P(("dp", "fsdp"), None, None),
            P(("dp", "fsdp"), None),
            P(("dp", "fsdp"), None),
            P("dp", None),
            P(("dp", "fsdp"), None),
            P("dp", None),
            P(("dp", "fsdp"), None),
            P("dp", None),
            P(("dp", "fsdp"), None),
            P(("dp", "fsdp")),
            P("fsdp", None),
            P("fsdp"),
            P("fsdp", None),
            P("fsdp", None),
            P("fsdp", None),
            P("fsdp", None),
            P("fsdp"),
            P("fsdp", None),
            P("fsdp"),
            P("fsdp", None),
            P("fsdp"),
            P(("dp", "fsdp"), None, None),
            P(("dp", "fsdp"), None),
        ),
        out_specs=(
            P(("dp", "fsdp"), None, None),
            P(("dp", "fsdp"), None),
            P(("dp", "fsdp"), None, None),
            P(("dp", "fsdp"), None),
            P(("dp", "fsdp"), None),
            P("dp", None),
            P("fsdp", None),
            P("fsdp"),
            P("fsdp", None),
            P("fsdp", None),
            P("fsdp", None),
            P("fsdp", None),
            P("fsdp"),
            P("fsdp", None),
            P("fsdp"),
            P("fsdp", None),
            P("fsdp"),
        ),
        check_vma=False,
    )
```

time: 2060 us -> 1150 us (0.56)
  waiting for transfers between devices: 1380 us -> 443 us
  blocking collectives: 279 us -> 0 us
  local copies, waits for them, and re-layouts: 55.8 us -> 282 us
  starting transfers between devices: 2.26 us -> 109 us
  matrix products: 231 us -> 187 us
  other arithmetic: 84.8 us -> 113 us
    reduce_scatter x5 -> x0, waiting for transfers between devices: 635 us -> none  [the longest x3 271 us: per_device(): lax.psum_scatter(shortened(attention_terms), 'fsdp', scatter_dimension=0,...]
    all_gather x5 -> x0, waiting for transfers between devices: 417 us -> none  [the longest x1 174 us: per_device(): lax.all_gather(first_set[0], 'fsdp', axis=0, tiled=True)]
    ppermute x4 -> x110, waiting for transfers between devices: 124 us -> 443 us  [swap(): return lax.ppermute(value, axis, pairs)]
    all_gather x2 -> x0, blocking collectives: 153 us -> none  [the longest x1 120 us: per_device(): lax.all_gather(first_set[2], 'fsdp', axis=0, tiled=True)]
    ppermute x4 -> x110, starting transfers between devices: 1.14 us -> 109 us  [swap(): return lax.ppermute(value, axis, pairs)]
    unnamed x15 -> x0, waiting for transfers between devices: 105 us -> none
    psum x1 -> x0, waiting for transfers between devices: 101 us -> none  [per_device(): lax.psum(shortened(attention_shards + mlp_shards), 'dp')]
    psum x3 -> x0, blocking collectives: 84.9 us -> none  [the longest x1 37.3 us: per_device(): lax.psum((placement * d_modulation[short_count:]).astype(jnp.bfloat16), '...]
  transfers between devices with their start and end apart: 17 -> 110, of which waited for: 12 -> 42; matrix products, arithmetic and copies ran while one was open for 11% -> 33% of each run, Pallas kernels for 0% -> 0%
where the time goes in v1:
time: 1150 us; the launch traced here: 1140 us
  waiting for transfers between devices  443 us (39%)
  local copies, waits for them, and re-layouts  282 us (25%)
  matrix products  187 us (16%)
  other arithmetic  113 us (10%)
  starting transfers between devices  109 us (9%)
    ppermute x110, waiting for transfers between devices, swap(): return lax.ppermute(value, axis, pairs)  443 us
    ppermute x110, starting transfers between devices, swap(): return lax.ppermute(value, axis, pairs)  109 us
    dynamic_update_slice x48, local copies, waits for them, and re-layouts, place(): return lax.dynamic_update_slice(buffer, block, where)  76.9 us
    dot_general x15, matrix products, product(): return jnp.dot(left, right, preferred_element_type=jnp.float32)  48 us
    dot_general x15, matrix products, product_tn(): lax.dot_general(left, right, (((0,), (0,)), ((), ())), preferred_element_...  46.8 us
    dot_general x15, matrix products, product_nt(): lax.dot_general(left, right, (((1,), (1,)), ((), ())), preferred_element_...  38.2 us
    unnamed x401, local copies, waits for them, and re-layouts  33.7 us
  transfers between devices with their start and end apart: 110, of which 42 were waited for; matrix products, arithmetic and copies ran while one was open for 33% of the time, Pallas kernels for 0%

profile of v1, /device:TPU:0, one launch (start us, length us, event | category | flops | bytes accessed | tf_op | source)
XLA Modules:
  0.0 1137.1 jit_solution(10740295844335306288)
XLA Ops:
  72.1 5.9 collective-permute-done.3
  92.9 16.3 %collective-permute-done.4 = f32[3,6964]{1,0:T(4,128)S(1)} collective-permute-done((f32[3,6964]{1,0:T(4,128)S(1)}, f32[3,6964]{1,0:T(4,128)S(1)}, u32[]{:S(2)}, u32[]{:S(2)}) %collective-permute-start.4) | collective-permute-done | bytes 83600 | tf_op jit(solution)/shard_map/ppermute | solution.py:15
  110.0 4.8 broadcast.349.clone
  161.6 6.7 collective-permute-done.10
  170.5 15.4 %collective-permute-done.33 = bf16[4,144,1152]{2,1,0:T(8,128)(2,1)} collective-permute-done((bf16[4,144,1152]{2,1,0:T(8,128)(2,1)}, bf16[4,144,1152]{2,1,0:T(8,128)(2,1)}, u32[]{:S(2)}, u32[]{:S(2)}) %collective-permute-start.33) | collective-permute-done | bytes 1327136 | tf_op jit(solution)/shard_map/ppermute | solution.py:15
  190.5 6.3 collective-permute-done.34
  199.3 23.2 %collective-permute-done.43 = bf16[4,144,1152]{2,1,0:T(8,128)(2,1)S(1)} collective-permute-done((bf16[4,144,1152]{2,1,0:T(8,128)(2,1)}, bf16[4,144,1152]{2,1,0:T(8,128)(2,1)S(1)}, u32[]{:S(2)}, u32[]{:S(2)}) %collective-permute-start.43) | collective-permute-done | bytes 1327136 | tf_op jit(solution)/shard_map/ppermute | solution.py:15
  224.5 14.0 %collective-permute-done.11 = bf16[4,144,640]{2,1,0:T(8,128)(2,1)S(1)} collective-permute-done((bf16[4,144,640]{2,1,0:T(8,128)(2,1)}, bf16[4,144,640]{2,1,0:T(8,128)(2,1)S(1)}, u32[]{:S(2)}, u32[]{:S(2)}) %collective-permute-start.11) | collective-permute-done | bytes 737312 | tf_op jit(solution)/shard_map/ppermute | solution.py:15
  251.1 8.3 collective-permute-done.21
  265.7 6.3 fusion.259
  316.4 18.8 %collective-permute-done.45 = bf16[4,144,1152]{2,1,0:T(8,128)(2,1)} collective-permute-done((bf16[4,144,1152]{2,1,0:T(8,128)(2,1)}, bf16[4,144,1152]{2,1,0:T(8,128)(2,1)}, u32[]{:S(2)}, u32[]{:S(2)}) %collective-permute-start.45) | collective-permute-done | bytes 1327136 | tf_op jit(solution)/shard_map/ppermute | solution.py:15
  344.1 7.3 collective-permute-done.28
  354.3 20.6 %collective-permute-done.27 = bf16[512,1152]{1,0:T(8,128)(2,1)S(1)} collective-permute-done((bf16[512,1152]{1,0:T(8,128)(2,1)S(1)}, bf16[512,1152]{1,0:T(8,128)(2,1)S(1)}, u32[]{:S(2)}, u32[]{:S(2)}) %collective-permute-start.27) | collective-permute-done | bytes 1179680 | tf_op jit(solution)/shard_map/ppermute | solution.py:15
  384.0 4.4 copy.318
  388.4 4.4 multiply_reduce_fusion.1
  398.6 6.3 fusion.6
  425.5 5.4 fusion.255
  433.2 5.3 convert_reduce_fusion.1
  442.6 7.5 fusion.257
  495.3 11.3 convert_reduce_fusion.2
  518.3 5.1 fusion.245
  524.6 4.9 convolution_add_fusion.12
  535.6 11.7 %convert_reduce_fusion.6 = (f32[1152]{0:T(1024)}, bf16[512,1152]{1,0:T(8,128)(2,1)}, f32[512,1152]{1,0:T(8,128)}, bf16[512,1152]{1,0:T(8,128)(2,1)}, f32[512,1152]{1,0:T(8,128)}, /*index=5*/f32[512,1152]{1,0:T(8,128)}) fusion(f32[256,6912]{1,0:T(8,128)S(1)} %bitcast.603, f32[256,6912]{1,0:T(8,128)} %copy-done.2, f32[512]{0:T(512)} %broadcast_multiply_fusion.2, ...), kind=kOutput, calls=%fused_computation.193 | convolution fusion | flops 1381956480 | bytes 46316032 | tf_op jit(solution)/shard_map/dot_general | solution.py:117
  547.3 4.8 multiply_reduce_fusion.4
  552.2 12.0 %multiply_reduce_fusion = (f32[16,256]{1,0:T(8,128)S(1)}, f32[16,256,1024]{2,1,0:T(8,128)}) fusion(f32[16,256,1024]{2,1,0:T(8,128)} %copy-done.3, f32[16,256]{1,0:T(8,128)S(1)} %log_add_fusion, bf16[1024,16,72]{0,2,1:T(8,128)(2,1)S(1)} %bitcast.657, bf16[512,16,72]{0,2,1:T(8,128)(2,1)S(1)} %get-tuple-element.118), kind=kOutput, calls=%fused_computation.24 | convolution fusion | flops 620752896 | bytes 36536320 | tf_op jit(solution)/shard_map/nqhe,nkhe->nhqk/dot_general | solution.py:195
  564.2 12.1 %multiply_convert_fusion = bf16[16,256,1024]{2,1,0:T(8,128)(2,1)S(1)} fusion(f32[16,256,1024]{2,1,0:T(8,128)} %get-tuple-element.168, f32[16,256,1024]{2,1,0:T(8,128)} %copy-done.3, f32[16,256]{1,0:T(8,128)S(1)} %get-tuple-element.167, f32[16,256]{1,0:T(8,128)S(1)} %log_add_fusion), kind=kLoop, calls=%fused_computation.23 | loop fusion | flops 20971520 | bytes 41975808 | tf_op jit(solution)/shard_map/convert_element_type | solution.py:197
  583.7 5.4 multiply_reduce_fusion.2
  594.8 6.1 fusion.270
  635.9 4.3 copy.328
  661.7 14.5 %pad_maximum_fusion = bf16[4608,1152]{1,0:T(8,128)(2,1)} fusion(bf16[1152,1152]{1,0:T(8,128)(2,1)} %convolution_convert_fusion, bf16[1152,1152]{1,0:T(8,128)(2,1)} %convolution_convert_fusion.1, bf16[1152,1152]{1,0:T(8,128)(2,1)} %convolution_convert_fusion.2, bf16[1152,1152]{1,0:T(8,128)(2,1)} %convolution_convert_fusion.3), kind=kLoop, calls=%fused_computation.31 | loop fusion | flops 42467328 | bytes 21233664 | tf_op jit(solution)/shard_map/concatenate | solution.py:399
  676.2 8.5 constant_dynamic-slice_fusion.4
  701.9 5.2 copy.329
  728.5 10.6 collective-permute-done.51
  797.7 4.4 collective-permute-done.61
  804.7 12.1 %collective-permute-done.65 = bf16[2,10,6964]{2,1,0:T(8,128)(2,1)S(1)} collective-permute-done((bf16[2,10,6964]{2,1,0:T(8,128)(2,1)S(1)}, bf16[2,10,6964]{2,1,0:T(8,128)(2,1)S(1)}, u32[]{:S(2)}, u32[]{:S(2)}) %collective-permute-start.65) | collective-permute-done | bytes 278592 | tf_op jit(solution)/shard_map/ppermute | solution.py:15
  839.2 16.5 %collective-permute-done.69 = bf16[4,144,640]{2,1,0:T(8,128)(2,1)S(1)} collective-permute-done((bf16[4,144,640]{2,1,0:T(8,128)(2,1)S(1)}, bf16[4,144,640]{2,1,0:T(8,128)(2,1)S(1)}, u32[]{:S(2)}, u32[]{:S(2)}) %collective-permute-start.69) | collective-permute-done | bytes 737312 | tf_op jit(solution)/shard_map/ppermute | solution.py:15
  858.0 6.7 collective-permute-done.76
  871.2 43.3 %collective-permute-done.77 = bf16[4,144,512]{2,1,0:T(8,128)(2,1)S(1)} collective-permute-done((bf16[4,144,512]{2,1,0:T(8,128)(2,1)S(1)}, bf16[4,144,512]{2,1,0:T(8,128)(2,1)S(1)}, u32[]{:S(2)}, u32[]{:S(2)}) %collective-permute-start.77) | collective-permute-done | bytes 589856 | tf_op jit(solution)/shard_map/ppermute | solution.py:15
  923.7 9.9 collective-permute-done.79
  937.9 5.9 collective-permute-done.72
  948.5 89.1 %collective-permute-done.82 = bf16[144,1152]{1,0:T(8,128)(2,1)S(1)} collective-permute-done((bf16[144,1152]{1,0:T(8,128)(2,1)S(1)}, bf16[144,1152]{1,0:T(8,128)(2,1)S(1)}, u32[]{:S(2)}, u32[]{:S(2)}) %collective-permute-start.82) | collective-permute-done | bytes 331808 | tf_op jit(solution)/shard_map/ppermute | solution.py:15
  1037.6 9.8 collective-permute-done.83
  1055.7 6.5 collective-permute-done.96
  1062.2 18.5 %collective-permute-done.95 = bf16[144,1152]{1,0:T(8,128)(2,1)S(1)} collective-permute-done((bf16[144,1152]{1,0:T(8,128)(2,1)S(1)}, bf16[144,1152]{1,0:T(8,128)(2,1)S(1)}, u32[]{:S(2)}, u32[]{:S(2)}) %collective-permute-start.95) | collective-permute-done | bytes 331808 | tf_op jit(solution)/shard_map/ppermute | solution.py:15
  1092.8 5.6 collective-permute-done.106
  1098.4 17.9 %collective-permute-done.105 = bf16[144,1152]{1,0:T(8,128)(2,1)S(1)} collective-permute-done((bf16[144,1152]{1,0:T(8,128)(2,1)S(1)}, bf16[144,1152]{1,0:T(8,128)(2,1)S(1)}, u32[]{:S(2)}, u32[]{:S(2)}) %collective-permute-start.105) | collective-permute-done | bytes 331808 | tf_op jit(solution)/shard_map/ppermute | solution.py:15
  1120.5 8.8 collective-permute-done.108
  1129.3 6.1 collective-permute-done.109
  (993 shorter events, 568.5 us)
Async XLA Ops:
  7.5 75.2 %collective-permute-start.6 = (bf16[144,640]{1,0:T(8,128)(2,1)}, bf16[144,640]{1,0:T(8,128)(2,1)}, u32[]{:S(2)}, u32[]{:S(2)}) collective-permute-start(bf16[144,640]{1,0:T(8,128)(2,1)} %get-tuple-element.73), channel_id=1, source_target_pairs={{0,2},{1,3},{2,0},{3,1},{4,6},{5,7},{6,4},{7,5},{8,10},{9,11},{10,... | collective-permute-start | bytes 552968 | tf_op jit(solution)/shard_map/ppermute | solution.py:15
  10.6 77.1 %collective-permute-start.7 = (bf16[144,640]{1,0:T(8,128)(2,1)}, bf16[144,640]{1,0:T(8,128)(2,1)}, u32[]{:S(2)}, u32[]{:S(2)}) collective-permute-start(bf16[144,640]{1,0:T(8,128)(2,1)} %get-tuple-element.73), channel_id=1, source_target_pairs={{0,4},{1,5},{2,6},{3,7},{4,0},{5,1},{6,2},{7,3},{8,12},{9,13},{10,... | collective-permute-start | bytes 552968 | tf_op jit(solution)/shard_map/ppermute | solution.py:15
  13.2 76.1 %collective-permute-start.8 = (bf16[144,640]{1,0:T(8,128)(2,1)}, bf16[144,640]{1,0:T(8,128)(2,1)}, u32[]{:S(2)}, u32[]{:S(2)}) collective-permute-start(bf16[144,640]{1,0:T(8,128)(2,1)} %get-tuple-element.73), channel_id=1, source_target_pairs={{0,6},{1,7},{2,4},{3,5},{4,2},{5,3},{6,0},{7,1},{8,14},{9,15},{10,... | collective-permute-start | bytes 552968 | tf_op jit(solution)/shard_map/ppermute | solution.py:15
  18.2 40.8 %collective-permute-start.16 = (bf16[144,512]{1,0:T(8,128)(2,1)}, bf16[144,512]{1,0:T(8,128)(2,1)}, u32[]{:S(2)}, u32[]{:S(2)}) collective-permute-start(bf16[144,512]{1,0:T(8,128)(2,1)} %get-tuple-element.71), channel_id=1, source_target_pairs={{0,2},{1,3},{2,0},{3,1},{4,6},{5,7},{6,4},{7,5},{8,10},{9,11},{10,... | collective-permute-start | bytes 442376 | tf_op jit(solution)/shard_map/ppermute | solution.py:15
  63.3 69.1 %collective-permute-start.30 = (bf16[144,1152]{1,0:T(8,128)(2,1)}, bf16[144,1152]{1,0:T(8,128)(2,1)}, u32[]{:S(2)}, u32[]{:S(2)}) collective-permute-start(bf16[144,1152]{1,0:T(8,128)(2,1)} %get-tuple-element.63), channel_id=1, source_target_pairs={{0,2},{1,3},{2,0},{3,1},{4,6},{5,7},{6,4},{7,5},{8,10},{9,11},{10,... | collective-permute-start | bytes 995336 | tf_op jit(solution)/shard_map/ppermute | solution.py:15
  78.0 58.1 %collective-permute-start.31 = (bf16[144,1152]{1,0:T(8,128)(2,1)}, bf16[144,1152]{1,0:T(8,128)(2,1)}, u32[]{:S(2)}, u32[]{:S(2)}) collective-permute-start(bf16[144,1152]{1,0:T(8,128)(2,1)} %get-tuple-element.63), channel_id=1, source_target_pairs={{0,4},{1,5},{2,6},{3,7},{4,0},{5,1},{6,2},{7,3},{8,12},{9,13},{10,... | collective-permute-start | bytes 995336 | tf_op jit(solution)/shard_map/ppermute | solution.py:15
  82.7 55.1 %collective-permute-start.32 = (bf16[144,1152]{1,0:T(8,128)(2,1)}, bf16[144,1152]{1,0:T(8,128)(2,1)}, u32[]{:S(2)}, u32[]{:S(2)}) collective-permute-start(bf16[144,1152]{1,0:T(8,128)(2,1)} %get-tuple-element.63), channel_id=1, source_target_pairs={{0,6},{1,7},{2,4},{3,5},{4,2},{5,3},{6,0},{7,1},{8,14},{9,15},{10,... | collective-permute-start | bytes 995336 | tf_op jit(solution)/shard_map/ppermute | solution.py:15
  87.7 56.3 %collective-permute-start.40 = (bf16[144,1152]{1,0:T(8,128)(2,1)S(1)}, bf16[144,1152]{1,0:T(8,128)(2,1)}, u32[]{:S(2)}, u32[]{:S(2)}) collective-permute-start(bf16[144,1152]{1,0:T(8,128)(2,1)S(1)} %copy-done.114), channel_id=1, source_target_pairs={{0,2},{1,3},{2,0},{3,1},{4,6},{5,7},{6,4},{7,5},{8,10},{9,11},{10,... | collective-permute-start | bytes 995336 | tf_op jit(solution)/shard_map/ppermute | solution.py:15
  117.0 31.2 %collective-permute-start.41 = (bf16[144,1152]{1,0:T(8,128)(2,1)S(1)}, bf16[144,1152]{1,0:T(8,128)(2,1)}, u32[]{:S(2)}, u32[]{:S(2)}) collective-permute-start(bf16[144,1152]{1,0:T(8,128)(2,1)S(1)} %copy-done.114), channel_id=1, source_target_pairs={{0,4},{1,5},{2,6},{3,7},{4,0},{5,1},{6,2},{7,3},{8,12},{9,13},{10,... | collective-permute-start | bytes 995336 | tf_op jit(solution)/shard_map/ppermute | solution.py:15
  136.0 107.4 %collective-permute-start.19 = (bf16[4,144,512]{2,1,0:T(8,128)(2,1)}, bf16[4,144,512]{2,1,0:T(8,128)(2,1)}, u32[]{:S(2)}, u32[]{:S(2)}) collective-permute-start(bf16[4,144,512]{2,1,0:T(8,128)(2,1)} %bitcast_dynamic-update-slice_fusion.44), channel_id=1, source_target_pairs={{0,16},{8,24},{16,0},{24,8},{1,17},{9,25},{17,1},{25,9},{2,18},{10... | collective-permute-start | bytes 1769480 | tf_op jit(solution)/shard_map/ppermute | solution.py:15
  148.2 37.8 %collective-permute-start.33 = (bf16[4,144,1152]{2,1,0:T(8,128)(2,1)}, bf16[4,144,1152]{2,1,0:T(8,128)(2,1)}, u32[]{:S(2)}, u32[]{:S(2)}) collective-permute-start(bf16[4,144,1152]{2,1,0:T(8,128)(2,1)} %bitcast_dynamic-update-slice_fusion.36), channel_id=1, source_target_pairs={{0,1},{1,0},{2,3},{3,2},{4,5},{5,4},{6,7},{7,6},{8,9},{9,8},{10,11... | collective-permute-start | bytes 3981320 | tf_op jit(solution)/shard_map/ppermute | solution.py:15
  149.9 46.9 %collective-permute-start.34 = (bf16[4,144,1152]{2,1,0:T(8,128)(2,1)}, bf16[4,144,1152]{2,1,0:T(8,128)(2,1)}, u32[]{:S(2)}, u32[]{:S(2)}) collective-permute-start(bf16[4,144,1152]{2,1,0:T(8,128)(2,1)} %bitcast_dynamic-update-slice_fusion.36), channel_id=1, source_target_pairs={{0,16},{8,24},{16,0},{24,8},{1,17},{9,25},{17,1},{25,9},{2,18},{10... | collective-permute-start | bytes 3981320 | tf_op jit(solution)/shard_map/ppermute | solution.py:15
  157.5 92.5 %collective-permute-start.20 = (bf16[4,144,512]{2,1,0:T(8,128)(2,1)}, bf16[4,144,512]{2,1,0:T(8,128)(2,1)S(1)}, u32[]{:S(2)}, u32[]{:S(2)}) collective-permute-start(bf16[4,144,512]{2,1,0:T(8,128)(2,1)} %bitcast_dynamic-update-slice_fusion.44), channel_id=1, source_target_pairs={{0,1},{1,0},{2,3},{3,2},{4,5},{5,4},{6,7},{7,6},{8,9},{9,8},{10,11... | collective-permute-start | bytes 1769480 | tf_op jit(solution)/shard_map/ppermute | solution.py:15
  168.4 54.1 %collective-permute-start.43 = (bf16[4,144,1152]{2,1,0:T(8,128)(2,1)}, bf16[4,144,1152]{2,1,0:T(8,128)(2,1)S(1)}, u32[]{:S(2)}, u32[]{:S(2)}) collective-permute-start(bf16[4,144,1152]{2,1,0:T(8,128)(2,1)} %bitcast_dynamic-update-slice_fusion.32), channel_id=1, source_target_pairs={{0,16},{8,24},{16,0},{24,8},{1,17},{9,25},{17,1},{25,9},{2,18},{10... | collective-permute-start | bytes 3981320 | tf_op jit(solution)/shard_map/ppermute | solution.py:15
  186.0 38.3 %collective-permute-start.44 = (bf16[4,144,1152]{2,1,0:T(8,128)(2,1)}, bf16[4,144,1152]{2,1,0:T(8,128)(2,1)S(1)}, u32[]{:S(2)}, u32[]{:S(2)}) collective-permute-start(bf16[4,144,1152]{2,1,0:T(8,128)(2,1)} %bitcast_dynamic-update-slice_fusion.32), channel_id=1, source_target_pairs={{0,1},{1,0},{2,3},{3,2},{4,5},{5,4},{6,7},{7,6},{8,9},{9,8},{10,11... | collective-permute-start | bytes 3981320 | tf_op jit(solution)/shard_map/ppermute | solution.py:15
  196.8 42.7 %collective-permute-start.12 = (bf16[4,144,640]{2,1,0:T(8,128)(2,1)}, bf16[4,144,640]{2,1,0:T(8,128)(2,1)S(1)}, u32[]{:S(2)}, u32[]{:S(2)}) collective-permute-start(bf16[4,144,640]{2,1,0:T(8,128)(2,1)} %bitcast_dynamic-update-slice_fusion.40), channel_id=1, source_target_pairs={{0,8},{8,0},{16,24},{24,16},{1,9},{9,1},{17,25},{25,17},{2,10},{10... | collective-permute-start | bytes 2211848 | tf_op jit(solution)/shard_map/ppermute | solution.py:15
  242.0 65.6 %collective-permute-start.36 = (bf16[4,144,1152]{2,1,0:T(8,128)(2,1)}, bf16[4,144,1152]{2,1,0:T(8,128)(2,1)}, u32[]{:S(2)}, u32[]{:S(2)}) collective-permute-start(bf16[4,144,1152]{2,1,0:T(8,128)(2,1)} %bitcast_dynamic-update-slice_fusion.36), channel_id=1, source_target_pairs={{0,8},{8,0},{16,24},{24,16},{1,9},{9,1},{17,25},{25,17},{2,10},{10... | collective-permute-start | bytes 3981320 | tf_op jit(solution)/shard_map/ppermute | solution.py:15
  243.4 95.5 %collective-permute-start.46 = (bf16[4,144,1152]{2,1,0:T(8,128)(2,1)}, bf16[4,144,1152]{2,1,0:T(8,128)(2,1)}, u32[]{:S(2)}, u32[]{:S(2)}) collective-permute-start(bf16[4,144,1152]{2,1,0:T(8,128)(2,1)} %bitcast_dynamic-update-slice_fusion.32), channel_id=1, source_target_pairs={{0,8},{8,0},{16,24},{24,16},{1,9},{9,1},{17,25},{25,17},{2,10},{10... | collective-permute-start | bytes 3981320 | tf_op jit(solution)/shard_map/ppermute | solution.py:15
  261.7 42.1 %collective-permute-start.35 = (bf16[4,144,1152]{2,1,0:T(8,128)(2,1)}, bf16[4,144,1152]{2,1,0:T(8,128)(2,1)}, u32[]{:S(2)}, u32[]{:S(2)}) collective-permute-start(bf16[4,144,1152]{2,1,0:T(8,128)(2,1)} %collective-permute-done.33), channel_id=1, source_target_pairs={{0,16},{8,24},{16,0},{24,8},{1,17},{9,25},{17,1},{25,9},{2,18},{10... | collective-permute-start | bytes 3981320 | tf_op jit(solution)/shard_map/ppermute | solution.py:15
  263.4 46.9 %collective-permute-start.37 = (bf16[4,144,1152]{2,1,0:T(8,128)(2,1)}, bf16[4,144,1152]{2,1,0:T(8,128)(2,1)}, u32[]{:S(2)}, u32[]{:S(2)}) collective-permute-start(bf16[4,144,1152]{2,1,0:T(8,128)(2,1)} %collective-permute-done.33), channel_id=1, source_target_pairs={{0,8},{8,0},{16,24},{24,16},{1,9},{9,1},{17,25},{25,17},{2,10},{10... | collective-permute-start | bytes 3981320 | tf_op jit(solution)/shard_map/ppermute | solution.py:15
  264.3 49.0 %collective-permute-start.38 = (bf16[4,144,1152]{2,1,0:T(8,128)(2,1)}, bf16[4,144,1152]{2,1,0:T(8,128)(2,1)}, u32[]{:S(2)}, u32[]{:S(2)}) collective-permute-start(bf16[4,144,1152]{2,1,0:T(8,128)(2,1)} %collective-permute-done.34), channel_id=1, source_target_pairs={{0,8},{8,0},{16,24},{24,16},{1,9},{9,1},{17,25},{25,17},{2,10},{10... | collective-permute-start | bytes 3981320 | tf_op jit(solution)/shard_map/ppermute | solution.py:15
  303.8 31.4 %collective-permute-start.45 = (bf16[4,144,1152]{2,1,0:T(8,128)(2,1)}, bf16[4,144,1152]{2,1,0:T(8,128)(2,1)}, u32[]{:S(2)}, u32[]{:S(2)}) collective-permute-start(bf16[4,144,1152]{2,1,0:T(8,128)(2,1)} %copy-done.100), channel_id=1, source_target_pairs={{0,1},{1,0},{2,3},{3,2},{4,5},{5,4},{6,7},{7,6},{8,9},{9,8},{10,11... | collective-permute-start | bytes 3981320 | tf_op jit(solution)/shard_map/ppermute | solution.py:15
  307.6 34.5 %collective-permute-start.47 = (bf16[4,144,1152]{2,1,0:T(8,128)(2,1)S(1)}, bf16[4,144,1152]{2,1,0:T(8,128)(2,1)S(1)}, u32[]{:S(2)}, u32[]{:S(2)}) collective-permute-start(bf16[4,144,1152]{2,1,0:T(8,128)(2,1)S(1)} %copy-done.101), channel_id=1, source_target_pairs={{0,8},{8,0},{16,24},{24,16},{1,9},{9,1},{17,25},{25,17},{2,10},{10... | collective-permute-start | bytes 3981320 | tf_op jit(solution)/shard_map/ppermute | solution.py:15
  310.3 42.8 %collective-permute-start.48 = (bf16[4,144,1152]{2,1,0:T(8,128)(2,1)S(1)}, bf16[4,144,1152]{2,1,0:T(8,128)(2,1)S(1)}, u32[]{:S(2)}, u32[]{:S(2)}) collective-permute-start(bf16[4,144,1152]{2,1,0:T(8,128)(2,1)S(1)} %copy-done.99), channel_id=1, source_target_pairs={{0,8},{8,0},{16,24},{24,16},{1,9},{9,1},{17,25},{25,17},{2,10},{10... | collective-permute-start | bytes 3981320 | tf_op jit(solution)/shard_map/ppermute | solution.py:15
  313.3 28.2 %collective-permute-start.26 = (bf16[256,1152]{1,0:T(8,128)(2,1)S(1)}, bf16[256,1152]{1,0:T(8,128)(2,1)S(1)}, u32[]{:S(2)}, u32[]{:S(2)}) collective-permute-start(bf16[256,1152]{1,0:T(8,128)(2,1)S(1)} %copy-done.55), channel_id=1, source_target_pairs={{0,2},{1,3},{2,0},{3,1},{4,6},{5,7},{6,4},{7,5},{8,10},{9,11},{10,... | collective-permute-start | bytes 1769480 | tf_op jit(solution)/shard_map/ppermute | solution.py:15
  339.0 101.0 %collective-permute-start.39 = (bf16[4,144,1152]{2,1,0:T(8,128)(2,1)}, bf16[4,144,1152]{2,1,0:T(8,128)(2,1)}, u32[]{:S(2)}, u32[]{:S(2)}) collective-permute-start(bf16[4,144,1152]{2,1,0:T(8,128)(2,1)} %collective-permute-done.35), channel_id=1, source_target_pairs={{0,8},{8,0},{16,24},{24,16},{1,9},{9,1},{17,25},{25,17},{2,10},{10... | collective-permute-start | bytes 3981320 | tf_op jit(solution)/shard_map/ppermute | solution.py:15
  341.5 108.6 %collective-permute-start.49 = (bf16[4,144,1152]{2,1,0:T(8,128)(2,1)}, bf16[4,144,1152]{2,1,0:T(8,128)(2,1)}, u32[]{:S(2)}, u32[]{:S(2)}) collective-permute-start(bf16[4,144,1152]{2,1,0:T(8,128)(2,1)} %collective-permute-done.45), channel_id=1, source_target_pairs={{0,8},{8,0},{16,24},{24,16},{1,9},{9,1},{17,25},{25,17},{2,10},{10... | collective-permute-start | bytes 3981320 | tf_op jit(solution)/shard_map/ppermute | solution.py:15
  342.1 32.8 %collective-permute-start.27 = (bf16[512,1152]{1,0:T(8,128)(2,1)S(1)}, bf16[512,1152]{1,0:T(8,128)(2,1)S(1)}, u32[]{:S(2)}, u32[]{:S(2)}) collective-permute-start(bf16[512,1152]{1,0:T(8,128)(2,1)S(1)} %pad_maximum_fusion.9), channel_id=1, source_target_pairs={{0,1},{1,0},{2,3},{3,2},{4,5},{5,4},{6,7},{7,6},{8,9},{9,8},{10,11... | collective-permute-start | bytes 3538952 | tf_op jit(solution)/shard_map/ppermute | solution.py:15
  352.6 28.3 %collective-permute-start.29 = (bf16[512,1152]{1,0:T(8,128)(2,1)}, bf16[512,1152]{1,0:T(8,128)(2,1)}, u32[]{:S(2)}, u32[]{:S(2)}) collective-permute-start(bf16[512,1152]{1,0:T(8,128)(2,1)} %pad_maximum_fusion.10), channel_id=1, source_target_pairs={{0,2},{1,3},{2,0},{3,1},{4,6},{5,7},{6,4},{7,5},{8,10},{9,11},{10,... | collective-permute-start | bytes 3538952 | tf_op jit(solution)/shard_map/ppermute | solution.py:15
  640.2 81.1 %collective-permute-start.50 = (bf16[2,256,1152]{2,1,0:T(8,128)(2,1)}, bf16[2,256,1152]{2,1,0:T(8,128)(2,1)}, u32[]{:S(2)}, u32[]{:S(2)}) collective-permute-start(bf16[2,256,1152]{2,1,0:T(8,128)(2,1)} %copy.328), channel_id=1, source_target_pairs={{0,2},{1,3},{2,0},{3,1},{4,6},{5,7},{6,4},{7,5},{8,10},{9,11},{10,... | collective-permute-start | bytes 3538952 | tf_op jit(solution)/shard_map/ppermute | solution.py:15
  652.2 72.9 %collective-permute-start.52 = (bf16[2,256,1152]{2,1,0:T(8,128)(2,1)}, bf16[2,256,1152]{2,1,0:T(8,128)(2,1)}, u32[]{:S(2)}, u32[]{:S(2)}) collective-permute-start(bf16[2,256,1152]{2,1,0:T(8,128)(2,1)} %pad_maximum_fusion.12), channel_id=1, source_target_pairs={{0,1},{1,0},{2,3},{3,2},{4,5},{5,4},{6,7},{7,6},{8,9},{9,8},{10,11... | collective-permute-start | bytes 3538952 | tf_op jit(solution)/shard_map/ppermute | solution.py:15
  661.2 169.2 %collective-permute-start.91 = (bf16[4,2,144,1152]{3,2,0,1:T(8,128)(2,1)}, bf16[4,2,144,1152]{3,2,0,1:T(8,128)(2,1)}, u32[]{:S(2)}, u32[]{:S(2)}) collective-permute-start(bf16[4,2,144,1152]{3,2,0,1:T(8,128)(2,1)} %convolution_convert_fusion.4), channel_id=1, source_target_pairs={{0,8},{8,0},{16,24},{24,16},{1,9},{9,1},{17,25},{25,17},{2,10},{10... | collective-permute-start | bytes 7962632 | tf_op jit(solution)/shard_map/ppermute | solution.py:15
  661.2 205.6 %collective-permute-start.89 = (bf16[4,2,144,1152]{3,2,1,0:T(8,128)(2,1)}, bf16[4,2,144,1152]{3,2,1,0:T(8,128)(2,1)}, u32[]{:S(2)}, u32[]{:S(2)}) collective-permute-start(bf16[4,2,144,1152]{3,2,1,0:T(8,128)(2,1)} %convolution_convert_fusion.5), channel_id=1, source_target_pairs={{0,8},{8,0},{16,24},{24,16},{1,9},{9,1},{17,25},{25,17},{2,10},{10... | collective-permute-start | bytes 7962632 | tf_op jit(solution)/shard_map/ppermute | solution.py:15
  720.0 105.8 %collective-permute-start.101 = (bf16[4,2,144,1152]{3,2,0,1:T(8,128)(2,1)}, bf16[4,2,144,1152]{3,2,0,1:T(8,128)(2,1)}, u32[]{:S(2)}, u32[]{:S(2)}) collective-permute-start(bf16[4,2,144,1152]{3,2,0,1:T(8,128)(2,1)} %bitcast.595), channel_id=1, source_target_pairs={{0,8},{8,0},{16,24},{24,16},{1,9},{9,1},{17,25},{25,17},{2,10},{10... | collective-permute-start | bytes 7962632 | tf_op jit(solution)/shard_map/ppermute | solution.py:15
  795.3 39.3 %collective-permute-start.75 = (bf16[4,2,144,512]{3,2,1,0:T(8,128)(2,1)}, bf16[4,2,144,512]{3,2,1,0:T(8,128)(2,1)}, u32[]{:S(2)}, u32[]{:S(2)}) collective-permute-start(bf16[4,2,144,512]{3,2,1,0:T(8,128)(2,1)} %slice.645), channel_id=1, source_target_pairs={{0,8},{8,0},{16,24},{24,16},{1,9},{9,1},{17,25},{25,17},{2,10},{10... | collective-permute-start | bytes 3538952 | tf_op jit(solution)/shard_map/ppermute | solution.py:15
  816.8 39.7 %collective-permute-start.74 = (bf16[4,2,144,512]{3,2,0,1:T(8,128)(2,1)}, bf16[4,2,144,512]{3,2,0,1:T(8,128)(2,1)}, u32[]{:S(2)}, u32[]{:S(2)}) collective-permute-start(bf16[4,2,144,512]{3,2,0,1:T(8,128)(2,1)} %slice.643), channel_id=1, source_target_pairs={{0,8},{8,0},{16,24},{24,16},{1,9},{9,1},{17,25},{25,17},{2,10},{10... | collective-permute-start | bytes 3538952 | tf_op jit(solution)/shard_map/ppermute | solution.py:15
  836.4 28.3 %collective-permute-start.76 = (bf16[4,2,144,512]{3,2,1,0:T(8,128)(2,1)S(1)}, bf16[4,2,144,512]{3,2,1,0:T(8,128)(2,1)S(1)}, u32[]{:S(2)}, u32[]{:S(2)}) collective-permute-start(bf16[4,2,144,512]{3,2,1,0:T(8,128)(2,1)S(1)} %fusion.68), channel_id=1, source_target_pairs={{0,16},{8,24},{16,0},{24,8},{1,17},{9,25},{17,1},{25,9},{2,18},{10... | collective-permute-start | bytes 3538952 | tf_op jit(solution)/shard_map/ppermute | solution.py:15
  838.8 215.2 %collective-permute-start.100 = (bf16[4,2,144,1152]{3,2,0,1:T(8,128)(2,1)S(1)}, bf16[4,2,144,1152]{3,2,0,1:T(8,128)(2,1)S(1)}, u32[]{:S(2)}, u32[]{:S(2)}) collective-permute-start(bf16[4,2,144,1152]{3,2,0,1:T(8,128)(2,1)S(1)} %bitcast.690), channel_id=1, source_target_pairs={{0,8},{8,0},{16,24},{24,16},{1,9},{9,1},{17,25},{25,17},{2,10},{10... | collective-permute-start | bytes 7962632 | tf_op jit(solution)/shard_map/ppermute | solution.py:15
  855.7 90.0 %collective-permute-start.92 = (bf16[4,144,1152]{2,1,0:T(8,128)(2,1)S(1)}, bf16[4,144,1152]{2,1,0:T(8,128)(2,1)S(1)}, u32[]{:S(2)}, u32[]{:S(2)}) collective-permute-start(bf16[4,144,1152]{2,1,0:T(8,128)(2,1)S(1)} %fusion.88), channel_id=1, source_target_pairs={{0,1},{1,0},{2,3},{3,2},{4,5},{5,4},{6,7},{7,6},{8,9},{9,8},{10,11... | collective-permute-start | bytes 3981320 | tf_op jit(solution)/shard_map/ppermute | solution.py:15
  856.5 58.7 %collective-permute-start.67 = (bf16[4,144,640]{2,1,0:T(8,128)(2,1)S(1)}, bf16[4,144,640]{2,1,0:T(8,128)(2,1)S(1)}, u32[]{:S(2)}, u32[]{:S(2)}) collective-permute-start(bf16[4,144,640]{2,1,0:T(8,128)(2,1)S(1)} %fusion.154), channel_id=1, source_target_pairs={{0,1},{1,0},{2,3},{3,2},{4,5},{5,4},{6,7},{7,6},{8,9},{9,8},{10,11... | collective-permute-start | bytes 2211848 | tf_op jit(solution)/shard_map/ppermute | solution.py:15
  864.7 51.7 %collective-permute-start.70 = (bf16[4,144,640]{2,1,0:T(8,128)(2,1)S(1)}, bf16[4,144,640]{2,1,0:T(8,128)(2,1)S(1)}, u32[]{:S(2)}, u32[]{:S(2)}) collective-permute-start(bf16[4,144,640]{2,1,0:T(8,128)(2,1)S(1)} %fusion.85), channel_id=1, source_target_pairs={{0,16},{8,24},{16,0},{24,8},{1,17},{9,25},{17,1},{25,9},{2,18},{10... | collective-permute-start | bytes 2211848 | tf_op jit(solution)/shard_map/ppermute | solution.py:15
  866.8 47.6 %collective-permute-start.77 = (bf16[4,144,512]{2,1,0:T(8,128)(2,1)S(1)}, bf16[4,144,512]{2,1,0:T(8,128)(2,1)S(1)}, u32[]{:S(2)}, u32[]{:S(2)}) collective-permute-start(bf16[4,144,512]{2,1,0:T(8,128)(2,1)S(1)} %fusion.162), channel_id=1, source_target_pairs={{0,1},{1,0},{2,3},{3,2},{4,5},{5,4},{6,7},{7,6},{8,9},{9,8},{10,11... | collective-permute-start | bytes 1769480 | tf_op jit(solution)/shard_map/ppermute | solution.py:15
  937.2 111.8 %collective-permute-start.90 = (bf16[4,144,1152]{2,1,0:T(8,128)(2,1)S(1)}, bf16[4,144,1152]{2,1,0:T(8,128)(2,1)S(1)}, u32[]{:S(2)}, u32[]{:S(2)}) collective-permute-start(bf16[4,144,1152]{2,1,0:T(8,128)(2,1)S(1)} %fusion.87), channel_id=1, source_target_pairs={{0,1},{1,0},{2,3},{3,2},{4,5},{5,4},{6,7},{7,6},{8,9},{9,8},{10,11... | collective-permute-start | bytes 3981320 | tf_op jit(solution)/shard_map/ppermute | solution.py:15
  943.8 110.2 %collective-permute-start.102 = (bf16[4,2,144,1152]{3,2,0,1:T(8,128)(2,1)}, bf16[4,2,144,1152]{3,2,0,1:T(8,128)(2,1)S(1)}, u32[]{:S(2)}, u32[]{:S(2)}) collective-permute-start(bf16[4,2,144,1152]{3,2,0,1:T(8,128)(2,1)} %fusion.7), channel_id=1, source_target_pairs={{0,16},{8,24},{16,0},{24,8},{1,17},{9,25},{17,1},{25,9},{2,18},{10... | collective-permute-start | bytes 7962632 | tf_op jit(solution)/shard_map/ppermute | solution.py:15
  946.0 103.0 %collective-permute-start.93 = (bf16[4,144,1152]{2,1,0:T(8,128)(2,1)S(1)}, bf16[4,144,1152]{2,1,0:T(8,128)(2,1)S(1)}, u32[]{:S(2)}, u32[]{:S(2)}) collective-permute-start(bf16[4,144,1152]{2,1,0:T(8,128)(2,1)S(1)} %fusion.17), channel_id=1, source_target_pairs={{0,16},{8,24},{16,0},{24,8},{1,17},{9,25},{17,1},{25,9},{2,18},{10... | collective-permute-start | bytes 3981320 | tf_op jit(solution)/shard_map/ppermute | solution.py:15
  947.3 90.2 %collective-permute-start.82 = (bf16[144,1152]{1,0:T(8,128)(2,1)S(1)}, bf16[144,1152]{1,0:T(8,128)(2,1)S(1)}, u32[]{:S(2)}, u32[]{:S(2)}) collective-permute-start(bf16[144,1152]{1,0:T(8,128)(2,1)S(1)} %pad_maximum_fusion.16), channel_id=1, source_target_pairs={{0,16},{8,24},{16,0},{24,8},{1,17},{9,25},{17,1},{25,9},{2,18},{10... | collective-permute-start | bytes 995336 | tf_op jit(solution)/shard_map/ppermute | solution.py:15
  1055.0 30.4 %collective-permute-start.103 = (bf16[4,144,1152]{2,1,0:T(8,128)(2,1)S(1)}, bf16[4,144,1152]{2,1,0:T(8,128)(2,1)S(1)}, u32[]{:S(2)}, u32[]{:S(2)}) collective-permute-start(bf16[4,144,1152]{2,1,0:T(8,128)(2,1)S(1)} %fusion.89), channel_id=1, source_target_pairs={{0,1},{1,0},{2,3},{3,2},{4,5},{5,4},{6,7},{7,6},{8,9},{9,8},{10,11... | collective-permute-start | bytes 3981320 | tf_op jit(solution)/shard_map/ppermute | solution.py:15
  1082.1 34.7 %collective-permute-start.99 = (bf16[144,1152]{1,0:T(8,128)(2,1)S(1)}, bf16[144,1152]{1,0:T(8,128)(2,1)S(1)}, u32[]{:S(2)}, u32[]{:S(2)}) collective-permute-start(bf16[144,1152]{1,0:T(8,128)(2,1)S(1)} %get-tuple-element.46), channel_id=1, source_target_pairs={{0,24},{8,16},{16,8},{24,0},{1,25},{9,17},{17,9},{25,1},{2,26},{10... | collective-permute-start | bytes 995336 | tf_op jit(solution)/shard_map/ppermute | solution.py:15
  (258 other events, 2245.0 us)

commit v2 on v1

--- a/solution.py
+++ b/solution.py
@@ -1,6 +1,11 @@
+import functools
+import math
+
 import jax
 import jax.numpy as jnp
 from jax import lax
+from jax.experimental import pallas as pl
+from jax.experimental.pallas import tpu as pltpu
 from jax.sharding import PartitionSpec as P
 
 CHAN = 128
@@ -15,102 +20,497 @@
     return lax.ppermute(value, axis, pairs)
 
 
-def place(buffer, block, *where):
-    return lax.dynamic_update_slice(buffer, block, where)
-
-
-def gather_small(rows, axis):
-    mask = 1
-    while mask < lax.axis_size(axis):
-        rows = jnp.concatenate([rows, swap(rows, axis, mask)], 0)
-        mask *= 2
-    return rows
-
-
-def gather_blocks(block, y_first):
-    half = lax.axis_size("fsdp") // 2
-    position = lax.axis_index("fsdp") // 2
-    line = jnp.zeros((half,) + block.shape, block.dtype)
-    line = place(line, block[None], position, 0, 0)
-    for step in range(1, half):
-        line = place(line, swap(block, "fsdp", 2 * step)[None], position ^ step, 0, 0)
-    held = {(0, 0): line}
-    if y_first:
-        held[0, 1] = swap(line, "fsdp", 1)
-        held[2, 0] = swap(line, "dp", 2)
-        held[2, 1] = swap(held[0, 1], "dp", 2)
-    else:
-        held[2, 0] = swap(line, "dp", 2)
-        held[0, 1] = swap(line, "fsdp", 1)
-        held[2, 1] = swap(held[2, 0], "fsdp", 1)
-    for role, side in list(held):
-        held[role ^ 1, side] = swap(held[role, side], "dp", 1)
-    return held
-
-
-def stack_roles(parts, rows):
-    role, side = lax.axis_index("dp"), lax.axis_index("fsdp") % 2
-    half = lax.axis_size("fsdp") // 2
-    width = sum(part[0, 0].shape[2] for part in parts)
-    whole = jnp.zeros((4, half, 2, rows, width), jnp.bfloat16)
-    offset = 0
-    for part in parts:
-        for (role_xor, side_xor), line in part.items():
-            whole = place(
-                whole, line[None, :, None], role ^ role_xor, 0, side ^ side_xor, 0, offset
-            )
-        offset += part[0, 0].shape[2]
-    return whole.reshape(4, half * 2 * rows, width)
-
-
-def stack_rows(part, rows):
-    role, side = lax.axis_index("dp"), lax.axis_index("fsdp") % 2
-    half = lax.axis_size("fsdp") // 2
-    width = part[0, 0].shape[2]
-    whole = jnp.zeros((half, 2, 4, rows, width), jnp.bfloat16)
-    for (role_xor, side_xor), line in part.items():
-        whole = place(whole, line[:, None, None], 0, side ^ side_xor, role ^ role_xor, 0, 0)
-    return whole.reshape(half * 8 * rows, width)
-
-
 def low(value):
     return value.astype(jnp.bfloat16)
 
 
-def scatter_blocks(terms, y_first):
+def packed(parts, unit):
+    flat = jnp.concatenate([part.reshape(-1) for part in parts])
+    return jnp.pad(flat, (0, -flat.size % (unit * 128))).reshape(-1, 128)
+
+
+def unpacked(rows, shapes):
+    lead = rows.shape[:-2]
+    flat = rows.reshape(lead + (-1,))
+    parts, start = [], 0
+    for shape in shapes:
+        size = math.prod(shape)
+        parts.append(flat[..., start : start + size].reshape(lead + shape))
+        start += size
+    return parts
+
+
+MESH_IDS = pl.DeviceIdType.MESH
+VMEM_BYTES = 60 * 1024 * 1024
+
+
+def flipped(value, step, size):
+    total, bit = 0, 1
+    while bit < size:
+        digit = (value // bit) % 2
+        total = total + bit * ((digit + 1) % 2 if step & bit else digit)
+        bit *= 2
+    return total
+
+
+def greet(peers):
+    barrier = pltpu.get_barrier_semaphore()
+    for peer in peers:
+        pl.semaphore_signal(barrier, inc=1, device_id=peer, device_id_type=MESH_IDS)
+    pl.semaphore_wait(barrier, len(peers))
+
+
+def remote(source, target, send_sem, recv_sem, peer):
+    return pltpu.make_async_remote_copy(
+        src_ref=source,
+        dst_ref=target,
+        send_sem=send_sem,
+        recv_sem=recv_sem,
+        device_id=peer,
+        device_id_type=MESH_IDS,
+    )
+
+
+def exchange_kernel(axis, size, spread_out, rows_ref, out_ref, send_sem, recv_sem):
+    me = lax.axis_index(axis)
+    greet([{axis: (me + step) % size} for step in range(1, size)])
+
+    def piece(target):
+        return rows_ref.at[target] if spread_out else rows_ref
+
+    sent = []
+    for step in range(1, size):
+        peer = (me + step) % size
+        copy = remote(
+            piece(peer), out_ref.at[me], send_sem.at[step], recv_sem.at[size - step], {axis: peer}
+        )
+        copy.start()
+        sent.append(copy)
+    out_ref[me] = rows_ref[me] if spread_out else rows_ref[...]
+    for step in range(1, size):
+        peer = (me + step) % size
+        remote(
+            piece(peer), out_ref.at[peer], send_sem.at[step], recv_sem.at[step], {axis: peer}
+        ).wait_recv()
+    for copy in sent:
+        copy.wait_send()
+
+
+def exchange(rows, axis, spread_out, number):
+    size = lax.axis_size(axis)
+    block = rows.shape[1:] if spread_out else rows.shape
+    return pl.pallas_call(
+        functools.partial(exchange_kernel, axis, size, spread_out),
+        out_shape=jax.ShapeDtypeStruct((size,) + block, rows.dtype),
+        in_specs=[pl.BlockSpec(memory_space=pltpu.VMEM)],
+        out_specs=pl.BlockSpec(memory_space=pltpu.VMEM),
+        scratch_shapes=[pltpu.SemaphoreType.DMA((size,)), pltpu.SemaphoreType.DMA((size,))],
+        compiler_params=pltpu.CompilerParams(
+            collective_id=number, has_side_effects=True, vmem_limit_bytes=VMEM_BYTES
+        ),
+        name=f"exchange{number}",
+    )(rows)
+
+
+class Place:
+    def __init__(self, half):
+        self.half = half
+        self.role = lax.axis_index("dp")
+        shard = lax.axis_index("fsdp")
+        self.line, self.side = shard // 2, shard % 2
+        self.other_side = (self.side + 1) % 2
+        self.roles = [flipped(self.role, step, 4) for step in range(4)]
+        self.lines = [flipped(self.line, step, half) for step in range(half)]
+        self.sides = [self.side, self.other_side]
+        self.across = {"dp": self.roles[2]}
+        self.beside = {"fsdp": self.line * 2 + self.other_side}
+        self.core = {"dp": self.roles[1]}
+        self.along = [{"fsdp": line * 2 + self.side} for line in self.lines]
+
+    def greet(self, also=()):
+        greet([self.across, self.beside, self.core] + self.along[1:] + list(also))
+
+
+def cut(rows):
+    first = (rows // 2 + 15) // 16 * 16
+    return [(0, first), (first, rows - first)]
+
+
+class GatherUnit:
+    def __init__(self, at, piece, out, by_shard, start, count, side_first, send_sem, recv_sem):
+        self.at, self.piece, self.out, self.by_shard = at, piece, out, by_shard
+        self.rows = pl.ds(start, count)
+        self.side_first, self.send_sem, self.recv_sem = side_first, send_sem, recv_sem
+        self.sent = []
+
+    def view(self, role, line, side):
+        if self.by_shard:
+            return self.out.at[line, side, role, self.rows]
+        return self.out.at[role, line, side, self.rows]
+
+    def send(self, number, source, target, peer):
+        copy = remote(source, target, self.send_sem.at[number], self.recv_sem.at[number], peer)
+        copy.start()
+        self.sent.append(copy)
+
+    def got(self, number, target):
+        remote(
+            target, target, self.send_sem.at[number], self.recv_sem.at[number], self.at.core
+        ).wait_recv()
+
+    def numbers(self):
+        half = self.at.half
+        return half, 2 * half, 3 * half, 3 * half + 1
+
+    def begin(self):
+        at = self.at
+        own = self.piece.at[self.rows]
+        target = self.view(at.role, at.line, at.side)
+        for step in range(1, at.half):
+            self.send(step, own, target, at.along[step])
+        self.fan(0, own, target)
+
+    def fan(self, step, source, target):
+        beside, across, _, _ = self.numbers()
+        self.send(beside + step, source, target, self.at.beside)
+        self.send(across + step, source, target, self.at.across)
+
+    def line_step(self, step):
+        at = self.at
+        view = self.view(at.role, at.lines[step], at.side)
+        self.got(step, view)
+        self.fan(step, view, view)
+
+    def second(self):
+        at, every = self.at, slice(None)
+        beside, across, second, core = self.numbers()
+        for step in range(at.half):
+            if self.side_first:
+                self.got(beside + step, self.view(at.role, at.lines[step], at.other_side))
+            else:
+                self.got(across + step, self.view(at.roles[2], at.lines[step], at.side))
+        own = self.view(at.role, every, at.side)
+        if self.side_first:
+            view = self.view(at.role, every, at.other_side)
+            self.send(second, view, view, at.across)
+        else:
+            view = self.view(at.roles[2], every, at.side)
+            self.send(second, view, view, at.beside)
+        self.send(core, own, own, at.core)
+        self.send(core + 1, view, view, at.core)
+
+    def third(self):
+        at, every = self.at, slice(None)
+        beside, across, second, core = self.numbers()
+        for step in range(at.half):
+            if self.side_first:
+                self.got(across + step, self.view(at.roles[2], at.lines[step], at.side))
+            else:
+                self.got(beside + step, self.view(at.role, at.lines[step], at.other_side))
+        if self.side_first:
+            view = self.view(at.roles[2], every, at.side)
+        else:
+            view = self.view(at.role, every, at.other_side)
+        self.send(core + 2, view, view, at.core)
+        last = self.view(at.roles[2], every, at.other_side)
+        self.got(second, last)
+        self.send(core + 3, last, last, at.core)
+
+    def finish(self):
+        at, every = self.at, slice(None)
+        core = self.numbers()[3]
+        near, far = at.roles[1], at.roles[3]
+        views = [
+            self.view(near, every, at.side),
+            self.view(near, every, at.other_side),
+            self.view(far, every, at.side),
+            self.view(far, every, at.other_side),
+        ]
+        if not self.side_first:
+            views[1], views[2] = views[2], views[1]
+        for step, view in enumerate(views):
+            self.got(core + step, view)
+        for copy in self.sent:
+            copy.wait_send()
+
+
+def gather_kernel(half, by_shard, *refs):
+    count = len(by_shard)
+    pieces, outs = refs[:count], refs[count : 2 * count]
+    send_sem, recv_sem, local_sem = refs[2 * count :]
+    at = Place(half)
+    at.greet()
+    pairs, local = [], []
+    for matrix in range(count):
+        rows = pieces[matrix].shape[0]
+        pairs.append(
+            [
+                GatherUnit(
+                    at,
+                    pieces[matrix],
+                    outs[matrix],
+                    by_shard[matrix],
+                    start,
+                    size,
+                    part == 0,
+                    send_sem.at[2 * matrix + part],
+                    recv_sem.at[2 * matrix + part],
+                )
+                for part, (start, size) in enumerate(cut(rows))
+            ]
+        )
+        target = outs[matrix]
+        if by_shard[matrix]:
+            target = target.at[at.line, at.side, at.role]
+        else:
+            target = target.at[at.role, at.line, at.side]
+        copy = pltpu.make_async_copy(pieces[matrix], target, local_sem.at[matrix])
+        copy.start()
+        local.append(copy)
+    for unit in pairs[0]:
+        unit.begin()
+    for copy in local:
+        copy.wait()
+    for matrix in range(count + 1):
+        if matrix < count:
+            for step in range(1, half):
+                for unit in pairs[matrix]:
+                    unit.line_step(step)
+            if matrix + 1 < count:
+                for unit in pairs[matrix + 1]:
+                    unit.begin()
+            for unit in pairs[matrix]:
+                unit.second()
+        if matrix:
+            for unit in pairs[matrix - 1]:
+                unit.third()
+    for pair in pairs:
+        for unit in pair:
+            unit.finish()
+
+
+def gather(pieces, by_shard, number):
     half = lax.axis_size("fsdp") // 2
-    position = lax.axis_index("fsdp") // 2
-    side = lax.axis_index("fsdp") % 2
-
-    def on_side(value, which):
-        return lax.dynamic_index_in_dim(value, which, 1, keepdims=False)
-
-    far = terms[2] + swap(low(terms[3]), "dp", 1).astype(jnp.float32)
-    near = terms[0] + swap(low(terms[1]), "dp", 1).astype(jnp.float32)
-    if y_first:
-        far = on_side(far, side) + swap(low(on_side(far, side ^ 1)), "fsdp", 1)
-        near = on_side(near, side) + swap(low(on_side(near, side ^ 1)), "fsdp", 1)
-        near = near + swap(low(far), "dp", 2)
-    else:
-        near = near + swap(low(far), "dp", 2)
-        near = on_side(near, side) + swap(low(on_side(near, side ^ 1)), "fsdp", 1)
-
-    def at(index):
-        return lax.dynamic_index_in_dim(near, index, 0, keepdims=False)
-
-    total = at(position)
-    for step in range(1, half):
-        total = total + swap(low(at(position ^ step)), "fsdp", 2 * step)
-    return low(total)
-
-
-def share_roles(block):
-    role = lax.axis_index("dp")
-    whole = jnp.zeros((4,) + block.shape, jnp.float32)
-    whole = place(whole, block[None].astype(jnp.float32), role, 0, 0)
-    for step in range(1, 4):
-        whole = place(whole, swap(block, "dp", step)[None].astype(jnp.float32), role ^ step, 0, 0)
-    return whole
+    count = len(pieces)
+    units = 2 * count
+    any_space = pl.BlockSpec(memory_space=pl.ANY)
+    shapes = []
+    for piece, rows_first in zip(pieces, by_shard):
+        lead = (half, 2, 4) if rows_first else (4, half, 2)
+        shapes.append(jax.ShapeDtypeStruct(lead + piece.shape, piece.dtype))
+    return pl.pallas_call(
+        functools.partial(gather_kernel, half, by_shard),
+        out_shape=shapes,
+        in_specs=[pl.BlockSpec(memory_space=pltpu.VMEM)] * count,
+        out_specs=[any_space] * count,
+        scratch_shapes=[
+            pltpu.SemaphoreType.DMA((units, 3 * half + 5)),
+            pltpu.SemaphoreType.DMA((units, 3 * half + 5)),
+            pltpu.SemaphoreType.DMA((count,)),
+        ],
+        compiler_params=pltpu.CompilerParams(
+            collective_id=number, has_side_effects=True, vmem_limit_bytes=VMEM_BYTES
+        ),
+        name=f"gather{number}",
+    )(*pieces)
+
+
+def accumulate(target, source):
+    rows = target.shape[0]
+    chunk = 16 if rows % 16 == 0 else rows
+
+    def step(index, carry):
+        place_of = pl.ds(pl.multiple_of(index * chunk, chunk), chunk)
+        total = target[place_of].astype(jnp.float32) + source[place_of].astype(jnp.float32)
+        target[place_of] = total.astype(target.dtype)
+        return carry
+
+    lax.fori_loop(0, rows // chunk, step, 0)
+
+
+class ScatterUnit:
+    def __init__(self, at, terms, out, start, count, across_first, send_sem, recv_sem, buffers):
+        self.at, self.terms, self.out = at, terms, out
+        self.rows = pl.ds(start, count)
+        self.across_first, self.send_sem, self.recv_sem = across_first, send_sem, recv_sem
+        self.core_buf, self.first_buf, self.last_buf, self.line_buf = buffers
+        self.sent = []
+        half = at.half
+        self.base_first, self.base_last = 4, 6
+        self.base_line, self.base_share = 6 + half, 6 + 2 * half
+        self.first_peer = at.across if across_first else at.beside
+        self.last_peer = at.beside if across_first else at.across
+
+    def own_terms(self, first, last, core):
+        role_step, side_step = (first, last) if self.across_first else (last, first)
+        role = self.at.roles[2 * role_step + core]
+        return self.terms.at[role, :, self.at.sides[side_step], self.rows]
+
+    def send(self, number, source, target, peer):
+        copy = remote(source, target, self.send_sem.at[number], self.recv_sem.at[number], peer)
+        copy.start()
+        self.sent.append(copy)
+
+    def got(self, number, target):
+        remote(
+            target, target, self.send_sem.at[number], self.recv_sem.at[number], self.at.core
+        ).wait_recv()
+
+    def add_lines(self, target, source):
+        def step(line, carry):
+            accumulate(target.at[line], source.at[line])
+            return carry
+
+        lax.fori_loop(0, self.at.half, step, 0)
+
+    def begin(self):
+        for first in (1, 0):
+            for last in (1, 0):
+                self.send(
+                    2 * first + last,
+                    self.own_terms(first, last, 1),
+                    self.core_buf.at[first, last],
+                    self.at.core,
+                )
+
+    def paired(self, first, last):
+        buffer = self.core_buf.at[first, last]
+        self.got(2 * first + last, buffer)
+        self.add_lines(buffer, self.own_terms(first, last, 0))
+        if first:
+            self.send(self.base_first + last, buffer, self.first_buf.at[last], self.first_peer)
+
+    def joined(self, last):
+        buffer = self.first_buf.at[last]
+        self.got(self.base_first + last, buffer)
+        self.add_lines(buffer, self.core_buf.at[0, last])
+        if last:
+            for step in list(range(self.at.half - 1, 0, -1)) + [0]:
+                line = self.at.lines[step]
+                self.send(
+                    self.base_last + step, buffer.at[line], self.last_buf.at[line], self.last_peer
+                )
+
+    def lined(self, step):
+        line = self.at.lines[step]
+        block = self.last_buf.at[line]
+        self.got(self.base_last + step, block)
+        accumulate(block, self.first_buf.at[0, line])
+        if step:
+            self.send(self.base_line + step, block, self.line_buf.at[step], self.at.along[step])
+
+    def end(self):
+        at = self.at
+        own = self.last_buf.at[at.line]
+        for step in range(1, at.half):
+            self.got(self.base_line + step, self.line_buf.at[step])
+            accumulate(own, self.line_buf.at[step])
+        self.out[at.role, self.rows] = own[...]
+        target = self.out.at[at.role, self.rows]
+        for step in (1, 2, 3):
+            self.send(self.base_share + step, own, target, {"dp": at.roles[step]})
+
+    def finish(self):
+        for step in (1, 2, 3):
+            self.got(self.base_share + step, self.out.at[self.at.roles[step], self.rows])
+        for copy in self.sent:
+            copy.wait_send()
+
+
+def scatter_program(pairs, begun=False):
+    half = pairs[0][0].at.half
+    for pair in pairs:
+        for unit in pair:
+            unit.begin()
+    stages = [
+        [lambda unit: unit.paired(1, 1), lambda unit: unit.paired(1, 0)],
+        [lambda unit: unit.paired(0, 1), lambda unit: unit.paired(0, 0)],
+        [lambda unit: unit.joined(1), lambda unit: unit.joined(0)],
+        [lambda unit, step=step: unit.lined(step) for step in list(range(half - 1, 0, -1)) + [0]],
+        [lambda unit: unit.end()],
+    ]
+    for turn in range(len(stages) + len(pairs) - 1):
+        for index, pair in reversed(list(enumerate(pairs))):
+            if 0 <= turn - index < len(stages):
+                for action in stages[turn - index]:
+                    for unit in pair:
+                        action(unit)
+    for pair in pairs:
+        for unit in pair:
+            unit.finish()
+
+
+def scatter_buffers(half, rows, columns):
+    shapes = []
+    for _, size in cut(rows):
+        for lead in ((2, 2, half), (2, half), (half,), (half,)):
+            shapes.append(pltpu.VMEM(lead + (size, columns), jnp.bfloat16))
+    return shapes
+
+
+def scatter_kernel(half, layout, *refs):
+    inputs = sum(layout)
+    ins, outs = refs[:inputs], refs[inputs : inputs + len(layout)]
+    rest = refs[inputs + len(layout) :]
+    terms, rest = rest[: len(layout)], rest[len(layout) :]
+    send_sem, recv_sem, local_sem, buffers = rest[0], rest[1], rest[2], rest[3:]
+    at = Place(half)
+    local, taken = [], 0
+    for matrix, many in enumerate(layout):
+        for role in range(4):
+            source = ins[taken + role] if many == 4 else ins[taken].at[:, :, role]
+            copy = pltpu.make_async_copy(
+                source, terms[matrix].at[role], local_sem.at[4 * matrix + role]
+            )
+            copy.start()
+            local.append(copy)
+        taken += many
+    at.greet([{"dp": at.roles[3]}])
+    for copy in local:
+        copy.wait()
+    pairs = []
+    for matrix in range(len(layout)):
+        pairs.append(
+            [
+                ScatterUnit(
+                    at,
+                    terms[matrix],
+                    outs[matrix],
+                    start,
+                    size,
+                    part == 0,
+                    send_sem.at[2 * matrix + part],
+                    recv_sem.at[2 * matrix + part],
+                    buffers[4 * (2 * matrix + part) : 4 * (2 * matrix + part) + 4],
+                )
+                for part, (start, size) in enumerate(cut(terms[matrix].shape[3]))
+            ]
+        )
+    scatter_program(pairs)
+
+
+def scatter(gradients, number):
+    half = lax.axis_size("fsdp") // 2
+    layout = tuple(len(gradient) for gradient in gradients)
+    flat = [block for gradient in gradients for block in gradient]
+    rows, columns = flat[0].shape[-2:]
+    count = len(layout)
+    scratch = [pltpu.VMEM((4, half, 2, rows, columns), jnp.bfloat16)] * count
+    scratch += [pltpu.SemaphoreType.DMA((2 * count, 2 * half + 10))] * 2
+    scratch += [pltpu.SemaphoreType.DMA((4 * count,))]
+    for _ in range(count):
+        scratch += scatter_buffers(half, rows, columns)
+    return pl.pallas_call(
+        functools.partial(scatter_kernel, half, layout),
+        out_shape=[jax.ShapeDtypeStruct((4, rows, columns), jnp.bfloat16)] * count,
+        in_specs=[pl.BlockSpec(memory_space=pl.ANY)] * len(flat),
+        out_specs=[pl.BlockSpec(memory_space=pltpu.VMEM)] * count,
+        scratch_shapes=scratch,
+        compiler_params=pltpu.CompilerParams(
+            collective_id=number, has_side_effects=True, vmem_limit_bytes=VMEM_BYTES
+        ),
+        name=f"scatter{number}",
+    )(*flat)
 
 
 def product(left, right):
@@ -254,41 +654,20 @@
     fsdp_count = lax.axis_size("fsdp")
     role = lax.axis_index("dp")
     group_row = fsdp_index // SPLIT
-    first_member = (fsdp_index % SPLIT == 0).astype(jnp.float32)
-    group_total = fsdp_count // SPLIT
     half = fsdp_count // 2
     shard_rows = w_qkv.shape[0]
     unit_rows = w_fc2.shape[0] // 4
-    first_columns = (model_width // 256 + 1) * 128
-
-    def block_of(matrix, start, width):
-        return lax.dynamic_slice_in_dim(matrix, start, width, 1)
-
-    mixed_shard = jnp.concatenate([w_qkv, w_proj], 1)
-    first_part = gather_blocks(block_of(mixed_shard, role * model_width, first_columns), True)
-    second_part = gather_blocks(
-        block_of(mixed_shard, role * model_width + first_columns, model_width - first_columns), False
-    )
-    attention_full = stack_roles([first_part, second_part], shard_rows)
-    fc1_part = gather_blocks(block_of(w_fc1, role * model_width, model_width), True)
-    fc2_part = gather_blocks(lax.dynamic_slice_in_dim(w_fc2, role * unit_rows, unit_rows, 0), False)
     short_act = low(jax.nn.silu(short_cond))
     long_act = low(jax.nn.silu(long_cond))
-    message = jnp.concatenate([short_act, b_proj[None], b_fc1[None], b_fc2[None]], 1)
-    message = gather_small(message, "fsdp")
-    members = jnp.arange(fsdp_count) ^ fsdp_index
-    act_rows = message[:, :model_width]
-    biases = jnp.take(message[:, model_width:], members, axis=0).astype(jnp.float32)
-    proj_bias = biases[:, :shard_rows].reshape(-1)
-    fc1_bias = biases[:, shard_rows : shard_rows + 4 * shard_rows].reshape(-1)
-    fc2_bias = biases[:, 5 * shard_rows :].reshape(-1)
-    groups = jnp.arange(group_total) ^ group_row
-    item_act = jnp.concatenate([act_rows, jnp.take(long_act, groups, axis=0)], 0)
-
-    def own_columns(rows):
-        return lax.dynamic_slice_in_dim(rows, fsdp_index * shard_rows, shard_rows, 1)
-
-    item_columns = own_columns(item_act)
+    message = exchange(packed([short_act, b_proj, b_fc1, b_fc2], 16), "fsdp", False, 0)
+    act_rows, proj_bias, fc1_bias, fc2_bias = unpacked(
+        message, [(model_width,), b_proj.shape, b_fc1.shape, b_fc2.shape]
+    )
+    proj_bias, fc1_bias, fc2_bias = (
+        bias.reshape(-1).astype(jnp.float32) for bias in (proj_bias, fc1_bias, fc2_bias)
+    )
+    item_act = jnp.concatenate([act_rows, long_act], 0)
+    item_columns = lax.dynamic_slice_in_dim(item_act, fsdp_index * shard_rows, shard_rows, 1)
     bias_row = lax.dynamic_update_slice_in_dim(
         jnp.zeros((fsdp_count * b_ada.shape[0],), jnp.float32),
         b_ada.astype(jnp.float32),
@@ -303,19 +682,17 @@
         ],
         1,
     )
-    short_part, long_part = partial[:fsdp_count], partial[fsdp_count:]
-    mask = fsdp_count // 2
-    while mask:
-        if mask >= SPLIT:
-            step = mask // SPLIT
-            taken = swap(jnp.concatenate([short_part[mask:], long_part[step:]], 0), "fsdp", mask)
-            long_part = long_part[:step] + taken[mask:]
-        else:
-            taken = swap(jnp.concatenate([short_part[mask:], long_part], 0), "fsdp", mask)
-            long_part = long_part + taken[mask:]
-        short_part = short_part[:mask] + taken[:mask]
-        mask //= 2
-    conditioned = jnp.concatenate([short_part, long_part], 0)
+    width = partial.shape[1]
+    for_device = jnp.stack(
+        [partial[:fsdp_count], jnp.repeat(partial[fsdp_count:], SPLIT, axis=0)], 1
+    ).reshape(fsdp_count, -1)
+    for_device = jnp.pad(for_device, ((0, 0), (0, -for_device.shape[1] % 1024)))
+    shares = exchange(for_device.reshape(fsdp_count, -1, 128), "fsdp", True, 1)
+    conditioned = unpacked(jnp.sum(shares, axis=0), [(2, width)])[0]
+    mixed_shard = jnp.concatenate([w_qkv, w_proj], 1)
+    attention_piece = lax.dynamic_slice_in_dim(mixed_shard, role * model_width, model_width, 1)
+    (attention_full,) = gather([attention_piece], (False,), 2)
+    attention_full = attention_full.reshape(4, -1, model_width)
     mod_width = 6 * model_width
     modulation = conditioned[:, :mod_width]
     head_sigmoid = jax.nn.sigmoid(conditioned[:, mod_width : mod_width + head_count])
@@ -341,6 +718,13 @@
     hidden1 = low(normed1 * (1.0 + scale1) + shift1)
     q_rows, k_rows, v_rows = (low(product(hidden1, attention_full[part])) for part in range(3))
 
+    fc1_piece = lax.dynamic_slice_in_dim(w_fc1, role * model_width, model_width, 1)
+    fc2_piece = lax.dynamic_slice_in_dim(w_fc2, role * unit_rows, unit_rows, 0)
+    q_rows, k_rows, v_rows, fc1_piece, fc2_piece = lax.optimization_barrier(
+        (q_rows, k_rows, v_rows, fc1_piece, fc2_piece)
+    )
+    fc1_full, fc2_full = gather([fc1_piece, fc2_piece], (False, True), 3)
+
     def split_heads(rows, count):
         return rows.reshape(count, -1, head_count, head_width)
 
@@ -370,8 +754,7 @@
     attention = low((head_rows * head_gate_rows).reshape(row_count, model_width))
     projected = product(attention, attention_full[3]) + proj_bias
     mixed = x_rows + gate1 * projected
-    fc1_full = stack_roles([fc1_part], shard_rows)
-    fc2_full = stack_rows(fc2_part, unit_rows)
+    fc1_full = fc1_full.reshape(4, -1, model_width)
     fc2_full = fc2_full.reshape(4, -1, model_width)
     normed2, inverse2 = norm_parts(mixed)
     hidden2 = low(normed2 * (1.0 + scale2) + shift2)
@@ -398,11 +781,6 @@
     slot_gate2 = slot_sum(gradient * keep_rows * down_rows, short_count, len_short)
     grad_fc2 = jnp.concatenate([low(product_tn(part, d_down)) for part in activated], 0)
     grad_fc2 = grad_fc2.reshape(half, 2, 4, unit_rows, model_width)
-    fc2_terms = [
-        lax.dynamic_index_in_dim(grad_fc2, role ^ step, 2, keepdims=False) for step in range(4)
-    ]
-    fc2_block = scatter_blocks(fc2_terms, False)
-    g_w_fc2 = share_roles(fc2_block).reshape(4 * unit_rows, model_width)
     d_ups, d_groups = [], []
     d_hidden2 = 0.0
     for part in range(4):
@@ -412,17 +790,15 @@
         d_ups.append(low(pulls[part](d_activated * gates[part])[0]))
         d_hidden2 = d_hidden2 + product_nt(d_ups[part], fc1_full[part])
     d_group = jnp.concatenate(d_groups, 1)
-    up_stack = jnp.stack(d_ups)
-
-    def role_term(left, right):
-        return product_tn(left, right).reshape(half, 2, shard_rows, -1)
-
-    fc1_terms = [
-        role_term(hidden2, lax.dynamic_index_in_dim(up_stack, role ^ step, 0, keepdims=False))
-        for step in range(4)
-    ]
-    fc1_block = scatter_blocks(fc1_terms, True)
-    g_w_fc1 = share_roles(fc1_block).transpose(1, 0, 2).reshape(shard_rows, -1)
+
+    def blocks(grad):
+        return low(grad).reshape(half, 2, shard_rows, model_width)
+
+    fc1_sum, fc2_sum = scatter(
+        [[blocks(product_tn(hidden2, d_up)) for d_up in d_ups], [grad_fc2]], 4
+    )
+    g_w_fc1 = fc1_sum.transpose(1, 0, 2).reshape(shard_rows, -1).astype(jnp.float32)
+    g_w_fc2 = fc2_sum.reshape(-1, model_width).astype(jnp.float32)
     slot_shift2 = slot_sum(d_hidden2, short_count, len_short)
     slot_scale2 = slot_sum(d_hidden2 * normed2, short_count, len_short)
     d_mixed = gradient + norm_back(d_hidden2 * (1.0 + scale2), normed2, inverse2)
@@ -437,20 +813,7 @@
         [jnp.sum(d_projected, axis=0, dtype=jnp.float32)]
         + [jnp.sum(d_up, axis=0, dtype=jnp.float32) for d_up in d_ups]
         + [jnp.sum(d_down, axis=0, dtype=jnp.float32)]
-    )[None]
-    for axis in ("fsdp", "dp"):
-        mask = 1
-        while mask < lax.axis_size(axis):
-            bias_grad = bias_grad + swap(bias_grad, axis, mask)
-            mask *= 2
-    bias_grad = bias_grad[0]
-
-    def own_bias(start, count):
-        return lax.dynamic_slice_in_dim(bias_grad, start + fsdp_index * count, count, 0)
-
-    g_b_proj = own_bias(0, shard_rows)
-    g_b_fc1 = own_bias(model_width, 4 * shard_rows)
-    g_b_fc2 = own_bias(5 * model_width, shard_rows)
+    )
     long_dq, long_dk, long_dv = attend_back(
         long_queries, long_keys, long_values, long_log, split_heads(d_heads[short_rows:], 1), scaling
     )
@@ -477,24 +840,19 @@
         )
 
     dq_rows, dk_rows, dv_rows = join(short_dq, long_dq), join(short_dk, own_dk), join(short_dv, own_dv)
-    right_stack = jnp.stack([dq_rows, dk_rows, dv_rows, d_projected])
-    left_stack = jnp.stack([hidden1, attention])
-    attention_terms = []
-    for step in range(4):
-        which = role ^ step
-        right = lax.dynamic_index_in_dim(right_stack, which, 0, keepdims=False)
-        left = lax.dynamic_index_in_dim(left_stack, which // 3, 0, keepdims=False)
-        attention_terms.append(role_term(left, right))
-    attention_block = jnp.concatenate(
+    (attention_sum,) = scatter(
         [
-            scatter_blocks([term[..., :first_columns] for term in attention_terms], True),
-            scatter_blocks([term[..., first_columns:] for term in attention_terms], False),
+            [
+                blocks(product_tn(hidden1, dq_rows)),
+                blocks(product_tn(hidden1, dk_rows)),
+                blocks(product_tn(hidden1, dv_rows)),
+                blocks(product_tn(attention, d_projected)),
+            ]
         ],
-        1,
-    )
-    attention_grad = share_roles(attention_block)
-    g_w_qkv = attention_grad[:3].transpose(1, 0, 2).reshape(shard_rows, -1)
-    g_w_proj = attention_grad[3]
+        5,
+    )
+    g_w_qkv = attention_sum[:3].transpose(1, 0, 2).reshape(shard_rows, -1).astype(jnp.float32)
+    g_w_proj = attention_sum[3].astype(jnp.float32)
     d_hidden1 = (
         product_nt(dq_rows, attention_full[0])
         + product_nt(dk_rows, attention_full[1])
@@ -520,28 +878,27 @@
         ],
         1,
     )
-    long_sum = d_conditioned[short_count:]
-    for mask in (1, 2):
-        long_sum = long_sum + swap(long_sum, "fsdp", mask)
-    own_rows = low(jnp.concatenate([d_conditioned[:short_count], long_sum], 0))[None]
-    member_rows = gather_small(own_rows, "fsdp")
-    ordered = jnp.take(member_rows, members, axis=0)
-    d_items = jnp.concatenate([ordered[:, 0], ordered[::SPLIT, 1]], 0)
+    member_rows = exchange(packed([low(d_conditioned), low(bias_grad)], 16), "fsdp", False, 6)
+    member_rows, bias_rows = unpacked(member_rows, [(2, width), bias_grad.shape])
+    long_sum = jnp.sum(
+        member_rows[:, 1].astype(jnp.float32).reshape(-1, SPLIT, width), axis=1
+    )
+    d_items = jnp.concatenate([member_rows[:, 0], low(long_sum)], 0)
+    group_bias = jnp.sum(bias_rows.astype(jnp.float32), axis=0)
     d_silu = (
         product_nt(d_items[:, :mod_width], w_ada)
         + product_nt(d_items[:, mod_width : mod_width + head_count], w_head_router)
         + product_nt(d_items[:, mod_width + head_count :], w_group_router)
     )
-    d_silu = jnp.take(gather_small(d_silu[None], "fsdp"), members, axis=0)
+    d_silu = unpacked(exchange(packed([d_silu], 8), "fsdp", False, 7), [d_silu.shape])[0]
     d_silu = d_silu.transpose(1, 0, 2).reshape(-1, model_width)
     d_short_cond = lax.dynamic_slice_in_dim(d_silu, fsdp_index, 1, 0) * silu_grad(short_cond)
     d_long_cond = d_silu[fsdp_count:] * silu_grad(long_cond)
-    replicas = jnp.arange(lax.axis_size("dp")) ^ role
-    factors = jnp.take(gather_small(d_items[None], "dp"), replicas, axis=0)
-    factors = factors.reshape(-1, factors.shape[2])
-    ordered_act = jnp.concatenate([jnp.take(act_rows, members, axis=0), long_act], 0)
-    act_factors = jnp.take(gather_small(own_columns(ordered_act)[None], "dp"), replicas, axis=0)
-    act_factors = act_factors.reshape(-1, shard_rows)
+    replicas = exchange(packed([d_items, low(group_bias), item_columns], 16), "dp", False, 8)
+    factors, bias_rows, act_factors = unpacked(
+        replicas, [d_items.shape, group_bias.shape, item_columns.shape]
+    )
+    factors, act_factors = factors.reshape(-1, width), act_factors.reshape(-1, shard_rows)
     g_w_ada = product_tn(act_factors, factors[:, :mod_width])
     g_w_head_router = product_tn(act_factors, factors[:, mod_width : mod_width + head_count])
     g_w_group_router = product_tn(act_factors, factors[:, mod_width + head_count :])
@@ -551,6 +908,14 @@
         b_ada.shape[0],
         0,
     )
+    bias_sum = jnp.sum(bias_rows.astype(jnp.float32), axis=0)
+
+    def own_bias(start, count):
+        return lax.dynamic_slice_in_dim(bias_sum, start + fsdp_index * count, count, 0)
+
+    g_b_proj = own_bias(0, shard_rows)
+    g_b_fc1 = own_bias(model_width, 4 * shard_rows)
+    g_b_fc2 = own_bias(5 * model_width, shard_rows)
     return (
         y_short,
         y_long,

time: 1150 us -> 920 us (0.80)
  Pallas kernels: 0 us -> 457 us
  waiting for transfers between devices: 443 us -> 30.5 us
  local copies, waits for them, and re-layouts: 282 us -> 126 us
  starting transfers between devices: 109 us -> 7.64 us
    pallas_call x0 -> x9, Pallas kernels: none -> 457 us  [the longest x2 235 us: scatter(): pl.pallas_call(functools.partial(scatter_kernel, half, layout), out_shape...]
    ppermute x110 -> x8, waiting for transfers between devices: 443 us -> 30.5 us  [swap(): return lax.ppermute(value, axis, pairs)]
    ppermute x110 -> x8, starting transfers between devices: 109 us -> 7.64 us  [swap(): return lax.ppermute(value, axis, pairs)]
    dynamic_update_slice x48 -> x0, local copies, waits for them, and re-layouts: 76.9 us -> none  [place(): return lax.dynamic_update_slice(buffer, block, where)]
    concatenate x1, other arithmetic: 14.5 us -> 27.9 us  [per_device(): jnp.concatenate([low(product_tn(part, d_down)) for part in activated], 0)]
    dynamic_slice x5 -> x3, local copies, waits for them, and re-layouts: 15.2 us -> 3.16 us  [the longest x1 1.86 us: per_device(): fc2_piece = lax.dynamic_slice_in_dim(w_fc2, role * unit_rows, unit_rows, 0)]
    unnamed x401 -> x329, local copies, waits for them, and re-layouts: 33.7 us -> 38.8 us
  transfers between devices with their start and end apart: 110 -> 8, of which waited for: 42 -> 2; matrix products, arithmetic and copies ran while one was open for 33% -> 11% of each run, Pallas kernels for 0% -> 28%
where the time goes in v2:
time: 920 us; the launch traced here: 915 us
  Pallas kernels  457 us (50%)
  matrix products  177 us (19%)
  local copies, waits for them, and re-layouts  126 us (14%)
  other arithmetic  113 us (12%)
  waiting for transfers between devices  30.5 us (3%)
    pallas_call x2, Pallas kernels, scatter(): pl.pallas_call(functools.partial(scatter_kernel, half, layout), out_shape...  235 us
    pallas_call x2, Pallas kernels, gather(): pl.pallas_call(functools.partial(gather_kernel, half, by_shard), out_shap...  169 us
    pallas_call x5, Pallas kernels, exchange(): pl.pallas_call(functools.partial(exchange_kernel, axis, size, spread_out)...  53.2 us
    dot_general x15, matrix products, product_tn(): lax.dot_general(left, right, (((0,), (0,)), ((), ())), preferred_element_...  44.9 us
    dot_general x15, matrix products, product_nt(): lax.dot_general(left, right, (((1,), (1,)), ((), ())), preferred_element_...  42.2 us
    dot_general x15, matrix products, product(): return jnp.dot(left, right, preferred_element_type=jnp.float32)  39.4 us
    unnamed x329, local copies, waits for them, and re-layouts  38.8 us
    ppermute x8, waiting for transfers between devices, swap(): return lax.ppermute(value, axis, pairs)  30.5 us
  transfers between devices with their start and end apart: 8, of which 2 were waited for; matrix products, arithmetic and copies ran while one was open for 11% of the time, Pallas kernels for 28%

profile of v2, /device:TPU:0, one launch (start us, length us, event | category | flops | bytes accessed | tf_op | source)
XLA Modules:
  0.0 914.7 jit_solution(2293910858729203422)
XLA Ops:
  4.8 9.8 %exchange0.1 = bf16[8,16,128]{2,1,0:T(8,128)(2,1)} custom-call(bf16[16,128]{1,0:T(8,128)(2,1)} %pad_bitcast_fusion.4.rows_ref), custom_call_target="tpu_custom_call" | custom-call | tf_op jit(solution)/shard_map/exchange0/pallas_call | solution.py:102
  24.5 12.6 %exchange1.1 = f32[8,112,128]{2,1,0:T(8,128)} custom-call(f32[8,112,128]{2,1,0:T(8,128)} %bitcast.362), custom_call_target="tpu_custom_call" | custom-call | tf_op jit(solution)/shard_map/exchange1/pallas_call | solution.py:102
  44.7 61.0 %gather2.1 = bf16[4,4,2,144,1152]{4,3,2,1,0:T(8,128)(2,1)} custom-call(bf16[144,1152]{1,0:T(8,128)(2,1)} %get-tuple-element.159.refs_0_), custom_call_target="tpu_custom_call" | custom-call | tf_op jit(solution)/shard_map/gather2/pallas_call | solution.py:301
  105.8 6.2 fusion.166
  132.9 3.3 collective-permute-start.2
  143.8 108.0 %gather3.1 = (bf16[4,4,2,144,1152]{4,3,2,1,0:T(8,128)(2,1)}, bf16[4,2,4,144,1152]{4,3,2,1,0:T(8,128)(2,1)}) custom-call(bf16[144,1152]{1,0:T(8,128)(2,1)} %get-tuple-element.29.refs_0_, bf16[144,1152]{1,0:T(8,128)(2,1)} %constant_dynamic-slice_fusion.2.refs_1_), custom_call_target="tpu_custom_call" | custom-call | tf_op jit(solution)/shard_map/gather3/pallas_call | solution.py:301
  251.9 8.0 fusion.165
  262.6 4.7 fusion.164
  291.0 18.1 %collective-permute-done.1 = bf16[512,1152]{1,0:T(8,128)(2,1)S(1)} collective-permute-done((bf16[512,1152]{1,0:T(8,128)(2,1)S(1)}, bf16[512,1152]{1,0:T(8,128)(2,1)S(1)}, u32[]{:S(2)}, u32[]{:S(2)}) %collective-permute-start.1) | collective-permute-done | bytes 1179680 | tf_op jit(solution)/shard_map/ppermute | solution.py:20
  312.0 4.3 copy.159
  319.5 4.3 copy.161
  323.8 4.4 multiply_reduce_fusion.1
  328.1 3.6 fusion
  334.6 8.9 fusion.6
  346.5 3.7 fusion.163
  355.3 3.4 fusion.96
  359.1 4.1 convolution_add_fusion.9
  363.2 3.4 fusion.95
  367.0 4.1 convolution_add_fusion.11
  371.1 3.6 fusion.94
  375.0 4.1 convolution_add_fusion.13
  379.1 3.4 fusion.93
  397.9 4.1 convolution_add_fusion.6
  402.0 11.5 %fusion.154 = (bf16[1152]{0:T(1024)(128)(2,1)}, bf16[512,1152]{1,0:T(8,128)(2,1)}, bf16[1152]{0:T(1024)(128)(2,1)}, bf16[512,1152]{1,0:T(8,128)(2,1)}, bf16[1152...) fusion(f32[512,1152]{1,0:T(8,128)S(1)} %copy-done.17, ...), kind=kLoop, calls=%fused_computation.365 | loop fusion | flops 54259200 | bytes 33039360 | tf_op jit(solution)/shard_map/reduce_sum | solution.py:814
  413.5 3.6 fusion.180
  419.3 3.3 convolution_add_fusion.4
  424.6 9.0 fusion.150
  433.7 5.0 fusion.162
  440.7 11.8 %multiply_reduce_fusion = (f32[16,256]{1,0:T(8,128)S(1)}, f32[16,256,1024]{2,1,0:T(8,128)}) fusion(f32[16,256,1024]{2,1,0:T(8,128)} %copy-done.3, f32[16,256]{1,0:T(8,128)S(1)} %log_add_fusion, bf16[1024,16,72]{0,2,1:T(8,128)(2,1)S(1)} %bitcast.307, bf16[512,16,72]{0,2,1:T(8,128)(2,1)S(1)} %get-tuple-element.107), kind=kOutput, calls=%fused_computation.17 | convolution fusion | flops 620752896 | bytes 36536320 | tf_op jit(solution)/shard_map/nqhe,nkhe->nhqk/dot_general | solution.py:595
  452.6 12.0 %multiply_convert_fusion = bf16[16,256,1024]{2,1,0:T(8,128)(2,1)S(1)} fusion(f32[16,256,1024]{2,1,0:T(8,128)} %get-tuple-element.153, f32[16,256,1024]{2,1,0:T(8,128)} %copy-done.3, f32[16,256]{1,0:T(8,128)S(1)} %get-tuple-element.152, f32[16,256]{1,0:T(8,128)S(1)} %log_add_fusion), kind=kLoop, calls=%fused_computation.16 | loop fusion | flops 20971520 | bytes 41975808 | tf_op jit(solution)/shard_map/convert_element_type | solution.py:597
  474.1 3.3 multiply_convert_fusion.1
  480.8 6.4 fusion.177
  487.2 4.2 fusion.82
  492.4 3.3 fusion.97
  508.8 3.3 convolution_convert_fusion.4
  512.2 3.8 convolution_convert_fusion
  516.0 3.6 convolution_convert_fusion.1
  519.6 3.6 convolution_convert_fusion.2
  523.3 3.5 convolution_convert_fusion.3
  526.8 3.9 slice.412
  546.9 27.9 %pad_maximum_fusion = bf16[4608,1152]{1,0:T(8,128)(2,1)} fusion(bf16[1152,1152]{1,0:T(8,128)(2,1)S(1)} %copy-done.71, bf16[1152,1152]{1,0:T(8,128)(2,1)S(1)} %copy-done.72, bf16[1152,1152]{1,0:T(8,128)(2,1)S(1)} %copy-done.73, bf16[1152,1152]{1,0:T(8,128)(2,1)S(1)} %copy-done.74), kind=kLoop, calls=%fused_computation.24 | loop fusion | flops 42467328 | bytes 21233664 | tf_op jit(solution)/shard_map/concatenate | solution.py:782
  574.8 150.1 %scatter4.1 = (bf16[4,144,1152]{2,1,0:T(8,128)(2,1)}, bf16[4,144,1152]{2,1,0:T(8,128)(2,1)}) custom-call(bf16[4,2,144,1152]{3,2,1,0:T(8,128)(2,1)} %bitcast.347, bf16[4,2,144,1152]{3,2,1,0:T(8,128)(2,1)} %bitcast.348, bf16[4,2,144,1152]{3,2,1,0:T(8,128)(2,1)} %bitcast.349, bf16[4,2,144,1152]{3,2,1,0:T(8,128)(2,1)} %bitcast.350, ...), custom_call_target="tpu_custom_call" | custom-call | tf_op jit(solution)/shard_map/scatter4/pallas_call | solution.py:503
  736.7 12.3 %collective-permute-done.5 = bf16[256,1152]{0,1:T(8,128)(2,1)S(1)} collective-permute-done((bf16[256,1152]{0,1:T(8,128)(2,1)S(1)}, bf16[256,1152]{0,1:T(8,128)(2,1)S(1)}, u32[]{:S(2)}, u32[]{:S(2)}) %collective-permute-start.5) | collective-permute-done | bytes 589856 | tf_op jit(solution)/shard_map/ppermute | solution.py:20
  763.5 11.3 %exchange6.1 = bf16[8,176,128]{2,1,0:T(8,128)(2,1)} custom-call(bf16[176,128]{1,0:T(8,128)(2,1)} %pad_bitcast_fusion.2.rows_ref), custom_call_target="tpu_custom_call" | custom-call | tf_op jit(solution)/shard_map/exchange6/pallas_call | solution.py:102
  778.8 9.0 exchange7.1
  791.2 10.4 %exchange8.1 = bf16[4,624,128]{2,1,0:T(8,128)(2,1)} custom-call(bf16[624,128]{1,0:T(8,128)(2,1)} %pad_bitcast_fusion.1.rows_ref), custom_call_target="tpu_custom_call" | custom-call | tf_op jit(solution)/shard_map/exchange8/pallas_call | solution.py:102
  810.8 3.3 convolution_convert_fusion.10
  817.3 84.9 %scatter5.1 = bf16[4,144,1152]{2,1,0:T(8,128)(2,1)} custom-call(bf16[4,2,144,1152]{3,2,1,0:T(8,128)(2,1)} %bitcast.331, bf16[4,2,144,1152]{3,2,1,0:T(8,128)(2,1)} %bitcast.333, bf16[4,2,144,1152]{3,2,1,0:T(8,128)(2,1)} %bitcast.334, bf16[4,2,144,1152]{3,2,1,0:T(8,128)(2,1)} %bitcast.332), custom_call_target="tpu_custom_call" | custom-call | tf_op jit(solution)/shard_map/scatter5/pallas_call | solution.py:503
  (566 shorter events, 216.2 us)
Async XLA Ops:
  0.7 18.0 %copy-start = (bf16[144,6912]{1,0:T(8,128)(2,1)S(1)}, bf16[144,6912]{1,0:T(8,128)(2,1)}, u32[]{:S(2)}) copy-start(bf16[144,6912]{1,0:T(8,128)(2,1)} %param.33) | copy-start | bytes 5971972
  20.4 21.6 %copy-start.11 = (bf16[256,1152]{1,0:T(8,128)(2,1)S(1)}, bf16[256,1152]{1,0:T(8,128)(2,1)}, u32[]{:S(2)}) copy-start(bf16[256,1152]{1,0:T(8,128)(2,1)} %param.24) | copy-start | bytes 1769476
  20.4 21.6 %copy-start.13 = (bf16[1,256,1152]{2,1,0:T(8,128)(2,1)S(1)}, bf16[1,256,1152]{2,1,0:T(8,128)(2,1)}, u32[]{:S(2)}) copy-start(bf16[1,256,1152]{2,1,0:T(8,128)(2,1)} %param.23) | copy-start | bytes 1769476
  23.6 19.0 %copy-start.107 = (bf16[144,1152]{1,0:T(8,128)(2,1)S(1)}, bf16[144,1152]{1,0:T(8,128)(2,1)}, u32[]{:S(2)}) copy-start(bf16[144,1152]{1,0:T(8,128)(2,1)} %param.38) | copy-start | bytes 995332
  42.2 71.0 %copy-start.112 = (f32[512]{0:T(512)}, f32[512]{0:T(512)S(1)}, u32[]{:S(2)}) copy-start(f32[512]{0:T(512)S(1)} %broadcast_multiply_fusion.5) | copy-start | bytes 6148
  42.7 70.6 %copy-start.115 = (f32[512]{0:T(512)}, f32[512]{0:T(512)S(1)}, u32[]{:S(2)}) copy-start(f32[512]{0:T(512)S(1)} %add_rsqrt_fusion.1) | copy-start | bytes 6148
  105.8 6.2 copy-start.110
  111.9 7.1 copy-start.64
  111.9 10.0 %copy-start.62 = (bf16[1,4,2,144,1152]{4,3,2,1,0:T(8,128)(2,1)}, bf16[1,4,2,144,1152]{4,3,2,1,0:T(8,128)(2,1)S(1)}, u32[]{:S(2)}) copy-start(bf16[1,4,2,144,1152]{4,3,2,1,0:T(8,128)(2,1)S(1)} %get-tuple-element.91) | copy-start | bytes 7962628
  111.9 12.8 %copy-start.28 = (bf16[1,4,2,144,1152]{4,3,2,1,0:T(8,128)(2,1)}, bf16[1,4,2,144,1152]{4,3,2,1,0:T(8,128)(2,1)S(1)}, u32[]{:S(2)}) copy-start(bf16[1,4,2,144,1152]{4,3,2,1,0:T(8,128)(2,1)S(1)} %get-tuple-element.90) | copy-start | bytes 7962628
  131.8 147.6 %collective-permute-start = (bf16[256,1152]{1,0:T(8,128)(2,1)}, bf16[256,1152]{1,0:T(8,128)(2,1)}, u32[]{:S(2)}, u32[]{:S(2)}) collective-permute-start(bf16[256,1152]{1,0:T(8,128)(2,1)} %get-tuple-element.119), channel_id=1, source_target_pairs={{0,2},{1,3},{2,0},{3,1},{4,6},{5,7},{6,4},{7,5},{8,10},{9,11},{10,... | collective-permute-start | bytes 1769480 | tf_op jit(solution)/shard_map/ppermute | solution.py:20
  132.9 151.4 %collective-permute-start.2 = (bf16[256,1152]{1,0:T(8,128)(2,1)}, bf16[256,1152]{1,0:T(8,128)(2,1)}, u32[]{:S(2)}, u32[]{:S(2)}) collective-permute-start(bf16[256,1152]{1,0:T(8,128)(2,1)} %get-tuple-element.115), channel_id=1, source_target_pairs={{0,1},{1,0},{2,3},{3,2},{4,5},{5,4},{6,7},{7,6},{8,9},{9,8},{10,11... | collective-permute-start | bytes 1769480 | tf_op jit(solution)/shard_map/ppermute | solution.py:20
  136.4 6.7 copy-start.134
  136.4 6.7 copy-start.127
  143.1 116.8 %copy-start.129 = (s32[1,16]{1,0:T(1,128)}, s32[1,16]{1,0:T(1,128)S(1)}, u32[]{:S(2)}) copy-start(s32[1,16]{1,0:T(1,128)S(1)} %constant_dynamic-slice_fusion.1) | copy-start | bytes 196
  251.8 10.8 %copy-start.25 = (bf16[4,4,2,144,1152]{4,3,2,1,0:T(8,128)(2,1)S(1)}, bf16[4,4,2,144,1152]{4,3,2,1,0:T(8,128)(2,1)}, u32[]{:S(2)}) copy-start(bf16[4,4,2,144,1152]{4,3,2,1,0:T(8,128)(2,1)} %get-tuple-element.31) | copy-start | bytes 31850500
  275.7 6.6 copy-start.6
  275.7 6.6 copy-start.80
  280.7 28.3 %collective-permute-start.1 = (bf16[512,1152]{1,0:T(8,128)(2,1)S(1)}, bf16[512,1152]{1,0:T(8,128)(2,1)S(1)}, u32[]{:S(2)}, u32[]{:S(2)}) collective-permute-start(bf16[512,1152]{1,0:T(8,128)(2,1)S(1)} %pad_maximum_fusion.7), channel_id=1, source_target_pairs={{0,1},{1,0},{2,3},{3,2},{4,5},{5,4},{6,7},{7,6},{8,9},{9,8},{10,11... | collective-permute-start | bytes 3538952 | tf_op jit(solution)/shard_map/ppermute | solution.py:20
  282.3 6.3 slice-start.9
  287.5 28.8 %collective-permute-start.3 = (bf16[512,1152]{1,0:T(8,128)(2,1)}, bf16[512,1152]{1,0:T(8,128)(2,1)}, u32[]{:S(2)}, u32[]{:S(2)}) collective-permute-start(bf16[512,1152]{1,0:T(8,128)(2,1)} %pad_maximum_fusion.8), channel_id=1, source_target_pairs={{0,2},{1,3},{2,0},{3,1},{4,6},{5,7},{6,4},{7,5},{8,10},{9,11},{10,... | collective-permute-start | bytes 3538952 | tf_op jit(solution)/shard_map/ppermute | solution.py:20
  328.1 6.4 copy-start.3
  328.1 6.4 copy-start.41
  334.5 11.2 %slice-start.2 = ((s8[7077888]{0:T(1024)(128)(4,1)}), s8[4194304]{0:T(1024)(128)(4,1)S(1)}, s32[]{:S(2)}) async-start(s8[7077888]{0:T(1024)(128)(4,1)} %bitcast.265), calls=%async_computation.2 | async-start | bytes 8388608
  334.5 11.2 %slice-start.10 = ((s8[7077888]{0:T(1024)(128)(4,1)}), s8[4194304]{0:T(1024)(128)(4,1)S(1)}, s32[]{:S(2)}) async-start(s8[7077888]{0:T(1024)(128)(4,1)} %bitcast.273), calls=%async_computation.10 | async-start | bytes 8388608
  334.6 11.2 %slice-start.3 = ((s8[7077888]{0:T(1024)(128)(4,1)}), s8[2883584]{0:T(1024)(128)(4,1)S(1)}, s32[]{:S(2)}) async-start(s8[7077888]{0:T(1024)(128)(4,1)} %bitcast.265), calls=%async_computation.3 | async-start | bytes 5767168
  334.6 11.2 %slice-start.11 = ((s8[7077888]{0:T(1024)(128)(4,1)}), s8[2883584]{0:T(1024)(128)(4,1)S(1)}, s32[]{:S(2)}) async-start(s8[7077888]{0:T(1024)(128)(4,1)} %bitcast.273), calls=%async_computation.11 | async-start | bytes 5767168
  385.1 16.9 %copy-start.4 = (f32[256,4608]{1,0:T(8,128)}, f32[256,4608]{1,0:T(8,128)S(1)}, u32[]{:S(2)}) copy-start(f32[256,4608]{1,0:T(8,128)S(1)} %broadcast_in_dim.109) | copy-start | bytes 14155780
  388.8 13.2 %copy-start.5 = (f32[256,4608]{1,0:T(8,128)}, f32[256,4608]{1,0:T(8,128)S(1)}, u32[]{:S(2)}) copy-start(f32[256,4608]{1,0:T(8,128)S(1)} %reshape.609) | copy-start | bytes 14155780
  402.0 11.5 %copy-start.68 = (bf16[1,4,2,144,1152]{4,3,2,1,0:T(8,128)(2,1)S(1)}, bf16[1,4,2,144,1152]{4,3,2,1,0:T(8,128)(2,1)}, u32[]{:S(2)}) copy-start(bf16[1,4,2,144,1152]{4,3,2,1,0:T(8,128)(2,1)} %get-tuple-element.84) | copy-start | bytes 7962628
  440.6 30.3 %copy-start.61 = (bf16[512,16,72]{0,2,1:T(8,128)(2,1)}, bf16[512,16,72]{0,2,1:T(8,128)(2,1)S(1)}, u32[]{:S(2)}) copy-start(bf16[512,16,72]{0,2,1:T(8,128)(2,1)S(1)} %get-tuple-element.107) | copy-start | bytes 3538948
  452.6 12.0 %copy-start.10 = (bf16[1024,1152]{0,1:T(8,128)(2,1)S(1)}, bf16[1024,1152]{0,1:T(8,128)(2,1)}, u32[]{:S(2)}) copy-start(bf16[1024,1152]{0,1:T(8,128)(2,1)} %copy.161) | copy-start | bytes 7077892
  469.0 11.8 %slice-start.16 = ((s8[16777216]{0:T(1024)(128)(4,1)}), s8[4194304]{0:T(1024)(128)(4,1)S(1)}, s32[]{:S(2)}) async-start(s8[16777216]{0:T(1024)(128)(4,1)} %bitcast.279), calls=%async_computation.16 | async-start | bytes 8388608
  470.9 9.8 %slice-start.17 = ((s8[16777216]{0:T(1024)(128)(4,1)}), s8[4194304]{0:T(1024)(128)(4,1)S(1)}, s32[]{:S(2)}) async-start(s8[16777216]{0:T(1024)(128)(4,1)} %bitcast.279), calls=%async_computation.17 | async-start | bytes 8388608
  474.1 6.7 slice-start.18
  474.1 6.7 slice-start.19
  505.6 6.6 slice-start.20
  505.6 6.6 slice-start.22
  534.4 197.4 %collective-permute-start.4 = (bf16[2,256,1152]{1,2,0:T(8,128)(2,1)}, bf16[2,256,1152]{1,2,0:T(8,128)(2,1)}, u32[]{:S(2)}, u32[]{:S(2)}) collective-permute-start(bf16[2,256,1152]{1,2,0:T(8,128)(2,1)} %copy.164), channel_id=1, source_target_pairs={{0,2},{1,3},{2,0},{3,1},{4,6},{5,7},{6,4},{7,5},{8,10},{9,11},{10,... | collective-permute-start | bytes 3538952 | tf_op jit(solution)/shard_map/ppermute | solution.py:20
  538.6 196.2 %collective-permute-start.6 = (bf16[2,256,1152]{1,2,0:T(8,128)(2,1)}, bf16[2,256,1152]{1,2,0:T(8,128)(2,1)}, u32[]{:S(2)}, u32[]{:S(2)}) collective-permute-start(bf16[2,256,1152]{1,2,0:T(8,128)(2,1)} %pad_maximum_fusion.12), channel_id=1, source_target_pairs={{0,1},{1,0},{2,3},{3,2},{4,5},{5,4},{6,7},{7,6},{8,9},{9,8},{10,11... | collective-permute-start | bytes 3538952 | tf_op jit(solution)/shard_map/ppermute | solution.py:20
  731.8 18.3 %copy-start.136 = (f32[512,1152]{1,0:T(8,128)S(1)}, f32[512,1152]{1,0:T(8,128)}, u32[]{:S(2)}) copy-start(f32[512,1152]{1,0:T(8,128)} %fusion.97) | copy-start | bytes 7077892
  733.5 15.5 %collective-permute-start.5 = (bf16[256,1152]{0,1:T(8,128)(2,1)S(1)}, bf16[256,1152]{0,1:T(8,128)(2,1)S(1)}, u32[]{:S(2)}, u32[]{:S(2)}) collective-permute-start(bf16[256,1152]{0,1:T(8,128)(2,1)S(1)} %fusion.98), channel_id=1, source_target_pairs={{0,1},{1,0},{2,3},{3,2},{4,5},{5,4},{6,7},{7,6},{8,9},{9,8},{10,11... | collective-permute-start | bytes 1769480 | tf_op jit(solution)/shard_map/ppermute | solution.py:20
  734.8 15.3 %copy-start.63 = (bf16[1,4,2,144,1152]{4,3,2,1,0:T(8,128)(2,1)S(1)}, bf16[1,4,2,144,1152]{4,3,2,1,0:T(8,128)(2,1)}, u32[]{:S(2)}) copy-start(bf16[1,4,2,144,1152]{4,3,2,1,0:T(8,128)(2,1)} %copy-done.62) | copy-start | bytes 7962628
  734.8 17.4 %slice-start.14 = ((s8[7077888]{0:T(1024)(128)(4,1)}), s8[4194304]{0:T(1024)(128)(4,1)S(1)}, s32[]{:S(2)}) async-start(s8[7077888]{0:T(1024)(128)(4,1)} %bitcast.277), calls=%async_computation.14 | async-start | bytes 8388608
  736.6 13.5 %copy-start.102 = (bf16[16,72,256]{2,1,0:T(8,128)(2,1)S(1)}, bf16[16,72,256]{2,1,0:T(8,128)(2,1)}, u32[]{:S(2)}) copy-start(bf16[16,72,256]{2,1,0:T(8,128)(2,1)} %fusion.81) | copy-start | bytes 1769476
  736.6 15.4 %collective-permute-start.7 = (bf16[256,1152]{0,1:T(8,128)(2,1)S(1)}, bf16[256,1152]{0,1:T(8,128)(2,1)S(1)}, u32[]{:S(2)}, u32[]{:S(2)}) collective-permute-start(bf16[256,1152]{0,1:T(8,128)(2,1)S(1)} %fusion.99), channel_id=1, source_target_pairs={{0,2},{1,3},{2,0},{3,1},{4,6},{5,7},{6,4},{7,5},{8,10},{9,11},{10,... | collective-permute-start | bytes 1769480 | tf_op jit(solution)/shard_map/ppermute | solution.py:20
  776.9 12.4 %copy-start.120 = (bf16[1440]{0:T(1024)(128)(2,1)S(1)}, bf16[1440]{0:T(1024)(128)(2,1)}, u32[]{:S(2)}) copy-start(bf16[1440]{0:T(1024)(128)(2,1)} %reshape.624) | copy-start | bytes 8644
  908.1 5.8 copy-start.119
  (121 other events, 389.6 us)

commit v3 on v2

v3 whole, which is shorter than its diff:
```python
import functools
import math

import jax
import jax.numpy as jnp
from jax import lax
from jax.experimental import pallas as pl
from jax.experimental.pallas import tpu as pltpu
from jax.sharding import PartitionSpec as P

CHAN = 128
SPLIT = 4


epsilon = 1e-06


def low(value):
    return value.astype(jnp.bfloat16)


def packed(parts, unit):
    flat = jnp.concatenate([part.reshape(-1) for part in parts])
    return jnp.pad(flat, (0, -flat.size % (unit * 128))).reshape(-1, 128)


def unpacked(rows, shapes):
    lead = rows.shape[:-2]
    flat = rows.reshape(lead + (-1,))
    parts, start = [], 0
    for shape in shapes:
        size = math.prod(shape)
        parts.append(flat[..., start : start + size].reshape(lead + shape))
        start += size
    return parts


MESH_IDS = pl.DeviceIdType.MESH
VMEM_BYTES = 67_000_000
BY_ROLE, BY_SHARD, BY_COLUMN = range(3)


def flipped(value, step, size):
    total, bit = 0, 1
    while bit < size:
        digit = (value // bit) % 2
        total = total + bit * ((digit + 1) % 2 if step & bit else digit)
        bit *= 2
    return total


def greet(peers):
    barrier = pltpu.get_barrier_semaphore()
    for peer in peers:
        pl.semaphore_signal(barrier, inc=1, device_id=peer, device_id_type=MESH_IDS)
    pl.semaphore_wait(barrier, len(peers))


def remote(source, target, send_sem, recv_sem, peer):
    return pltpu.make_async_remote_copy(
        src_ref=source,
        dst_ref=target,
        send_sem=send_sem,
        recv_sem=recv_sem,
        device_id=peer,
        device_id_type=MESH_IDS,
    )


def exchange_kernel(axis, size, spread_out, rows_ref, out_ref, send_sem, recv_sem):
    me = lax.axis_index(axis)
    greet([{axis: (me + step) % size} for step in range(1, size)])

    def piece(target):
        return rows_ref.at[target] if spread_out else rows_ref

    sent = []
    for step in range(1, size):
        peer = (me + step) % size
        copy = remote(
            piece(peer), out_ref.at[me], send_sem.at[step], recv_sem.at[size - step], {axis: peer}
        )
        copy.start()
        sent.append(copy)
    out_ref[me] = rows_ref[me] if spread_out else rows_ref[...]
    for step in range(1, size):
        peer = (me + step) % size
        remote(
            piece(peer), out_ref.at[peer], send_sem.at[step], recv_sem.at[step], {axis: peer}
        ).wait_recv()
    for copy in sent:
        copy.wait_send()


def exchange(rows, axis, spread_out, number):
    size = lax.axis_size(axis)
    block = rows.shape[1:] if spread_out else rows.shape
    return pl.pallas_call(
        functools.partial(exchange_kernel, axis, size, spread_out),
        out_shape=jax.ShapeDtypeStruct((size,) + block, rows.dtype),
        in_specs=[pl.BlockSpec(memory_space=pltpu.VMEM)],
        out_specs=pl.BlockSpec(memory_space=pltpu.VMEM),
        scratch_shapes=[pltpu.SemaphoreType.DMA((size,)), pltpu.SemaphoreType.DMA((size,))],
        compiler_params=pltpu.CompilerParams(
            collective_id=number, has_side_effects=True, vmem_limit_bytes=VMEM_BYTES
        ),
        name=f"exchange{number}",
    )(rows)


class Place:
    def __init__(self, half):
        self.half = half
        self.role = lax.axis_index("dp")
        shard = lax.axis_index("fsdp")
        self.line, self.side = shard // 2, shard % 2
        self.other_side = (self.side + 1) % 2
        self.roles = [flipped(self.role, step, 4) for step in range(4)]
        self.lines = [flipped(self.line, step, half) for step in range(half)]
        self.sides = [self.side, self.other_side]
        self.across = {"dp": self.roles[2]}
        self.beside = {"fsdp": self.line * 2 + self.other_side}
        self.core = {"dp": self.roles[1]}
        self.along = [{"fsdp": line * 2 + self.side} for line in self.lines]

    def greet(self, also=()):
        greet([self.across, self.beside, self.core] + self.along[1:] + list(also))


def cut(rows):
    first = (rows // 2 + 15) // 16 * 16
    return [(0, first), (first, rows - first)]


def block_view(ref, layout, role, line, side, rows):
    if layout == BY_SHARD:
        return ref.at[line, side, role, rows]
    if layout == BY_ROLE:
        return ref.at[role, line, side, rows]
    width = ref.shape[-1] // 4
    return ref.at[line, side, rows, pl.ds(pl.multiple_of(role * width, 128), width)]


def whole_shape(layout, half, rows, columns):
    lead = {BY_ROLE: (4, half, 2), BY_SHARD: (half, 2, 4), BY_COLUMN: (half, 2)}[layout]
    return lead + (rows, 4 * columns if layout == BY_COLUMN else columns)


class GatherUnit:
    def __init__(self, at, piece, out, layout, start, count, side_first, send_sem, recv_sem):
        self.at, self.piece, self.out, self.layout = at, piece, out, layout
        self.rows = pl.ds(start, count)
        self.side_first, self.send_sem, self.recv_sem = side_first, send_sem, recv_sem
        self.sent = []

    def view(self, role, line, side):
        return block_view(self.out, self.layout, role, line, side, self.rows)

    def send(self, number, make):
        self.sent.append((number, make))
        self.copy_of(number, make).start()

    def copy_of(self, number, make):
        source, target, peer = make()
        return remote(source, target, self.send_sem.at[number], self.recv_sem.at[number], peer)

    def got(self, number, target):
        remote(
            target, target, self.send_sem.at[number], self.recv_sem.at[number], self.at.core
        ).wait_recv()

    def numbers(self):
        half = self.at.half
        return half, 2 * half, 3 * half, 3 * half + 1

    def begin(self):
        at = self.at

        def own_to(peer):
            return lambda: (
                self.piece.at[self.rows], self.view(at.role, at.line, at.side), peer
            )

        beside, across, _, _ = self.numbers()
        for step in range(1, at.half):
            self.send(step, own_to(at.along[step]))
        self.send(beside, own_to(at.beside))
        self.send(across, own_to(at.across))

    def pass_on(self, number, peer, *where):
        self.send(number, lambda: (self.view(*where), self.view(*where), peer))

    def line_step(self, step):
        at = self.at
        where = (at.role, at.lines[step], at.side)
        self.got(step, self.view(*where))
        beside, across, _, _ = self.numbers()
        self.pass_on(beside + step, at.beside, *where)
        self.pass_on(across + step, at.across, *where)

    def second(self):
        at, every = self.at, slice(None)
        beside, across, second, core = self.numbers()
        for step in range(at.half):
            if self.side_first:
                self.got(beside + step, self.view(at.role, at.lines[step], at.other_side))
            else:
                self.got(across + step, self.view(at.roles[2], at.lines[step], at.side))
        if self.side_first:
            where = (at.role, every, at.other_side)
            self.pass_on(second, at.across, *where)
        else:
            where = (at.roles[2], every, at.side)
            self.pass_on(second, at.beside, *where)
        self.pass_on(core, at.core, at.role, every, at.side)
        self.pass_on(core + 1, at.core, *where)

    def third(self):
        at, every = self.at, slice(None)
        beside, across, second, core = self.numbers()
        for step in range(at.half):
            if self.side_first:
                self.got(across + step, self.view(at.roles[2], at.lines[step], at.side))
            else:
                self.got(beside + step, self.view(at.role, at.lines[step], at.other_side))
        if self.side_first:
            self.pass_on(core + 2, at.core, at.roles[2], every, at.side)
        else:
            self.pass_on(core + 2, at.core, at.role, every, at.other_side)
        last = (at.roles[2], every, at.other_side)
        self.got(second, self.view(*last))
        self.pass_on(core + 3, at.core, *last)

    def finish(self):
        at, every = self.at, slice(None)
        core = self.numbers()[3]
        near, far = at.roles[1], at.roles[3]
        views = [
            self.view(near, every, at.side),
            self.view(near, every, at.other_side),
            self.view(far, every, at.side),
            self.view(far, every, at.other_side),
        ]
        if not self.side_first:
            views[1], views[2] = views[2], views[1]
        for step, view in enumerate(views):
            self.got(core + step, view)
        for number, make in self.sent:
            self.copy_of(number, make).wait_send()


def gather_start(at, layouts, pieces, outs, send_sem, recv_sem, local_sem):
    pairs, local = [], []
    for matrix, layout in enumerate(layouts):
        rows = pieces[matrix].shape[0]
        pairs.append(
            [
                GatherUnit(
                    at,
                    pieces[matrix],
                    outs[matrix],
                    layout,
                    start,
                    size,
                    part == 0,
                    send_sem.at[2 * matrix + part],
                    recv_sem.at[2 * matrix + part],
                )
                for part, (start, size) in enumerate(cut(rows))
            ]
        )

        def make(matrix=matrix, layout=layout, rows=rows):
            target = block_view(outs[matrix], layout, at.role, at.line, at.side, pl.ds(0, rows))
            return pltpu.make_async_copy(pieces[matrix], target, local_sem.at[matrix])

        make().start()
        local.append(make)
    for unit in pairs[0]:
        unit.begin()
    return pairs, local


def gather_actions(pairs, local):
    half, count = pairs[0][0].at.half, len(pairs)
    actions = []

    def each(pair, name, *given):
        def act():
            for unit in pair:
                getattr(unit, name)(*given)

        actions.append(act)

    def settle():
        for make in local:
            make().wait()

    actions.append(settle)
    for matrix in range(count + 1):
        if matrix < count:
            for step in range(1, half):
                each(pairs[matrix], "line_step", step)
            if matrix + 1 < count:
                each(pairs[matrix + 1], "begin")
            each(pairs[matrix], "second")
        if matrix:
            each(pairs[matrix - 1], "third")
    for pair in pairs:
        each(pair, "finish")
    return actions


def gather_scratch(count, half):
    return [
        pltpu.SemaphoreType.DMA((2 * count, 3 * half + 5)),
        pltpu.SemaphoreType.DMA((2 * count, 3 * half + 5)),
        pltpu.SemaphoreType.DMA((count,)),
    ]


def gather_kernel(half, layouts, *refs):
    count = len(layouts)
    at = Place(half)
    at.greet()
    pairs, local = gather_start(
        at, layouts, refs[:count], refs[count : 2 * count], *refs[2 * count :]
    )
    for action in gather_actions(pairs, local):
        action()


def gather(pieces, layouts, number):
    half = lax.axis_size("fsdp") // 2
    count = len(pieces)
    return pl.pallas_call(
        functools.partial(gather_kernel, half, layouts),
        out_shape=[
            jax.ShapeDtypeStruct(whole_shape(layout, half, *piece.shape), piece.dtype)
            for piece, layout in zip(pieces, layouts)
        ],
        in_specs=[pl.BlockSpec(memory_space=pltpu.VMEM)] * count,
        out_specs=[pl.BlockSpec(memory_space=pl.ANY)] * count,
        scratch_shapes=gather_scratch(count, half),
        compiler_params=pltpu.CompilerParams(
            collective_id=number, has_side_effects=True, vmem_limit_bytes=VMEM_BYTES
        ),
        name=f"gather{number}",
    )(*pieces)


def accumulate(target, source):
    rows = target.shape[0]
    chunk = 16 if rows % 16 == 0 else rows

    def step(index, carry):
        place_of = pl.ds(pl.multiple_of(index * chunk, chunk), chunk)
        target[place_of] = target[place_of] + source[place_of]
        return carry

    lax.fori_loop(0, rows // chunk, step, 0)


class ScatterUnit:
    def __init__(self, at, terms, out, layout, start, count, across_first, sems, buffers):
        self.at, self.terms, self.out, self.layout = at, terms, out, layout
        self.rows = pl.ds(start, count)
        self.across_first = across_first
        self.send_sem, self.recv_sem, self.stage_sem = sems
        self.core_buf, self.first_buf, self.last_buf, self.line_buf, self.stage = buffers
        self.sent = []
        half = at.half
        self.base_first, self.base_last = 4, 6
        self.base_line, self.base_share = 6 + half, 6 + 2 * half
        self.first_peer = at.across if across_first else at.beside
        self.last_peer = at.beside if across_first else at.across

    def own_terms(self, first, last, core):
        role_step, side_step = (first, last) if self.across_first else (last, first)
        role = self.at.roles[2 * role_step + core]
        return block_view(
            self.terms, self.layout, role, slice(None), self.at.sides[side_step], self.rows
        )

    def out_view(self, role):
        if self.layout == BY_COLUMN:
            width = self.out.shape[1] // 4
            return self.out.at[self.rows, pl.ds(pl.multiple_of(role * width, 128), width)]
        return self.out.at[role, self.rows]

    def send(self, number, make):
        self.sent.append((number, make))
        self.copy_of(number, make).start()

    def copy_of(self, number, make):
        source, target, peer = make()
        return remote(source, target, self.send_sem.at[number], self.recv_sem.at[number], peer)

    def got(self, number, target):
        remote(
            target, target, self.send_sem.at[number], self.recv_sem.at[number], self.at.core
        ).wait_recv()

    def add_lines(self, target, source):
        def step(line, carry):
            accumulate(target.at[line], source.at[line])
            return carry

        lax.fori_loop(0, self.at.half, step, 0)

    def begin(self):
        for first in (1, 0):
            for last in (1, 0):
                self.send(
                    2 * first + last,
                    lambda first=first, last=last: (
                        self.own_terms(first, last, 1), self.core_buf.at[first, last], self.at.core
                    ),
                )

    def paired(self, first, last):
        buffer = self.core_buf.at[first, last]
        load = pltpu.make_async_copy(self.own_terms(first, last, 0), self.stage, self.stage_sem)
        load.start()
        self.got(2 * first + last, buffer)
        load.wait()
        self.add_lines(buffer, self.stage)
        if first:
            self.send(
                self.base_first + last,
                lambda: (
                    self.core_buf.at[first, last], self.first_buf.at[last], self.first_peer
                ),
            )

    def joined(self, last):
        buffer = self.first_buf.at[last]
        self.got(self.base_first + last, buffer)
        self.add_lines(buffer, self.core_buf.at[0, last])
        if last:
            for step in list(range(self.at.half - 1, 0, -1)) + [0]:
                self.send(
                    self.base_last + step,
                    lambda line=self.at.lines[step]: (
                        self.first_buf.at[last, line], self.last_buf.at[line], self.last_peer
                    ),
                )

    def lined(self, step):
        line = self.at.lines[step]
        block = self.last_buf.at[line]
        self.got(self.base_last + step, block)
        accumulate(block, self.first_buf.at[0, line])
        if step:
            self.send(
                self.base_line + step,
                lambda: (self.last_buf.at[line], self.line_buf.at[step], self.at.along[step]),
            )

    def end(self):
        at = self.at
        own = self.last_buf.at[at.line]
        for step in range(1, at.half):
            self.got(self.base_line + step, self.line_buf.at[step])
            accumulate(own, self.line_buf.at[step])
        target = self.out_view(at.role)
        target[...] = own[...]
        for step in (1, 2, 3):
            self.send(
                self.base_share + step,
                lambda step=step: (
                    self.last_buf.at[at.line], self.out_view(at.role), {"dp": at.roles[step]}
                ),
            )

    def finish(self):
        for step in (1, 2, 3):
            self.got(self.base_share + step, self.out_view(self.at.roles[step]))
        for number, make in self.sent:
            self.copy_of(number, make).wait_send()


def scatter_actions(pairs):
    half = pairs[0][0].at.half
    steps = list(range(half - 1, 0, -1)) + [0]
    stages = [
        [("paired", 1, 1), ("paired", 1, 0)],
        [("paired", 0, 1), ("paired", 0, 0)],
        [("joined", 1), ("joined", 0)],
        [("lined", step) for step in steps],
        [("end",)],
    ]
    actions = []

    def each(pair, name, *given):
        def act():
            for unit in pair:
                getattr(unit, name)(*given)

        actions.append(act)

    for turn in range(len(stages) + len(pairs) - 1):
        for index, pair in reversed(list(enumerate(pairs))):
            if 0 <= turn - index < len(stages):
                for call in stages[turn - index]:
                    each(pair, *call)
    for pair in pairs:
        each(pair, "finish")
    return actions


def scatter_start(at, layouts, terms, outs, scratch):
    sems, buffers = scratch[:3], scratch[3:]
    pairs = []
    for matrix, layout in enumerate(layouts):
        pair = []
        for part, (start, size) in enumerate(cut(terms[matrix].shape[-2])):
            unit = 2 * matrix + part
            pair.append(
                ScatterUnit(
                    at,
                    terms[matrix],
                    outs[matrix],
                    layout,
                    start,
                    size,
                    part == 0,
                    [sem.at[unit] for sem in sems],
                    buffers[5 * unit : 5 * unit + 5],
                )
            )
        pairs.append(pair)
    for pair in pairs:
        for unit in pair:
            unit.begin()
    return pairs


def scatter_scratch(count, half, rows, columns):
    scratch = [pltpu.SemaphoreType.DMA((2 * count, 2 * half + 10))] * 2
    scratch += [pltpu.SemaphoreType.DMA((2 * count,))]
    for _ in range(count):
        for _, size in cut(rows):
            for lead in ((2, 2, half), (2, half), (half,), (half,), (half,)):
                scratch.append(pltpu.VMEM(lead + (size, columns), jnp.bfloat16))
    return scratch


def scatter_outs(layouts, rows, columns):
    return [
        jax.ShapeDtypeStruct(
            (rows, 4 * columns) if layout == BY_COLUMN else (4, rows, columns), jnp.bfloat16
        )
        for layout in layouts
    ]


def roles_kernel(half, *refs):
    ins, out, terms, local_sem, scratch = refs[:4], refs[4], refs[5], refs[6], refs[7:]
    at = Place(half)
    local = []
    for role in range(4):
        copy = pltpu.make_async_copy(ins[role], terms.at[role], local_sem.at[role])
        copy.start()
        local.append(copy)
    at.greet([{"dp": at.roles[3]}])
    for copy in local:
        copy.wait()
    pairs = scatter_start(at, (BY_ROLE,), [terms], [out], scratch)
    for action in scatter_actions(pairs):
        action()


def scatter_roles(gradients, number):
    half = lax.axis_size("fsdp") // 2
    rows, columns = gradients[0].shape[-2:]
    return pl.pallas_call(
        functools.partial(roles_kernel, half),
        out_shape=scatter_outs((BY_ROLE,), rows, columns)[0],
        in_specs=[pl.BlockSpec(memory_space=pl.ANY)] * 4,
        out_specs=pl.BlockSpec(memory_space=pltpu.VMEM),
        scratch_shapes=[
            pltpu.VMEM((4, half, 2, rows, columns), jnp.bfloat16),
            pltpu.SemaphoreType.DMA((4,)),
        ]
        + scatter_scratch(1, half, rows, columns),
        compiler_params=pltpu.CompilerParams(
            collective_id=number, has_side_effects=True, vmem_limit_bytes=VMEM_BYTES
        ),
        name=f"scatter{number}",
    )(*gradients)


def head_window(head, width, columns):
    tile = jnp.minimum(head * width // 128, columns // 128 - 2)
    lane = lax.broadcasted_iota(jnp.int32, (1, 256), 1) + tile * 128
    inside = jnp.logical_and(lane >= head * width, lane < (head + 1) * width)
    return pl.ds(pl.multiple_of(tile * 128, 128), 256), jnp.where(inside, 1.0, 0.0)


def dot_nt(left, right):
    return lax.dot_general(
        left, right, (((1,), (1,)), ((), ())), preferred_element_type=jnp.float32
    )


def dot_tn(left, right):
    return lax.dot_general(
        left, right, (((0,), (0,)), ((), ())), preferred_element_type=jnp.float32
    )


def attend_head(head, width, q_ref, k_ref, v_ref, o_ref, log_ref):
    scaling = width ** (-0.5)
    window, inside = head_window(head, width, q_ref.shape[1])
    queries = q_ref[:, window] * inside.astype(jnp.bfloat16)
    scores = dot_nt(queries, k_ref[:, window]) * scaling
    row_max = jnp.max(scores, axis=-1, keepdims=True)
    exponent = jnp.exp(scores - row_max)
    row_total = jnp.sum(exponent, axis=-1, keepdims=True)
    weights = (exponent * (1.0 / row_total)).astype(jnp.bfloat16)
    result = jnp.dot(weights, v_ref[:, window], preferred_element_type=jnp.float32)
    o_ref[:, window] += result * inside
    lane = lax.broadcasted_iota(jnp.int32, (1, log_ref.shape[1]), 1)
    log_ref[...] = jnp.where(lane == head, row_max + jnp.log(row_total), log_ref[...])


def attend_back_head(head, width, q_ref, k_ref, v_ref, g_ref, log_ref, dq_ref, dk_ref, dv_ref):
    scaling = width ** (-0.5)
    window, inside = head_window(head, width, q_ref.shape[1])
    inside_low = inside.astype(jnp.bfloat16)
    queries, grads = q_ref[:, window] * inside_low, g_ref[:, window] * inside_low
    key_rows = k_ref[:, window]
    lane = lax.broadcasted_iota(jnp.int32, (1, log_ref.shape[1]), 1)
    log_total = jnp.sum(jnp.where(lane == head, log_ref[...], 0.0), axis=-1, keepdims=True)
    weights = jnp.exp(dot_nt(queries, key_rows) * scaling - log_total)
    dv_ref[:, window] += dot_tn(weights.astype(jnp.bfloat16), grads)
    d_weights = dot_nt(grads, v_ref[:, window])
    inner = jnp.sum(weights * d_weights, axis=-1, keepdims=True)
    d_scores = (weights * (d_weights - inner)).astype(jnp.bfloat16)
    dq_ref[:, window] += jnp.dot(d_scores, key_rows, preferred_element_type=jnp.float32) * (
        inside * scaling
    )
    dk_ref[:, window] += dot_tn(d_scores, queries) * scaling


def run_heads(head_count, attend_one, actions):
    spread_over = {}
    for index, action in enumerate(actions):
        spread_over.setdefault(index * head_count // len(actions), []).append(action)

    def step(head, carry):
        attend_one(head)
        for when, group in spread_over.items():

            @pl.when(head == when)
            def _(group=group):
                for action in group:
                    action()

        return carry

    lax.fori_loop(0, head_count, step, 0)


def forward_kernel(half, layouts, heads, *refs):
    count = len(layouts)
    q_ref, k_ref, v_ref = refs[:3]
    pieces = refs[3 : 3 + count]
    o_ref, log_ref, keys, values = refs[3 + count : 7 + count]
    outs = refs[7 + count : 7 + 2 * count]
    send_sem, recv_sem = refs[7 + 2 * count : 9 + 2 * count]
    at = Place(half)
    width = q_ref.shape[1] // heads
    rows = keys.shape[0] // 4
    short = q_ref.shape[0] - rows
    own = pl.ds(short, rows)
    beside, along = at.beside, at.along[1]

    def quarter(buffer, index):
        return buffer.at[pl.ds(index * rows, rows)]

    at.greet()
    sent = []

    def send(number, source, target, peer):
        copy = remote(source, target, send_sem.at[number], recv_sem.at[number], peer)
        copy.start()
        sent.append(copy)

    def got(number, target):
        remote(target, target, send_sem.at[number], recv_sem.at[number], along).wait_recv()

    send(0, k_ref.at[own], quarter(keys, 1), beside)
    send(1, v_ref.at[own], quarter(values, 2), along)
    send(2, v_ref.at[own], quarter(values, 1), beside)
    send(3, k_ref.at[own], quarter(keys, 2), along)
    pairs, local = gather_start(at, layouts, pieces, outs, *refs[9 + 2 * count :])
    quarter(keys, 0)[...] = k_ref[own]
    quarter(values, 0)[...] = v_ref[own]
    o_ref[...] = jnp.zeros_like(o_ref)
    log_ref[...] = jnp.zeros_like(log_ref)

    def pass_on():
        got(0, quarter(keys, 1))
        send(4, quarter(keys, 1), quarter(keys, 3), along)
        got(1, quarter(values, 2))
        send(5, quarter(values, 2), quarter(values, 3), beside)

    actions = gather_actions(pairs, local)
    early = 1 + (half - 1)
    first = pl.ds(0, short)
    run_heads(
        heads,
        lambda head: attend_head(
            head,
            width,
            q_ref.at[first],
            k_ref.at[first],
            v_ref.at[first],
            o_ref.at[first],
            log_ref.at[first],
        ),
        [lambda: None, lambda: None, lambda: None] + actions[:early],
    )
    pass_on()
    for action in actions[early : early + 2]:
        action()
    got(2, quarter(values, 1))
    got(3, quarter(keys, 2))
    got(4, quarter(keys, 3))
    got(5, quarter(values, 3))
    run_heads(
        heads,
        lambda head: attend_head(
            head, width, q_ref.at[own], keys, values, o_ref.at[own], log_ref.at[own]
        ),
        actions[early + 2 : -count],
    )
    for action in actions[-count:]:
        action()
    for copy in sent:
        copy.wait_send()


def attention_forward(q_rows, k_rows, v_rows, pieces, layouts, heads, rows, number):
    half = lax.axis_size("fsdp") // 2
    count = len(pieces)
    vmem, hbm = pl.BlockSpec(memory_space=pltpu.VMEM), pl.BlockSpec(memory_space=pl.ANY)
    total, columns = q_rows.shape
    outs = [
        jax.ShapeDtypeStruct((total, columns), jnp.float32),
        jax.ShapeDtypeStruct((total, 128), jnp.float32),
        jax.ShapeDtypeStruct((4 * rows, columns), jnp.bfloat16),
        jax.ShapeDtypeStruct((4 * rows, columns), jnp.bfloat16),
    ] + [
        jax.ShapeDtypeStruct(whole_shape(layout, half, *piece.shape), piece.dtype)
        for piece, layout in zip(pieces, layouts)
    ]
    return pl.pallas_call(
        functools.partial(forward_kernel, half, layouts, heads),
        out_shape=outs,
        in_specs=[vmem] * (3 + count),
        out_specs=[vmem] * 4 + [hbm] * count,
        scratch_shapes=[pltpu.SemaphoreType.DMA((6,)), pltpu.SemaphoreType.DMA((6,))]
        + gather_scratch(count, half),
        compiler_params=pltpu.CompilerParams(
            collective_id=number, has_side_effects=True, vmem_limit_bytes=VMEM_BYTES
        ),
        name=f"attention{number}",
    )(q_rows, k_rows, v_rows, *pieces)


def backward_kernel(half, layouts, heads, *refs):
    count = len(layouts)
    q_ref, k_ref, v_ref, g_ref, log_ref, keys, values = refs[:7]
    terms = refs[7 : 7 + count]
    dq_out, dk_out, dv_out = refs[7 + count : 10 + count]
    outs = refs[10 + count : 10 + 2 * count]
    rest = refs[10 + 2 * count :]
    dq, dk, dv, wide, wide_got, slim, slim_got, send_sem, recv_sem = rest[:9]
    at = Place(half)
    width = q_ref.shape[1] // heads
    rows = keys.shape[0] // 4
    short = q_ref.shape[0] - rows
    own, first = pl.ds(short, rows), pl.ds(0, short)
    beside, along = at.beside, at.along[1]
    at.greet([{"dp": at.roles[3]}])
    pairs = scatter_start(at, layouts, terms, outs, rest[9:])
    actions = scatter_actions(pairs)
    dq[...] = jnp.zeros_like(dq)
    dk[...] = jnp.zeros_like(dk)
    dv[...] = jnp.zeros_like(dv)
    sent = []

    def send(number, source, target, peer):
        copy = remote(source, target, send_sem.at[number], recv_sem.at[number], peer)
        copy.start()
        sent.append(copy)

    def got(number, target):
        remote(target, target, send_sem.at[number], recv_sem.at[number], along).wait_recv()

    def quarter(index):
        return pl.ds(index * rows, rows)

    split = 2 * len(actions) // 5
    run_heads(
        heads,
        lambda head: attend_back_head(
            head,
            width,
            q_ref.at[own],
            keys,
            values,
            g_ref.at[own],
            log_ref.at[own],
            dq.at[own],
            dk,
            dv,
        ),
        actions[:split],
    )
    for part, (source, index) in enumerate([(dk, 2), (dk, 3), (dv, 1), (dv, 3)]):
        wide[part] = source[quarter(index)].astype(jnp.bfloat16)
    send(0, wide.at[pl.ds(0, 2)], wide_got.at[pl.ds(0, 2)], along)
    send(1, wide.at[pl.ds(2, 2)], wide_got.at[pl.ds(2, 2)], beside)
    short_dk, short_dv = dk.at[pl.ds(2 * rows, short)], dv.at[pl.ds(rows, short)]
    short_dk[...] = jnp.zeros_like(short_dk)
    short_dv[...] = jnp.zeros_like(short_dv)
    run_heads(
        heads,
        lambda head: attend_back_head(
            head,
            width,
            q_ref.at[first],
            k_ref.at[first],
            v_ref.at[first],
            g_ref.at[first],
            log_ref.at[first],
            dq.at[first],
            short_dk,
            short_dv,
        ),
        actions[split : split + 2],
    )
    dq_out[...] = dq[...].astype(jnp.bfloat16)
    dk_out[first] = short_dk[...].astype(jnp.bfloat16)
    dv_out[first] = short_dv[...].astype(jnp.bfloat16)
    got(0, wide_got.at[pl.ds(0, 2)])
    slim[0] = (dk[quarter(1)] + wide_got[1].astype(jnp.float32)).astype(jnp.bfloat16)
    send(2, slim.at[0], slim_got.at[0], beside)
    got(1, wide_got.at[pl.ds(2, 2)])
    slim[1] = (dv[quarter(2)] + wide_got[3].astype(jnp.float32)).astype(jnp.bfloat16)
    send(3, slim.at[1], slim_got.at[1], along)
    for action in actions[split + 2 : -count]:
        action()
    got(2, slim_got.at[0])
    total = dk[quarter(0)] + wide_got[0].astype(jnp.float32) + slim_got[0].astype(jnp.float32)
    dk_out[own] = total.astype(jnp.bfloat16)
    got(3, slim_got.at[1])
    total = dv[quarter(0)] + wide_got[2].astype(jnp.float32) + slim_got[1].astype(jnp.float32)
    dv_out[own] = total.astype(jnp.bfloat16)
    for action in actions[-count:]:
        action()
    for copy in sent:
        copy.wait_send()


def attention_backward(rows_in, keys, values, gradients, layouts, heads, rows, columns, number):
    half = lax.axis_size("fsdp") // 2
    count = len(gradients)
    vmem, hbm = pl.BlockSpec(memory_space=pltpu.VMEM), pl.BlockSpec(memory_space=pl.ANY)
    total, model_width = rows_in[0].shape
    quarter_rows = keys.shape[0] // 4
    low_rows = jax.ShapeDtypeStruct((total, model_width), jnp.bfloat16)
    return pl.pallas_call(
        functools.partial(backward_kernel, half, layouts, heads),
        out_shape=[low_rows] * 3 + scatter_outs(layouts, rows, columns),
        in_specs=[vmem] * 7 + [hbm] * count,
        out_specs=[vmem] * (3 + count),
        scratch_shapes=[
            pltpu.VMEM((total, model_width), jnp.float32),
            pltpu.VMEM((4 * quarter_rows, model_width), jnp.float32),
            pltpu.VMEM((4 * quarter_rows, model_width), jnp.float32),
            pltpu.VMEM((4, quarter_rows, model_width), jnp.bfloat16),
            pltpu.VMEM((4, quarter_rows, model_width), jnp.bfloat16),
            pltpu.VMEM((2, quarter_rows, model_width), jnp.bfloat16),
            pltpu.VMEM((2, quarter_rows, model_width), jnp.bfloat16),
            pltpu.SemaphoreType.DMA((4,)),
            pltpu.SemaphoreType.DMA((4,)),
        ]
        + scatter_scratch(count, half, rows, columns),
        compiler_params=pltpu.CompilerParams(
            collective_id=number, has_side_effects=True, vmem_limit_bytes=VMEM_BYTES
        ),
        name=f"attention{number}",
    )(*rows_in, keys, values, *gradients)


def product(left, right):
    return jnp.dot(left, right, preferred_element_type=jnp.float32)


def product_tn(left, right):
    return lax.dot_general(
        left, right, (((0,), (0,)), ((), ())), preferred_element_type=jnp.float32
    )


def product_nt(left, right):
    return lax.dot_general(
        left, right, (((1,), (1,)), ((), ())), preferred_element_type=jnp.float32
    )


def spread(per_slot, short_count, len_short, quarter_rows):
    width = per_slot.shape[1]
    short_part = jnp.broadcast_to(
        per_slot[:short_count, None, :], (short_count, len_short, width)
    ).reshape(short_count * len_short, width)
    long_part = jnp.broadcast_to(per_slot[short_count:], (quarter_rows, width))
    return jnp.concatenate([short_part, long_part], 0)


def slot_sum(values, short_count, len_short):
    short_rows = short_count * len_short
    short_part = jnp.sum(
        values[:short_rows].reshape((short_count, len_short) + values.shape[1:]), axis=1
    )
    long_part = jnp.sum(values[short_rows:], axis=0, keepdims=True)
    return jnp.concatenate([short_part, long_part], 0)


def norm_parts(values):
    average = jnp.mean(values, axis=-1, keepdims=True)
    centred = values - average
    variance = jnp.mean(centred * centred, axis=-1, keepdims=True)
    inverse = lax.rsqrt(variance + epsilon)
    return (centred * inverse, inverse)


def norm_back(gradient, normed, inverse):
    return inverse * (
        gradient
        - jnp.mean(gradient, axis=-1, keepdims=True)
        - normed * jnp.mean(gradient * normed, axis=-1, keepdims=True)
    )


def silu_grad(values):
    sigmoid_value = jax.nn.sigmoid(values)
    return sigmoid_value * (1.0 + values * (1.0 - sigmoid_value))


def gelu_tanh(values):
    return jax.nn.gelu(values, approximate=True)


def per_device(
    x_short,
    x_long,
    short_cond,
    long_cond,
    short_heads,
    long_heads,
    short_groups,
    long_groups,
    short_keep,
    long_keep,
    w_ada,
    b_ada,
    w_head_router,
    w_group_router,
    w_qkv,
    w_proj,
    b_proj,
    w_fc1,
    b_fc1,
    w_fc2,
    b_fc2,
    g_short,
    g_long,
):
    short_count, len_short, model_width = x_short.shape
    quarter_rows = x_long.shape[0]
    head_count = w_head_router.shape[1]
    head_width = model_width // head_count
    group_count = w_group_router.shape[1]
    slot_count = short_count + 1
    short_rows = short_count * len_short
    row_count = short_rows + quarter_rows
    fsdp_index = lax.axis_index("fsdp")
    fsdp_count = lax.axis_size("fsdp")
    role = lax.axis_index("dp")
    group_row = fsdp_index // SPLIT
    half = fsdp_count // 2
    shard_rows = w_qkv.shape[0]
    unit_rows = w_fc2.shape[0] // 4
    short_act = low(jax.nn.silu(short_cond))
    long_act = low(jax.nn.silu(long_cond))
    message = exchange(packed([short_act, b_proj, b_fc1, b_fc2], 16), "fsdp", False, 0)
    act_rows, proj_bias, fc1_bias, fc2_bias = unpacked(
        message, [(model_width,), b_proj.shape, b_fc1.shape, b_fc2.shape]
    )
    proj_bias, fc1_bias, fc2_bias = (
        bias.reshape(-1).astype(jnp.float32) for bias in (proj_bias, fc1_bias, fc2_bias)
    )
    item_act = jnp.concatenate([act_rows, long_act], 0)
    item_columns = lax.dynamic_slice_in_dim(item_act, fsdp_index * shard_rows, shard_rows, 1)
    bias_row = lax.dynamic_update_slice_in_dim(
        jnp.zeros((fsdp_count * b_ada.shape[0],), jnp.float32),
        b_ada.astype(jnp.float32),
        fsdp_index * b_ada.shape[0],
        0,
    )
    partial = jnp.concatenate(
        [
            product(item_columns, w_ada) + bias_row,
            product(item_columns, w_head_router),
            product(item_columns, w_group_router),
        ],
        1,
    )
    width = partial.shape[1]
    for_device = jnp.stack(
        [partial[:fsdp_count], jnp.repeat(partial[fsdp_count:], SPLIT, axis=0)], 1
    ).reshape(fsdp_count, -1)
    for_device = jnp.pad(for_device, ((0, 0), (0, -for_device.shape[1] % 1024)))
    shares = exchange(for_device.reshape(fsdp_count, -1, 128), "fsdp", True, 1)
    conditioned = unpacked(jnp.sum(shares, axis=0), [(2, width)])[0]
    mixed_shard = jnp.concatenate([w_qkv, w_proj], 1)
    attention_piece = lax.dynamic_slice_in_dim(mixed_shard, role * model_width, model_width, 1)
    (attention_full,) = gather([attention_piece], (BY_ROLE,), 2)
    attention_full = attention_full.reshape(4, -1, model_width)
    mod_width = 6 * model_width
    modulation = conditioned[:, :mod_width]
    head_sigmoid = jax.nn.sigmoid(conditioned[:, mod_width : mod_width + head_count])
    group_sigmoid = jax.nn.sigmoid(conditioned[:, mod_width + head_count :])
    head_mask = jnp.concatenate(
        [short_heads, lax.dynamic_slice_in_dim(long_heads, group_row, 1, 0)], 0
    ).astype(jnp.float32)
    group_mask = jnp.concatenate(
        [short_groups, lax.dynamic_slice_in_dim(long_groups, group_row, 1, 0)], 0
    ).astype(jnp.float32)
    head_gate = head_mask * 2.0 * head_sigmoid
    group_gate = group_mask * 2.0 * group_sigmoid
    shift1, scale1, gate1, shift2, scale2, gate2 = jnp.split(
        spread(modulation, short_count, len_short, quarter_rows), 6, axis=1
    )
    x_rows = jnp.concatenate([x_short.reshape(short_rows, model_width), x_long], 0).astype(
        jnp.float32
    )
    keep_rows = jnp.concatenate([short_keep.reshape(short_rows), long_keep], 0).astype(jnp.float32)[
        :, None
    ]
    normed1, inverse1 = norm_parts(x_rows)
    hidden1 = low(normed1 * (1.0 + scale1) + shift1)
    q_rows, k_rows, v_rows = (low(product(hidden1, attention_full[part])) for part in range(3))

    fc1_piece = lax.dynamic_slice_in_dim(w_fc1, role * model_width, model_width, 1)
    fc2_piece = lax.dynamic_slice_in_dim(w_fc2, role * unit_rows, unit_rows, 0)
    head_rows, log_rows, keys, values, fc1_full, fc2_full = attention_forward(
        q_rows,
        k_rows,
        v_rows,
        [fc1_piece, fc2_piece],
        (BY_COLUMN, BY_SHARD),
        head_count,
        quarter_rows,
        3,
    )
    head_rows = head_rows.reshape(row_count, head_count, head_width)
    head_gate_rows = spread(head_gate, short_count, len_short, quarter_rows)[:, :, None]
    attention = low((head_rows * head_gate_rows).reshape(row_count, model_width))
    projected = product(attention, attention_full[3]) + proj_bias
    mixed = x_rows + gate1 * projected
    fc1_full = fc1_full.reshape(model_width, -1)
    fc2_full = fc2_full.reshape(-1, model_width)
    normed2, inverse2 = norm_parts(mixed)
    hidden2 = low(normed2 * (1.0 + scale2) + shift2)
    channel_gate = spread(
        jnp.repeat(group_gate, CHAN, axis=1), short_count, len_short, quarter_rows
    )
    up_rows = product(hidden2, fc1_full) + fc1_bias
    gelu_value, gelu_pull = jax.vjp(gelu_tanh, up_rows)
    activated = low(gelu_value * channel_gate)
    down_rows = product(activated, fc2_full) + fc2_bias
    out_rows = mixed + gate2 * keep_rows * down_rows
    y_short = low(out_rows[:short_rows].reshape(x_short.shape))
    y_long = low(out_rows[short_rows:])
    gradient = jnp.concatenate([g_short.reshape(short_rows, model_width), g_long], 0).astype(
        jnp.float32
    )
    d_down = low(gradient * gate2 * keep_rows)
    slot_gate2 = slot_sum(gradient * keep_rows * down_rows, short_count, len_short)
    grad_fc2 = low(product_tn(activated, d_down)).reshape(half, 2, 4, unit_rows, model_width)
    d_activated = product_nt(d_down, fc2_full)
    d_channel = slot_sum(d_activated * gelu_value, short_count, len_short)
    d_group = jnp.sum(d_channel.reshape(slot_count, group_count, CHAN), axis=-1)
    d_up = low(gelu_pull(d_activated * channel_gate)[0])
    grad_fc1 = low(product_tn(hidden2, d_up)).reshape(half, 2, shard_rows, -1)
    d_hidden2 = product_nt(d_up, fc1_full)

    def blocks(grad):
        return low(grad).reshape(half, 2, shard_rows, model_width)

    slot_shift2 = slot_sum(d_hidden2, short_count, len_short)
    slot_scale2 = slot_sum(d_hidden2 * normed2, short_count, len_short)
    d_mixed = gradient + norm_back(d_hidden2 * (1.0 + scale2), normed2, inverse2)
    d_projected = low(d_mixed * gate1)
    slot_gate1 = slot_sum(d_mixed * projected, short_count, len_short)
    d_attention = product_nt(d_projected, attention_full[3]).reshape(
        row_count, head_count, head_width
    )
    d_head = slot_sum(jnp.sum(d_attention * head_rows, axis=-1), short_count, len_short)
    d_heads = low(d_attention * head_gate_rows)
    bias_grad = jnp.concatenate(
        [jnp.sum(part, axis=0, dtype=jnp.float32) for part in (d_projected, d_up, d_down)]
    )
    dq_rows, dk_rows, dv_rows, fc1_sum, fc2_sum = attention_backward(
        [q_rows, k_rows, v_rows, d_heads.reshape(row_count, model_width), log_rows],
        keys,
        values,
        [grad_fc1, grad_fc2],
        (BY_COLUMN, BY_SHARD),
        head_count,
        shard_rows,
        model_width,
        4,
    )
    g_w_fc1 = fc1_sum.astype(jnp.float32)
    g_w_fc2 = fc2_sum.reshape(-1, model_width).astype(jnp.float32)
    attention_sum = scatter_roles(
        [
            blocks(product_tn(hidden1, dq_rows)),
            blocks(product_tn(hidden1, dk_rows)),
            blocks(product_tn(hidden1, dv_rows)),
            blocks(product_tn(attention, d_projected)),
        ],
        5,
    )
    g_w_qkv = attention_sum[:3].transpose(1, 0, 2).reshape(shard_rows, -1).astype(jnp.float32)
    g_w_proj = attention_sum[3].astype(jnp.float32)
    d_hidden1 = (
        product_nt(dq_rows, attention_full[0])
        + product_nt(dk_rows, attention_full[1])
        + product_nt(dv_rows, attention_full[2])
    )
    slot_shift1 = slot_sum(d_hidden1, short_count, len_short)
    slot_scale1 = slot_sum(d_hidden1 * normed1, short_count, len_short)
    d_rows = d_mixed + norm_back(d_hidden1 * (1.0 + scale1), normed1, inverse1)
    dx_short = low(d_rows[:short_rows].reshape(x_short.shape))
    dx_long = low(d_rows[short_rows:])
    d_head_logit = d_head * head_mask * 2.0 * head_sigmoid * (1.0 - head_sigmoid)
    d_group_logit = d_group * group_mask * 2.0 * group_sigmoid * (1.0 - group_sigmoid)
    d_conditioned = jnp.concatenate(
        [
            slot_shift1,
            slot_scale1,
            slot_gate1,
            slot_shift2,
            slot_scale2,
            slot_gate2,
            d_head_logit,
            d_group_logit,
        ],
        1,
    )
    member_rows = exchange(packed([low(d_conditioned), low(bias_grad)], 16), "fsdp", False, 6)
    member_rows, bias_rows = unpacked(member_rows, [(2, width), bias_grad.shape])
    long_sum = jnp.sum(
        member_rows[:, 1].astype(jnp.float32).reshape(-1, SPLIT, width), axis=1
    )
    d_items = jnp.concatenate([member_rows[:, 0], low(long_sum)], 0)
    group_bias = jnp.sum(bias_rows.astype(jnp.float32), axis=0)
    d_silu = (
        product_nt(d_items[:, :mod_width], w_ada)
        + product_nt(d_items[:, mod_width : mod_width + head_count], w_head_router)
        + product_nt(d_items[:, mod_width + head_count :], w_group_router)
    )
    d_silu = unpacked(exchange(packed([d_silu], 8), "fsdp", False, 7), [d_silu.shape])[0]
    d_silu = d_silu.transpose(1, 0, 2).reshape(-1, model_width)
    d_short_cond = lax.dynamic_slice_in_dim(d_silu, fsdp_index, 1, 0) * silu_grad(short_cond)
    d_long_cond = d_silu[fsdp_count:] * silu_grad(long_cond)
    replicas = exchange(packed([d_items, low(group_bias), item_columns], 16), "dp", False, 8)
    factors, bias_rows, act_factors = unpacked(
        replicas, [d_items.shape, group_bias.shape, item_columns.shape]
    )
    factors, act_factors = factors.reshape(-1, width), act_factors.reshape(-1, shard_rows)
    g_w_ada = product_tn(act_factors, factors[:, :mod_width])
    g_w_head_router = product_tn(act_factors, factors[:, mod_width : mod_width + head_count])
    g_w_group_router = product_tn(act_factors, factors[:, mod_width + head_count :])
    g_b_ada = lax.dynamic_slice_in_dim(
        jnp.sum(factors[:, :mod_width].astype(jnp.float32), axis=0),
        fsdp_index * b_ada.shape[0],
        b_ada.shape[0],
        0,
    )
    bias_sum = jnp.sum(bias_rows.astype(jnp.float32), axis=0)

    def own_bias(start, count):
        return lax.dynamic_slice_in_dim(bias_sum, start + fsdp_index * count, count, 0)

    g_b_proj = own_bias(0, shard_rows)
    g_b_fc1 = own_bias(model_width, 4 * shard_rows)
    g_b_fc2 = own_bias(5 * model_width, shard_rows)
    return (
        y_short,
        y_long,
        dx_short,
        dx_long,
        d_short_cond,
        d_long_cond,
        g_w_ada,
        g_b_ada,
        g_w_head_router,
        g_w_group_router,
        g_w_qkv,
        g_w_proj,
        g_b_proj,
        g_w_fc1,
        g_b_fc1,
        g_w_fc2,
        g_b_fc2,
    )


def solution(mesh):
    return jax.shard_map(
        per_device,
        mesh=mesh,
        in_specs=(
            P(("dp", "fsdp"), None, None),
            P(("dp", "fsdp"), None),
            P(("dp", "fsdp"), None),
            P("dp", None),
            P(("dp", "fsdp"), None),
            P("dp", None),
            P(("dp", "fsdp"), None),
            P("dp", None),
            P(("dp", "fsdp"), None),
            P(("dp", "fsdp")),
            P("fsdp", None),
            P("fsdp"),
            P("fsdp", None),
            P("fsdp", None),
            P("fsdp", None),
            P("fsdp", None),
            P("fsdp"),
            P("fsdp", None),
            P("fsdp"),
            P("fsdp", None),
            P("fsdp"),
            P(("dp", "fsdp"), None, None),
            P(("dp", "fsdp"), None),
        ),
        out_specs=(
            P(("dp", "fsdp"), None, None),
            P(("dp", "fsdp"), None),
            P(("dp", "fsdp"), None, None),
            P(("dp", "fsdp"), None),
            P(("dp", "fsdp"), None),
            P("dp", None),
            P("fsdp", None),
            P("fsdp"),
            P("fsdp", None),
            P("fsdp", None),
            P("fsdp", None),
            P("fsdp", None),
            P("fsdp"),
            P("fsdp", None),
            P("fsdp"),
            P("fsdp", None),
            P("fsdp"),
        ),
        check_vma=False,
    )
```

time: 920 us -> 791 us (0.86)
  Pallas kernels: 457 us -> 527 us
  local copies, waits for them, and re-layouts: 126 us -> 56.4 us
  other arithmetic: 113 us -> 56.3 us
  matrix products: 177 us -> 143 us
  waiting for transfers between devices: 30.5 us -> 0 us
    pallas_call x4, Pallas kernels: 404 us -> 474 us  [the longest x1 181 us: attention_backward(): pl.pallas_call(functools.partial(backward_kernel, half, layouts, heads),...]
    dot_general x12 -> x0, matrix products: 50.7 us -> none  [the longest x2 14.9 us: attend_back(): jnp.einsum('nqhe,nkhe->nhqk', d_out, value_rows, preferred_element_type=j...]
    concatenate x5 -> x0, other arithmetic: 38.4 us -> none  [the longest x1 27.9 us: per_device(): jnp.concatenate([low(product_tn(part, d_down)) for part in activated], 0)]
    slice x20 -> x0, local copies, waits for them, and re-layouts: 36.4 us -> none  [the longest x6 12.2 us: per_device(): rows[:short_rows]]
    ppermute x8 -> x0, waiting for transfers between devices: 30.5 us -> none  [swap(): return lax.ppermute(value, axis, pairs)]
    unnamed x329 -> x167, local copies, waits for them, and re-layouts: 38.8 us -> 15.2 us
    convert_element_type x2 -> x1, other arithmetic: 15.4 us -> 1.77 us  [per_device(): g_w_fc1 = fc1_sum.astype(jnp.float32)]
    dot_general x15 -> x9, matrix products: 39.4 us -> 51 us  [product(): return jnp.dot(left, right, preferred_element_type=jnp.float32)]
  transfers between devices with their start and end apart: 8 -> 0, of which waited for: 2 -> 0; matrix products, arithmetic and copies ran while one was open for 11% -> 0% of each run, Pallas kernels for 28% -> 0%
where the time goes in v3:
time: 791 us; the launch traced here: 785 us
  Pallas kernels  527 us (67%)
  matrix products  143 us (18%)
  local copies, waits for them, and re-layouts  56.4 us (7%)
  other arithmetic  56.3 us (7%)
    pallas_call x1, Pallas kernels, attention_backward(): pl.pallas_call(functools.partial(backward_kernel, half, layouts, heads),...  181 us
    pallas_call x1, Pallas kernels, attention_forward(): pl.pallas_call(functools.partial(forward_kernel, half, layouts, heads), o...  148 us
    pallas_call x1, Pallas kernels, scatter_roles(): pl.pallas_call(functools.partial(roles_kernel, half), out_shape=scatter_o...  83.7 us
    pallas_call x1, Pallas kernels, gather(): pl.pallas_call(functools.partial(gather_kernel, half, layouts), out_shape...  61.1 us
    pallas_call x5, Pallas kernels, exchange(): pl.pallas_call(functools.partial(exchange_kernel, axis, size, spread_out)...  53.4 us
    dot_general x9, matrix products, product(): return jnp.dot(left, right, preferred_element_type=jnp.float32)  51 us
    dot_general x9, matrix products, product_tn(): lax.dot_general(left, right, (((0,), (0,)), ((), ())), preferred_element_...  47.8 us
    dot_general x9, matrix products, product_nt(): lax.dot_general(left, right, (((1,), (1,)), ((), ())), preferred_element_...  44 us

profile of v3, /device:TPU:0, one launch (start us, length us, event | category | flops | bytes accessed | tf_op | source)
XLA Modules:
  0.0 785.0 jit_solution(13099528860822749945)
XLA Ops:
  6.5 1.7 fusion.24
  10.1 9.8 %exchange0.1 = bf16[8,16,128]{2,1,0:T(8,128)(2,1)} custom-call(bf16[16,128]{1,0:T(8,128)(2,1)} %pad_bitcast_fusion.4.rows_ref), custom_call_target="tpu_custom_call" | custom-call | tf_op jit(solution)/shard_map/exchange0/pallas_call | solution.py:98
  24.8 1.7 constant_dynamic-slice_fusion.2.refs_4_
  26.5 1.9 convolution_add_fusion
  30.2 12.6 %exchange1.1 = f32[8,112,128]{2,1,0:T(8,128)} custom-call(f32[8,112,128]{2,1,0:T(8,128)} %bitcast.179), custom_call_target="tpu_custom_call" | custom-call | tf_op jit(solution)/shard_map/exchange1/pallas_call | solution.py:98
  45.0 2.0 fusion.44
  47.3 2.5 copy.100
  50.8 2.3 copy-done.1
  53.1 2.9 copy-done.2
  56.0 1.6 fusion.18
  57.6 61.1 %gather2.1 = bf16[4,4,2,144,1152]{4,3,2,1,0:T(8,128)(2,1)} custom-call(bf16[144,1152]{1,0:T(8,128)(2,1)} %get-tuple-element.104.refs_0_), custom_call_target="tpu_custom_call" | custom-call | tf_op jit(solution)/shard_map/gather2/pallas_call | solution.py:336
  118.7 6.0 fusion.85
  124.7 3.4 convolution_convert_fusion.7.refs_1_
  128.2 2.9 convolution_convert_fusion.6.refs_2_
  131.0 2.9 convolution_convert_fusion.8.refs_0_
  133.9 147.9 %attention3.1 = (f32[512,1152]{1,0:T(8,128)}, f32[512,128]{1,0:T(8,128)}, bf16[1024,1152]{1,0:T(8,128)(2,1)}, bf16[1024,1152]{1,0:T(8,128)(2,1)}, bf16[4,2,144,4...) custom-call(bf16[512,1152]{1,0:T(8,128)(2,1)} %convolution_convert_fusion.8.refs_0_, ...), custom_call_target="tpu_custom_call" | custom-call | tf_op jit(solution)/shard_map/attention3/pallas_call | solution.py:760
  281.8 2.6 multiply_convert_fusion.2
  284.5 3.7 copy.102
  288.3 5.9 fusion.84
  296.5 14.5 %fusion.73 = f32[512,4608]{1,0:T(8,128)} fusion(bf16[1152,4608]{1,0:T(8,128)(2,1)} %bitcast.196, f32[256,6912]{1,0:T(8,128)S(1)} %bitcast.131, f32[256,6912]{1,0:T(8,128)S(1)} %bitcast.137, f32[512,1152]{1,0:T(8,128)S(1)} %get-tuple-element.67, f32[512]{0:T(512)S(1)} %add_rsqrt_fusion, f32[512]{0:T(512)S(1)} %broadcast_multiply_fusion.4), kind=kOutput, calls=%fused_computation.212 | convolution fusion | flops 5440536576 | bytes 36573184 | tf_op jit(solution)/shard_map/dot_general | solution.py:902
  311.1 16.4 %fusion.10 = (f32[512,4608]{1,0:T(8,128)}, f32[512,4608]{1,0:T(8,128)}) fusion(f32[512,4608]{1,0:T(8,128)} %fusion.73, f32[4608]{0:T(1024)S(1)} %reshape.335, bf16[4608,1152]{1,0:T(8,128)(2,1)} %bitcast.148, f32[256,6912]{1,0:T(8,128)} %copy-done.1, f32[256,6912]{1,0:T(8,128)} %copy-done.2, f32[512]{0:T(512)S(1)} %copy-done.39, ...), kind=kOutput, calls=%fused_computation.43 | convolution fusion | flops 5464129536 | bytes 54284288 | tf_op jit(solution)/shard_map/dot_general | solution.py:912
  327.5 4.3 slice_reduce_fusion.1
  333.4 2.7 broadcast_in_dim.101
  336.1 2.9 reshape.311
  339.1 18.6 %convolution_add_fusion.1 = f32[512,1152]{1,0:T(8,128)} fusion(bf16[4608,1152]{1,0:T(8,128)(2,1)} %bitcast.149, f32[1152]{0:T(1024)S(1)} %copy-done.55, f32[256,4608]{1,0:T(8,128)} %broadcast_in_dim.101, f32[256,4608]{1,0:T(8,128)} %reshape.311, f32[512,4608]{1,0:T(8,128)} %fusion.73, f32[4608]{0:T(1024)S(1)} %reshape.335), kind=kOutput, calls=%fused_computation.39 | convolution fusion | flops 5464719360 | bytes 31873536 | tf_op jit(solution)/shard_map/dot_general | solution.py:902
  357.6 12.9 %fusion.81 = (bf16[4608]{0:T(1024)(128)(2,1)}, bf16[512,4608]{1,0:T(8,128)(2,1)}) fusion(f32[512,4608]{1,0:T(8,128)S(1)} %bitcast.141, f32[4608]{0:T(1024)S(1)} %reshape.335, f32[512,4608]{1,0:T(8,128)} %get-tuple-element.101, f32[256,4608]{1,0:T(8,128)} %broadcast_in_dim.101, f32[256,4608]{1,0:T(8,128)} %reshape.311), kind=kLoop, calls=%fused_computation.215 | loop fusion | flops 56618496 | bytes 33057792 | tf_op jit(solution)/shard_map/reduce_sum | solution.py:1119
  370.5 16.6 %convolution_convert_fusion = bf16[4608,1152]{1,0:T(8,128)(2,1)} fusion(f32[256,6912]{1,0:T(8,128)} %copy-done.1, f32[256,6912]{1,0:T(8,128)} %copy-done.2, f32[512]{0:T(512)S(1)} %copy-done.39, bf16[256,1152]{1,0:T(8,128)(2,1)S(1)} %copy-done.27, bf16[256,1152]{1,0:T(8,128)(2,1)} %bitcast.174, f32[256,4608]{1,0:T(8,128)} %broadcast_in_dim.101, ...), kind=kOutput, calls=%fused_computation.10 | convolution fusion | flops 5474156544 | bytes 44847104 | tf_op jit(solution)/shard_map/dot_general | solution.py:906
  387.1 13.8 %fusion.70 = (f32[512]{0:T(512)S(1)}, f32[512]{0:T(512)S(1)}, bf16[512,1152]{1,0:T(8,128)(2,1)S(1)}, f32[512,1152]{1,0:T(8,128)S(1)}, f32[512,1152]{1,0:T(8,128)S(1)}, /*index=5*/f32[512,1152]{1,0:T(8,128)S(1)}) fusion(f32[256,6912]{1,0:T(8,128)} %copy-done.1, f32[256,6912]{1,0:T(8,128)} %copy-done.2, f32[512]{0:T(512)S(1)} %add_rsqrt_fusion, ...), kind=kOutput, calls=%fused_computation.210 | convolution fusion | flops 5449382912 | bytes 43657216 | tf_op jit(solution)/shard_map/dot_general | solution.py:912
  403.3 6.2 fusion.83
  409.5 1.9 multiply_reduce_fusion
  414.3 4.8 convolution_convert_fusion.2
  419.1 12.4 %convolution_convert_fusion.1 = bf16[1152,4608]{1,0:T(8,128)(2,1)} fusion(bf16[512,4608]{1,0:T(8,128)(2,1)} %get-tuple-element.62, f32[256,6912]{1,0:T(8,128)} %copy-done.1, f32[256,6912]{1,0:T(8,128)} %copy-done.2, f32[512,1152]{1,0:T(8,128)S(1)} %copy-done.5, f32[512]{0:T(512)S(1)} %add_rsqrt_fusion, f32[512]{0:T(512)S(1)} %broadcast_multiply_fusion.4), kind=kOutput, calls=%fused_computation.11 | convolution fusion | flops 5445844992 | bytes 31854592 | tf_op jit(solution)/shard_map/dot_general | solution.py:906
  431.5 181.1 %attention4.1 = (bf16[512,1152]{1,0:T(8,128)(2,1)}, bf16[512,1152]{1,0:T(8,128)(2,1)}, bf16[512,1152]{1,0:T(8,128)(2,1)}, bf16[144,4608]{1,0:T(8,128)(2,1)}, bf16[4,144,1152]{2,1,0:T(8,128)(2,1)}) custom-call(bf16[512,1152]{1,0:T(8,128)(2,1)} %convolution_convert_fusion.8.refs_0_, bf16[512,1152]{1,0:T(8,128)(2,1)} %convolution_convert_fusion.7.refs_1_, ...), custom_call_target="tpu_custom_call" | custom-call | tf_op jit(solution)/shard_map/attention4/pallas_call | solution.py:877
  612.6 4.1 fusion.91
  616.9 4.2 convolution_add_fusion.3
  622.0 2.6 fusion.71
  624.7 2.7 fusion.13
  629.2 9.6 %exchange6.1 = bf16[8,176,128]{2,1,0:T(8,128)(2,1)} custom-call(bf16[176,128]{1,0:T(8,128)(2,1)} %pad_bitcast_fusion.2.rows_ref), custom_call_target="tpu_custom_call" | custom-call | tf_op jit(solution)/shard_map/exchange6/pallas_call | solution.py:98
  643.1 10.9 %exchange7.1 = f32[8,16,128]{2,1,0:T(8,128)} custom-call(f32[16,128]{1,0:T(8,128)} %pad_bitcast_fusion.3.rows_ref), custom_call_target="tpu_custom_call" | custom-call | tf_op jit(solution)/shard_map/exchange7/pallas_call | solution.py:98
  661.1 10.6 %exchange8.1 = bf16[4,624,128]{2,1,0:T(8,128)(2,1)} custom-call(bf16[624,128]{1,0:T(8,128)(2,1)} %pad_bitcast_fusion.1.rows_ref), custom_call_target="tpu_custom_call" | custom-call | tf_op jit(solution)/shard_map/exchange8/pallas_call | solution.py:98
  679.6 1.8 convert_element_type.224
  681.4 1.8 bitcast_convert_fusion
  684.0 3.2 convolution_convert_fusion.5
  687.3 3.3 convolution_convert_fusion.4
  690.5 3.3 convolution_convert_fusion.3
  693.8 83.7 %scatter5.1 = bf16[4,144,1152]{2,1,0:T(8,128)(2,1)} custom-call(bf16[4,2,144,1152]{3,2,1,0:T(8,128)(2,1)} %bitcast.162, bf16[4,2,144,1152]{3,2,1,0:T(8,128)(2,1)} %bitcast.163, bf16[4,2,144,1152]{3,2,1,0:T(8,128)(2,1)} %bitcast.164, bf16[4,2,144,1152]{3,2,1,0:T(8,128)(2,1)} %bitcast.161), custom_call_target="tpu_custom_call" | custom-call | tf_op jit(solution)/shard_map/scatter5/pallas_call | solution.py:577
  777.5 1.9 bitcast_convert_fusion.1
  782.1 2.6 fusion.42
  (297 shorter events, 52.2 us)
Async XLA Ops:
  0.7 22.4 %copy-start = (bf16[144,36]{0,1:T(8,128)(2,1)S(1)}, bf16[144,36]{0,1:T(8,128)(2,1)}, u32[]{:S(2)}) copy-start(bf16[144,36]{0,1:T(8,128)(2,1)} %param.36) | copy-start | bytes 31108
  0.7 8.1 %copy-start.47 = (f32[2,1152]{1,0:T(2,128)S(1)}, f32[2,1152]{1,0:T(2,128)}, u32[]{:S(2)}) copy-start(f32[2,1152]{1,0:T(2,128)} %param.26) | copy-start | bytes 27652
  0.7 8.1 %copy-start.52 = (f32[1,1152]{1,0:T(1,128)S(1)}, f32[1,1152]{1,0:T(1,128)}, u32[]{:S(2)}) copy-start(f32[1,1152]{1,0:T(1,128)} %param.25) | copy-start | bytes 13828
  0.7 8.7 %copy-start.62 = (bf16[144]{0:T(256)(128)(2,1)S(1)}, bf16[144]{0:T(256)(128)(2,1)}, u32[]{:S(2)}) copy-start(bf16[144]{0:T(256)(128)(2,1)} %param.43) | copy-start | bytes 868
  0.7 8.7 %copy-start.60 = (bf16[576]{0:T(1024)(128)(2,1)S(1)}, bf16[576]{0:T(1024)(128)(2,1)}, u32[]{:S(2)}) copy-start(bf16[576]{0:T(1024)(128)(2,1)} %param.41) | copy-start | bytes 3460
  0.7 8.7 %copy-start.61 = (bf16[144]{0:T(256)(128)(2,1)S(1)}, bf16[144]{0:T(256)(128)(2,1)}, u32[]{:S(2)}) copy-start(bf16[144]{0:T(256)(128)(2,1)} %param.39) | copy-start | bytes 868
  50.3 5.7 copy-start.6
  50.3 5.7 copy-start.9
  50.3 5.7 copy-start.44
  50.3 5.7 copy-start.48
  118.7 6.0 copy-start.32
  124.7 6.3 copy-start.25
  284.4 3.8 copy-start.18
  284.4 3.8 copy-start.7
  284.4 3.8 copy-start.10
  284.5 3.8 copy-start.42
  288.2 7.6 slice-start
  288.2 7.6 slice-start.6
  288.2 7.5 slice-start.1
  288.3 8.3 %slice-start.7 = ((s8[7077888]{0:T(1024)(128)(4,1)}), s8[2883584]{0:T(1024)(128)(4,1)S(1)}, s32[]{:S(2)}) async-start(s8[7077888]{0:T(1024)(128)(4,1)} %bitcast.136), calls=%async_computation.7 | async-start | bytes 5767168
  296.5 14.5 %copy-start.27 = (bf16[256,1152]{1,0:T(8,128)(2,1)S(1)}, bf16[256,1152]{1,0:T(8,128)(2,1)}, u32[]{:S(2)}) copy-start(bf16[256,1152]{1,0:T(8,128)(2,1)} %param.45) | copy-start | bytes 1769476
  296.5 14.5 %copy-start.28 = (bf16[1,256,1152]{2,1,0:T(8,128)(2,1)S(1)}, bf16[1,256,1152]{2,1,0:T(8,128)(2,1)}, u32[]{:S(2)}) copy-start(bf16[1,256,1152]{2,1,0:T(8,128)(2,1)} %param.44) | copy-start | bytes 1769476
  296.5 14.5 %copy-start.39 = (f32[512]{0:T(512)S(1)}, f32[512]{0:T(512)}, u32[]{:S(2)}) copy-start(f32[512]{0:T(512)} %add_convert_fusion.1) | copy-start | bytes 6148
  327.5 4.6 copy-start.63
  327.5 4.5 copy-start.64
  336.1 21.5 %slice-start.10 = ((s8[9437184]{0:T(1024)(128)(4,1)}), s8[4194304]{0:T(1024)(128)(4,1)S(1)}, s32[]{:S(2)}) async-start(s8[9437184]{0:T(1024)(128)(4,1)} %bitcast.140), calls=%async_computation.10 | async-start | bytes 8388608
  339.1 18.6 %slice-start.11 = ((s8[9437184]{0:T(1024)(128)(4,1)}), s8[4194304]{0:T(1024)(128)(4,1)S(1)}, s32[]{:S(2)}) async-start(s8[9437184]{0:T(1024)(128)(4,1)} %bitcast.140), calls=%async_computation.11 | async-start | bytes 8388608
  339.1 18.6 %slice-start.12 = ((s8[9437184]{0:T(1024)(128)(4,1)}), s8[1048576]{0:T(1024)(128)(4,1)S(1)}, s32[]{:S(2)}) async-start(s8[9437184]{0:T(1024)(128)(4,1)} %bitcast.140), calls=%async_computation.12 | async-start | bytes 2097152
  370.5 32.7 %slice-start.2 = ((s8[7077888]{0:T(1024)(128)(4,1)}), s8[2883584]{0:T(1024)(128)(4,1)S(1)}, s32[]{:S(2)}) async-start(s8[7077888]{0:T(1024)(128)(4,1)} %bitcast.132), calls=%async_computation.2 | async-start | bytes 5767168
  387.1 16.1 %slice-start.3 = ((s8[7077888]{0:T(1024)(128)(4,1)}), s8[4194304]{0:T(1024)(128)(4,1)S(1)}, s32[]{:S(2)}) async-start(s8[7077888]{0:T(1024)(128)(4,1)} %bitcast.132), calls=%async_computation.3 | async-start | bytes 8388608
  403.3 6.2 copy-start.13
  403.3 6.2 copy-start.26
  403.3 6.2 copy-start.41
  414.3 4.8 copy-start.5
  612.6 8.4 %slice-start.4 = ((s8[7077888]{0:T(1024)(128)(4,1)}), s8[4194304]{0:T(1024)(128)(4,1)S(1)}, s32[]{:S(2)}) async-start(s8[7077888]{0:T(1024)(128)(4,1)} %bitcast.134), calls=%async_computation.4 | async-start | bytes 8388608
  612.6 8.4 %slice-start.8 = ((s8[7077888]{0:T(1024)(128)(4,1)}), s8[4194304]{0:T(1024)(128)(4,1)S(1)}, s32[]{:S(2)}) async-start(s8[7077888]{0:T(1024)(128)(4,1)} %bitcast.138), calls=%async_computation.8 | async-start | bytes 8388608
  616.8 4.3 slice-start.5
  616.8 4.3 slice-start.9
  616.8 4.3 copy-start.8
  616.8 4.3 copy-start.11
  616.8 4.9 copy-start.15
  616.8 5.2 copy-start.34
  616.8 5.2 copy-start.45
  616.8 5.2 copy-start.49
  641.2 17.9 %copy-start.53 = (bf16[1440]{0:T(1024)(128)(2,1)S(1)}, bf16[1440]{0:T(1024)(128)(2,1)}, u32[]{:S(2)}) copy-start(bf16[1440]{0:T(1024)(128)(2,1)} %reshape.327) | copy-start | bytes 8644
  671.7 6.9 copy-start.22
  676.0 5.4 copy-start.20
  676.1 3.6 copy-start.31
  (32 other events, 65.7 us)

commit v4 on v3

--- a/solution.py
+++ b/solution.py
@@ -113,6 +113,7 @@
         self.half = half
         self.role = lax.axis_index("dp")
         shard = lax.axis_index("fsdp")
+        self.shard = shard
         self.line, self.side = shard // 2, shard % 2
         self.other_side = (self.side + 1) % 2
         self.roles = [flipped(self.role, step, 4) for step in range(4)]
@@ -123,9 +124,62 @@
         self.core = {"dp": self.roles[1]}
         self.along = [{"fsdp": line * 2 + self.side} for line in self.lines]
 
-    def greet(self, also=()):
-        greet([self.across, self.beside, self.core] + self.along[1:] + list(also))
-
+    def greet(self, every_shard=False):
+        if every_shard:
+            shards = [{"fsdp": (self.shard + step) % (2 * self.half)} for step in range(1, 2 * self.half)]
+        else:
+            shards = [self.beside] + self.along[1:]
+        greet([self.across, self.core] + shards)
+
+
+class Message:
+    def __init__(self, at, rows, out, spread_out, send_sem, recv_sem):
+        self.at, self.rows, self.out, self.spread_out = at, rows, out, spread_out
+        self.send_sem, self.recv_sem, self.sent = send_sem, recv_sem, []
+        self.size = 2 * at.half
+
+    def slot(self, shard):
+        return self.out.at[shard] if self.spread_out else self.out.at[self.at.role, shard]
+
+    def send(self, number, recv_number, source, target, peer):
+        copy = remote(source, target, self.send_sem.at[number], self.recv_sem.at[recv_number], peer)
+        copy.start()
+        self.sent.append(copy)
+
+    def got(self, number, target):
+        remote(
+            target, target, self.send_sem.at[number], self.recv_sem.at[number], self.at.core
+        ).wait_recv()
+
+    def begin(self):
+        me = self.at.shard
+        for step in range(1, self.size):
+            peer = (me + step) % self.size
+            source = self.rows.at[peer] if self.spread_out else self.rows
+            self.send(step, self.size - step, source, self.slot(me), {"fsdp": peer})
+        self.slot(me)[...] = self.rows[me] if self.spread_out else self.rows[...]
+
+    def arrive(self):
+        for step in range(1, self.size):
+            self.got(step, self.slot((self.at.shard + step) % self.size))
+        if not self.spread_out:
+            own = self.out.at[self.at.role]
+            self.send(self.size, self.size, own, own, self.at.across)
+            self.send(self.size + 1, self.size + 1, own, own, self.at.core)
+
+    def finish(self):
+        if not self.spread_out:
+            far = self.out.at[self.at.roles[2]]
+            self.got(self.size, far)
+            self.send(self.size + 2, self.size + 2, far, far, self.at.core)
+            self.got(self.size + 1, self.out.at[self.at.roles[1]])
+            self.got(self.size + 2, self.out.at[self.at.roles[3]])
+        for copy in self.sent:
+            copy.wait_send()
+
+
+def message_scratch(half):
+    return [pltpu.SemaphoreType.DMA((2 * half + 3,)), pltpu.SemaphoreType.DMA((2 * half + 3,))]
 
 def cut(rows):
     first = (rows // 2 + 15) // 16 * 16
@@ -249,7 +303,7 @@
             self.copy_of(number, make).wait_send()
 
 
-def gather_start(at, layouts, pieces, outs, send_sem, recv_sem, local_sem):
+def gather_start(at, layouts, orders, pieces, outs, send_sem, recv_sem, local_sem):
     pairs, local = [], []
     for matrix, layout in enumerate(layouts):
         rows = pieces[matrix].shape[0]
@@ -262,7 +316,7 @@
                     layout,
                     start,
                     size,
-                    part == 0,
+                    orders[matrix][part],
                     send_sem.at[2 * matrix + part],
                     recv_sem.at[2 * matrix + part],
                 )
@@ -319,34 +373,42 @@
     ]
 
 
-def gather_kernel(half, layouts, *refs):
+def gather_kernel(half, layouts, orders, *refs):
     count = len(layouts)
     at = Place(half)
-    at.greet()
+    rows, out = refs[count], refs[2 * count + 1]
+    scratch = refs[2 * count + 2 :]
+    message = Message(at, rows, out, True, *scratch[:2])
+    at.greet(True)
+    message.begin()
     pairs, local = gather_start(
-        at, layouts, refs[:count], refs[count : 2 * count], *refs[2 * count :]
+        at, layouts, orders, refs[:count], refs[count + 1 : 2 * count + 1], *scratch[2:]
     )
     for action in gather_actions(pairs, local):
         action()
-
-
-def gather(pieces, layouts, number):
+    message.arrive()
+    message.finish()
+
+
+def gather(pieces, layouts, orders, rows, number):
     half = lax.axis_size("fsdp") // 2
     count = len(pieces)
+    vmem, hbm = pl.BlockSpec(memory_space=pltpu.VMEM), pl.BlockSpec(memory_space=pl.ANY)
     return pl.pallas_call(
-        functools.partial(gather_kernel, half, layouts),
+        functools.partial(gather_kernel, half, layouts, orders),
         out_shape=[
             jax.ShapeDtypeStruct(whole_shape(layout, half, *piece.shape), piece.dtype)
             for piece, layout in zip(pieces, layouts)
-        ],
-        in_specs=[pl.BlockSpec(memory_space=pltpu.VMEM)] * count,
-        out_specs=[pl.BlockSpec(memory_space=pl.ANY)] * count,
-        scratch_shapes=gather_scratch(count, half),
+        ]
+        + [jax.ShapeDtypeStruct(rows.shape, rows.dtype)],
+        in_specs=[vmem] * (count + 1),
+        out_specs=[hbm] * count + [vmem],
+        scratch_shapes=message_scratch(half) + gather_scratch(count, half),
         compiler_params=pltpu.CompilerParams(
             collective_id=number, has_side_effects=True, vmem_limit_bytes=VMEM_BYTES
         ),
         name=f"gather{number}",
-    )(*pieces)
+    )(*pieces, rows)
 
 
 def accumulate(target, source):
@@ -465,7 +527,7 @@
             accumulate(own, self.line_buf.at[step])
         target = self.out_view(at.role)
         target[...] = own[...]
-        for step in (1, 2, 3):
+        for step in (2, 1):
             self.send(
                 self.base_share + step,
                 lambda step=step: (
@@ -474,7 +536,15 @@
             )
 
     def finish(self):
-        for step in (1, 2, 3):
+        roles = self.at.roles
+        self.got(self.base_share + 2, self.out_view(roles[2]))
+        self.send(
+            self.base_share + 3,
+            lambda: (self.out_view(roles[2]), self.out_view(roles[2]), self.at.core),
+        )
+
+    def close(self):
+        for step in (1, 3):
             self.got(self.base_share + step, self.out_view(self.at.roles[step]))
         for number, make in self.sent:
             self.copy_of(number, make).wait_send()
@@ -504,12 +574,13 @@
             if 0 <= turn - index < len(stages):
                 for call in stages[turn - index]:
                     each(pair, *call)
-    for pair in pairs:
-        each(pair, "finish")
+    for name in ("finish", "close"):
+        for pair in pairs:
+            each(pair, name)
     return actions
 
 
-def scatter_start(at, layouts, terms, outs, scratch):
+def scatter_start(at, layouts, orders, terms, outs, scratch):
     sems, buffers = scratch[:3], scratch[3:]
     pairs = []
     for matrix, layout in enumerate(layouts):
@@ -524,7 +595,7 @@
                     layout,
                     start,
                     size,
-                    part == 0,
+                    orders[matrix][part],
                     [sem.at[unit] for sem in sems],
                     buffers[5 * unit : 5 * unit + 5],
                 )
@@ -555,40 +626,78 @@
     ]
 
 
-def roles_kernel(half, *refs):
-    ins, out, terms, local_sem, scratch = refs[:4], refs[4], refs[5], refs[6], refs[7:]
+def roles_kernel(half, order, *refs):
+    ins, rows, out, rows_out = refs[:6], refs[6], refs[7], refs[8]
+    left, right, terms, local_sem = refs[9:13]
+    scratch = refs[13:]
     at = Place(half)
     local = []
-    for role in range(4):
-        copy = pltpu.make_async_copy(ins[role], terms.at[role], local_sem.at[role])
+    for index in range(6):
+        target = left.at[index] if index < 2 else right.at[index - 2]
+        copy = pltpu.make_async_copy(ins[index], target, local_sem.at[index])
         copy.start()
         local.append(copy)
-    at.greet([{"dp": at.roles[3]}])
+    message = Message(at, rows, rows_out, False, *scratch[:2])
+    at.greet(True)
+    message.begin()
     for copy in local:
         copy.wait()
-    pairs = scatter_start(at, (BY_ROLE,), [terms], [out], scratch)
-    for action in scatter_actions(pairs):
+    shard_rows, columns = terms.shape[3:]
+    chunks = 3
+    width = columns // chunks
+
+    def product_of(role, chunk):
+        window = pl.ds(pl.multiple_of(chunk * width, 128), width)
+        result = dot_tn(left[role // 3], right[role, :, window]).astype(jnp.bfloat16)
+        for shard in range(2 * half):
+            terms[role, shard // 2, shard % 2, :, window] = result[
+                shard * shard_rows : (shard + 1) * shard_rows
+            ]
+
+    def two_roles(first, second):
+        def step(index, carry):
+            role = jnp.where(index < chunks, first, second)
+            product_of(role, index % chunks)
+            return carry
+
+        lax.fori_loop(0, 2 * chunks, step, 0)
+
+    two_roles(at.roles[3], at.roles[1])
+    pairs = scatter_start(at, (BY_ROLE,), (order,), [terms], [out], scratch[2:])
+    two_roles(at.roles[2], at.roles[0])
+    actions = scatter_actions(pairs)
+    for action in actions[:5]:
         action()
-
-
-def scatter_roles(gradients, number):
+    message.arrive()
+    for action in actions[5:]:
+        action()
+    message.finish()
+
+
+def scatter_products(lefts, rights, order, message, number):
     half = lax.axis_size("fsdp") // 2
-    rows, columns = gradients[0].shape[-2:]
+    model_width = lefts[0].shape[1]
+    rows, columns = model_width // (2 * half), rights[0].shape[1]
+    vmem, hbm = pl.BlockSpec(memory_space=pltpu.VMEM), pl.BlockSpec(memory_space=pl.ANY)
     return pl.pallas_call(
-        functools.partial(roles_kernel, half),
-        out_shape=scatter_outs((BY_ROLE,), rows, columns)[0],
-        in_specs=[pl.BlockSpec(memory_space=pl.ANY)] * 4,
-        out_specs=pl.BlockSpec(memory_space=pltpu.VMEM),
+        functools.partial(roles_kernel, half, order),
+        out_shape=scatter_outs((BY_ROLE,), rows, columns)
+        + [jax.ShapeDtypeStruct((4, 2 * half) + message.shape, message.dtype)],
+        in_specs=[hbm] * 6 + [vmem],
+        out_specs=[vmem] * 2,
         scratch_shapes=[
+            pltpu.VMEM((2,) + lefts[0].shape, jnp.bfloat16),
+            pltpu.VMEM((4,) + rights[0].shape, jnp.bfloat16),
             pltpu.VMEM((4, half, 2, rows, columns), jnp.bfloat16),
-            pltpu.SemaphoreType.DMA((4,)),
+            pltpu.SemaphoreType.DMA((6,)),
         ]
+        + message_scratch(half)
         + scatter_scratch(1, half, rows, columns),
         compiler_params=pltpu.CompilerParams(
             collective_id=number, has_side_effects=True, vmem_limit_bytes=VMEM_BYTES
         ),
         name=f"scatter{number}",
-    )(*gradients)
+    )(*lefts, *rights, message)
 
 
 def head_window(head, width, columns):
@@ -663,7 +772,7 @@
     lax.fori_loop(0, head_count, step, 0)
 
 
-def forward_kernel(half, layouts, heads, *refs):
+def forward_kernel(half, layouts, orders, heads, *refs):
     count = len(layouts)
     q_ref, k_ref, v_ref = refs[:3]
     pieces = refs[3 : 3 + count]
@@ -695,7 +804,9 @@
     send(1, v_ref.at[own], quarter(values, 2), along)
     send(2, v_ref.at[own], quarter(values, 1), beside)
     send(3, k_ref.at[own], quarter(keys, 2), along)
-    pairs, local = gather_start(at, layouts, pieces, outs, *refs[9 + 2 * count :])
+    pairs, local = gather_start(
+        at, layouts, orders, pieces, outs, *refs[9 + 2 * count :]
+    )
     quarter(keys, 0)[...] = k_ref[own]
     quarter(values, 0)[...] = v_ref[own]
     o_ref[...] = jnp.zeros_like(o_ref)
@@ -743,7 +854,7 @@
         copy.wait_send()
 
 
-def attention_forward(q_rows, k_rows, v_rows, pieces, layouts, heads, rows, number):
+def attention_forward(q_rows, k_rows, v_rows, pieces, layouts, orders, heads, rows, number):
     half = lax.axis_size("fsdp") // 2
     count = len(pieces)
     vmem, hbm = pl.BlockSpec(memory_space=pltpu.VMEM), pl.BlockSpec(memory_space=pl.ANY)
@@ -758,7 +869,7 @@
         for piece, layout in zip(pieces, layouts)
     ]
     return pl.pallas_call(
-        functools.partial(forward_kernel, half, layouts, heads),
+        functools.partial(forward_kernel, half, layouts, orders, heads),
         out_shape=outs,
         in_specs=[vmem] * (3 + count),
         out_specs=[vmem] * 4 + [hbm] * count,
@@ -771,7 +882,7 @@
     )(q_rows, k_rows, v_rows, *pieces)
 
 
-def backward_kernel(half, layouts, heads, *refs):
+def backward_kernel(half, layouts, orders, heads, *refs):
     count = len(layouts)
     q_ref, k_ref, v_ref, g_ref, log_ref, keys, values = refs[:7]
     terms = refs[7 : 7 + count]
@@ -785,8 +896,8 @@
     short = q_ref.shape[0] - rows
     own, first = pl.ds(short, rows), pl.ds(0, short)
     beside, along = at.beside, at.along[1]
-    at.greet([{"dp": at.roles[3]}])
-    pairs = scatter_start(at, layouts, terms, outs, rest[9:])
+    at.greet()
+    pairs = scatter_start(at, layouts, orders, terms, outs, rest[9:])
     actions = scatter_actions(pairs)
     dq[...] = jnp.zeros_like(dq)
     dk[...] = jnp.zeros_like(dk)
@@ -853,7 +964,7 @@
     got(1, wide_got.at[pl.ds(2, 2)])
     slim[1] = (dv[quarter(2)] + wide_got[3].astype(jnp.float32)).astype(jnp.bfloat16)
     send(3, slim.at[1], slim_got.at[1], along)
-    for action in actions[split + 2 : -count]:
+    for action in actions[split + 2 : -2 * count]:
         action()
     got(2, slim_got.at[0])
     total = dk[quarter(0)] + wide_got[0].astype(jnp.float32) + slim_got[0].astype(jnp.float32)
@@ -861,13 +972,15 @@
     got(3, slim_got.at[1])
     total = dv[quarter(0)] + wide_got[2].astype(jnp.float32) + slim_got[1].astype(jnp.float32)
     dv_out[own] = total.astype(jnp.bfloat16)
-    for action in actions[-count:]:
+    for action in actions[-2 * count :]:
         action()
     for copy in sent:
         copy.wait_send()
 
 
-def attention_backward(rows_in, keys, values, gradients, layouts, heads, rows, columns, number):
+def attention_backward(
+    rows_in, keys, values, gradients, layouts, orders, heads, rows, columns, number
+):
     half = lax.axis_size("fsdp") // 2
     count = len(gradients)
     vmem, hbm = pl.BlockSpec(memory_space=pltpu.VMEM), pl.BlockSpec(memory_space=pl.ANY)
@@ -875,7 +988,7 @@
     quarter_rows = keys.shape[0] // 4
     low_rows = jax.ShapeDtypeStruct((total, model_width), jnp.bfloat16)
     return pl.pallas_call(
-        functools.partial(backward_kernel, half, layouts, heads),
+        functools.partial(backward_kernel, half, layouts, orders, heads),
         out_shape=[low_rows] * 3 + scatter_outs(layouts, rows, columns),
         in_specs=[vmem] * 7 + [hbm] * count,
         out_specs=[vmem] * (3 + count),
@@ -1007,6 +1120,7 @@
         bias.reshape(-1).astype(jnp.float32) for bias in (proj_bias, fc1_bias, fc2_bias)
     )
     item_act = jnp.concatenate([act_rows, long_act], 0)
+    own_long_act = lax.dynamic_slice_in_dim(long_act, group_row, 1, 0)
     item_columns = lax.dynamic_slice_in_dim(item_act, fsdp_index * shard_rows, shard_rows, 1)
     bias_row = lax.dynamic_update_slice_in_dim(
         jnp.zeros((fsdp_count * b_ada.shape[0],), jnp.float32),
@@ -1026,12 +1140,17 @@
     for_device = jnp.stack(
         [partial[:fsdp_count], jnp.repeat(partial[fsdp_count:], SPLIT, axis=0)], 1
     ).reshape(fsdp_count, -1)
-    for_device = jnp.pad(for_device, ((0, 0), (0, -for_device.shape[1] % 1024)))
-    shares = exchange(for_device.reshape(fsdp_count, -1, 128), "fsdp", True, 1)
-    conditioned = unpacked(jnp.sum(shares, axis=0), [(2, width)])[0]
+    for_device = low(jnp.pad(for_device, ((0, 0), (0, -for_device.shape[1] % 2048))))
     mixed_shard = jnp.concatenate([w_qkv, w_proj], 1)
     attention_piece = lax.dynamic_slice_in_dim(mixed_shard, role * model_width, model_width, 1)
-    (attention_full,) = gather([attention_piece], (BY_ROLE,), 2)
+    attention_full, shares = gather(
+        [attention_piece],
+        (BY_ROLE,),
+        ((True, False),),
+        for_device.reshape(fsdp_count, -1, 128),
+        2,
+    )
+    conditioned = unpacked(jnp.sum(shares.astype(jnp.float32), axis=0), [(2, width)])[0]
     attention_full = attention_full.reshape(4, -1, model_width)
     mod_width = 6 * model_width
     modulation = conditioned[:, :mod_width]
@@ -1066,6 +1185,7 @@
         v_rows,
         [fc1_piece, fc2_piece],
         (BY_COLUMN, BY_SHARD),
+        ((True, False), (True, True)),
         head_count,
         quarter_rows,
         3,
@@ -1102,9 +1222,6 @@
     grad_fc1 = low(product_tn(hidden2, d_up)).reshape(half, 2, shard_rows, -1)
     d_hidden2 = product_nt(d_up, fc1_full)
 
-    def blocks(grad):
-        return low(grad).reshape(half, 2, shard_rows, model_width)
-
     slot_shift2 = slot_sum(d_hidden2, short_count, len_short)
     slot_scale2 = slot_sum(d_hidden2 * normed2, short_count, len_short)
     d_mixed = gradient + norm_back(d_hidden2 * (1.0 + scale2), normed2, inverse2)
@@ -1124,6 +1241,7 @@
         values,
         [grad_fc1, grad_fc2],
         (BY_COLUMN, BY_SHARD),
+        ((True, False), (True, True)),
         head_count,
         shard_rows,
         model_width,
@@ -1131,17 +1249,6 @@
     )
     g_w_fc1 = fc1_sum.astype(jnp.float32)
     g_w_fc2 = fc2_sum.reshape(-1, model_width).astype(jnp.float32)
-    attention_sum = scatter_roles(
-        [
-            blocks(product_tn(hidden1, dq_rows)),
-            blocks(product_tn(hidden1, dk_rows)),
-            blocks(product_tn(hidden1, dv_rows)),
-            blocks(product_tn(attention, d_projected)),
-        ],
-        5,
-    )
-    g_w_qkv = attention_sum[:3].transpose(1, 0, 2).reshape(shard_rows, -1).astype(jnp.float32)
-    g_w_proj = attention_sum[3].astype(jnp.float32)
     d_hidden1 = (
         product_nt(dq_rows, attention_full[0])
         + product_nt(dk_rows, attention_full[1])
@@ -1167,13 +1274,24 @@
         ],
         1,
     )
-    member_rows = exchange(packed([low(d_conditioned), low(bias_grad)], 16), "fsdp", False, 6)
-    member_rows, bias_rows = unpacked(member_rows, [(2, width), bias_grad.shape])
+    message = packed([low(d_conditioned), low(bias_grad), short_act, own_long_act], 16)
+    attention_sum, all_rows = scatter_products(
+        [hidden1, attention],
+        [dq_rows, dk_rows, dv_rows, d_projected],
+        (False, False),
+        message,
+        5,
+    )
+    g_w_qkv = attention_sum[:3].transpose(1, 0, 2).reshape(shard_rows, -1).astype(jnp.float32)
+    g_w_proj = attention_sum[3].astype(jnp.float32)
+    all_rows, bias_rows, all_short, all_long = unpacked(
+        all_rows, [(2, width), bias_grad.shape, (model_width,), (model_width,)]
+    )
     long_sum = jnp.sum(
-        member_rows[:, 1].astype(jnp.float32).reshape(-1, SPLIT, width), axis=1
-    )
-    d_items = jnp.concatenate([member_rows[:, 0], low(long_sum)], 0)
-    group_bias = jnp.sum(bias_rows.astype(jnp.float32), axis=0)
+        all_rows[:, :, 1].astype(jnp.float32).reshape(4, -1, SPLIT, width), axis=2
+    )
+    factors = jnp.concatenate([all_rows[:, :, 0], low(long_sum)], 1)
+    d_items = lax.dynamic_index_in_dim(factors, role, 0, keepdims=False)
     d_silu = (
         product_nt(d_items[:, :mod_width], w_ada)
         + product_nt(d_items[:, mod_width : mod_width + head_count], w_head_router)
@@ -1183,11 +1301,11 @@
     d_silu = d_silu.transpose(1, 0, 2).reshape(-1, model_width)
     d_short_cond = lax.dynamic_slice_in_dim(d_silu, fsdp_index, 1, 0) * silu_grad(short_cond)
     d_long_cond = d_silu[fsdp_count:] * silu_grad(long_cond)
-    replicas = exchange(packed([d_items, low(group_bias), item_columns], 16), "dp", False, 8)
-    factors, bias_rows, act_factors = unpacked(
-        replicas, [d_items.shape, group_bias.shape, item_columns.shape]
-    )
-    factors, act_factors = factors.reshape(-1, width), act_factors.reshape(-1, shard_rows)
+    act_factors = jnp.concatenate([all_short, all_long[:, ::SPLIT]], 1)
+    act_factors = lax.dynamic_slice_in_dim(
+        act_factors, fsdp_index * shard_rows, shard_rows, 2
+    ).reshape(-1, shard_rows)
+    factors = factors.reshape(-1, width)
     g_w_ada = product_tn(act_factors, factors[:, :mod_width])
     g_w_head_router = product_tn(act_factors, factors[:, mod_width : mod_width + head_count])
     g_w_group_router = product_tn(act_factors, factors[:, mod_width + head_count :])
@@ -1197,7 +1315,7 @@
         b_ada.shape[0],
         0,
     )
-    bias_sum = jnp.sum(bias_rows.astype(jnp.float32), axis=0)
+    bias_sum = jnp.sum(bias_rows.astype(jnp.float32), axis=(0, 1))
 
     def own_bias(start, count):
         return lax.dynamic_slice_in_dim(bias_sum, start + fsdp_index * count, count, 0)

time: 791 us -> 775 us (0.980)
  matrix products: 143 us -> 129 us
    pallas_call x4, Pallas kernels: 474 us -> 511 us  [the longest x1 173 us: attention_backward(): pl.pallas_call(functools.partial(backward_kernel, half, layouts, orders,...]
    pallas_call x5 -> x2, Pallas kernels: 53.4 us -> 17.6 us  [exchange(): pl.pallas_call(functools.partial(exchange_kernel, axis, size, spread_out)...]
    dot_general x9 -> x5, matrix products: 47.8 us -> 32.9 us  [product_tn(): lax.dot_general(left, right, (((0,), (0,)), ((), ())), preferred_element_...]
    unnamed x167 -> x165, local copies, waits for them, and re-layouts: 15.2 us -> 16.3 us
where the time goes in v4:
time: 775 us; the launch traced here: 770 us
  Pallas kernels  529 us (68%)
  matrix products  129 us (17%)
  other arithmetic  56.2 us (7%)
  local copies, waits for them, and re-layouts  53.9 us (7%)
    pallas_call x1, Pallas kernels, attention_backward(): pl.pallas_call(functools.partial(backward_kernel, half, layouts, orders,...  173 us
    pallas_call x1, Pallas kernels, attention_forward(): pl.pallas_call(functools.partial(forward_kernel, half, layouts, orders, h...  156 us
    pallas_call x1, Pallas kernels, scatter_products(): pl.pallas_call(functools.partial(roles_kernel, half, order), out_shape=sc...  114 us
    pallas_call x1, Pallas kernels, gather(): pl.pallas_call(functools.partial(gather_kernel, half, layouts, orders), o...  68.6 us
    dot_general x9, matrix products, product(): return jnp.dot(left, right, preferred_element_type=jnp.float32)  51 us
    dot_general x9, matrix products, product_nt(): lax.dot_general(left, right, (((1,), (1,)), ((), ())), preferred_element_...  45.2 us
    dot_general x5, matrix products, product_tn(): lax.dot_general(left, right, (((0,), (0,)), ((), ())), preferred_element_...  32.9 us
    reduce_sum x2, other arithmetic, per_device(): jnp.sum(part, axis=0, dtype=jnp.float32)  19.1 us

profile of v4, /device:TPU:0, one launch (start us, length us, event | category | flops | bytes accessed | tf_op | source)
XLA Modules:
  0.0 770.4 jit_solution(12933779400979014349)
XLA Ops:
  4.4 1.5 convert_reduce_fusion
  6.5 1.7 fusion.24
  11.3 9.8 %exchange0.1 = bf16[8,16,128]{2,1,0:T(8,128)(2,1)} custom-call(bf16[16,128]{1,0:T(8,128)(2,1)} %pad_bitcast_fusion.3.rows_ref), custom_call_target="tpu_custom_call" | custom-call | tf_op jit(solution)/shard_map/exchange0/pallas_call | solution.py:98
  25.3 1.9 convolution_add_fusion
  28.6 1.7 constant_dynamic-slice_fusion.2.refs_4_
  30.4 1.9 fusion.44
  32.3 68.6 %gather2.1 = (bf16[4,4,2,144,1152]{4,3,2,1,0:T(8,128)(2,1)}, bf16[8,112,128]{2,1,0:T(8,128)(2,1)}) custom-call(bf16[144,1152]{1,0:T(8,128)(2,1)} %get-tuple-element.114.refs_0_, bf16[8,112,128]{2,1,0:T(8,128)(2,1)} %bitcast.156), custom_call_target="tpu_custom_call" | custom-call | tf_op jit(solution)/shard_map/gather2/pallas_call | solution.py:397
  103.3 2.2 copy.110
  106.5 3.1 copy-done.1
  110.2 3.0 copy-done.2
  113.2 1.7 slice-done.14
  115.5 2.0 fusion.83
  117.5 3.4 convolution_convert_fusion.3.refs_1_
  120.9 2.9 convolution_convert_fusion.2.refs_2_
  123.8 2.9 convolution_convert_fusion.4.refs_0_
  126.7 155.8 %attention3.1 = (f32[512,1152]{1,0:T(8,128)}, f32[512,128]{1,0:T(8,128)}, bf16[1024,1152]{1,0:T(8,128)(2,1)}, bf16[1024,1152]{1,0:T(8,128)(2,1)}, bf16[4,2,144,4...) custom-call(bf16[512,1152]{1,0:T(8,128)(2,1)} %convolution_convert_fusion.4.refs_0_, ...), custom_call_target="tpu_custom_call" | custom-call | tf_op jit(solution)/shard_map/attention3/pallas_call | solution.py:871
  282.5 2.6 multiply_convert_fusion.2.refs_1_
  285.1 3.9 copy.112
  289.1 5.9 fusion.82
  297.4 14.5 %fusion.71 = f32[512,4608]{1,0:T(8,128)} fusion(bf16[1152,4608]{1,0:T(8,128)(2,1)} %bitcast.169, f32[256,6912]{1,0:T(8,128)S(1)} %bitcast.114, f32[256,6912]{1,0:T(8,128)S(1)} %bitcast.120, f32[512,1152]{1,0:T(8,128)S(1)} %get-tuple-element.75, f32[512]{0:T(512)S(1)} %add_rsqrt_fusion, f32[512]{0:T(512)S(1)} %broadcast_multiply_fusion.4), kind=kOutput, calls=%fused_computation.205 | convolution fusion | flops 5440536576 | bytes 36573184 | tf_op jit(solution)/shard_map/dot_general | solution.py:1015
  311.9 16.6 %fusion.10 = (f32[512,4608]{1,0:T(8,128)}, f32[512,4608]{1,0:T(8,128)}) fusion(f32[512,4608]{1,0:T(8,128)} %fusion.71, f32[4608]{0:T(1024)S(1)} %reshape.317, bf16[4608,1152]{1,0:T(8,128)(2,1)} %bitcast.133, f32[256,6912]{1,0:T(8,128)} %copy-done.1, f32[256,6912]{1,0:T(8,128)} %copy-done.2, f32[512]{0:T(512)S(1)} %copy-done.36, ...), kind=kOutput, calls=%fused_computation.39 | convolution fusion | flops 5464129536 | bytes 54284288 | tf_op jit(solution)/shard_map/dot_general | solution.py:1025
  328.5 4.3 slice_reduce_fusion.1
  334.4 2.7 broadcast_in_dim.101
  337.1 2.9 reshape.298
  340.0 18.6 %convolution_add_fusion.1 = f32[512,1152]{1,0:T(8,128)} fusion(bf16[4608,1152]{1,0:T(8,128)(2,1)} %bitcast.134, f32[1152]{0:T(1024)S(1)} %copy-done.54, f32[256,4608]{1,0:T(8,128)} %broadcast_in_dim.101, f32[256,4608]{1,0:T(8,128)} %reshape.298, f32[512,4608]{1,0:T(8,128)} %fusion.71, f32[4608]{0:T(1024)S(1)} %reshape.317), kind=kOutput, calls=%fused_computation.35 | convolution fusion | flops 5464719360 | bytes 31873536 | tf_op jit(solution)/shard_map/dot_general | solution.py:1015
  358.7 12.9 %fusion.79 = (bf16[4608]{0:T(1024)(128)(2,1)}, bf16[512,4608]{1,0:T(8,128)(2,1)}) fusion(f32[512,4608]{1,0:T(8,128)S(1)} %bitcast.124, f32[4608]{0:T(1024)S(1)} %reshape.317, f32[512,4608]{1,0:T(8,128)} %get-tuple-element.111, f32[256,4608]{1,0:T(8,128)} %broadcast_in_dim.101, f32[256,4608]{1,0:T(8,128)} %reshape.298), kind=kLoop, calls=%fused_computation.208 | loop fusion | flops 56618496 | bytes 33057792 | tf_op jit(solution)/shard_map/reduce_sum | solution.py:1236
  371.6 16.2 %convolution_convert_fusion = bf16[4608,1152]{1,0:T(8,128)(2,1)} fusion(f32[256,6912]{1,0:T(8,128)} %copy-done.1, f32[256,6912]{1,0:T(8,128)} %copy-done.2, f32[512]{0:T(512)S(1)} %copy-done.36, bf16[256,1152]{1,0:T(8,128)(2,1)S(1)} %copy-done.27, bf16[256,1152]{1,0:T(8,128)(2,1)} %bitcast.149, f32[256,4608]{1,0:T(8,128)} %broadcast_in_dim.101, ...), kind=kOutput, calls=%fused_computation.10 | convolution fusion | flops 5474156544 | bytes 44847104 | tf_op jit(solution)/shard_map/dot_general | solution.py:1019
  387.8 13.9 %fusion.68 = (f32[512]{0:T(512)S(1)}, f32[512]{0:T(512)S(1)}, bf16[512,1152]{1,0:T(8,128)(2,1)S(1)}, f32[512,1152]{1,0:T(8,128)S(1)}, f32[512,1152]{1,0:T(8,128)S(1)}, /*index=5*/f32[512,1152]{1,0:T(8,128)S(1)}) fusion(f32[256,6912]{1,0:T(8,128)} %copy-done.1, f32[256,6912]{1,0:T(8,128)} %copy-done.2, f32[512]{0:T(512)S(1)} %add_rsqrt_fusion, ...), kind=kOutput, calls=%fused_computation.203 | convolution fusion | flops 5449382912 | bytes 43657216 | tf_op jit(solution)/shard_map/dot_general | solution.py:1025
  404.0 6.2 fusion.81
  410.2 2.9 multiply_reduce_fusion
  413.3 1.3 fusion.67
  414.7 2.4 copy.111.refs_3_
  417.1 12.4 %convolution_convert_fusion.1 = bf16[1152,4608]{1,0:T(8,128)(2,1)} fusion(bf16[512,4608]{1,0:T(8,128)(2,1)} %get-tuple-element.70, f32[256,6912]{1,0:T(8,128)} %copy-done.1, f32[256,6912]{1,0:T(8,128)} %copy-done.2, f32[512,1152]{1,0:T(8,128)S(1)} %copy-done.5, f32[512]{0:T(512)S(1)} %add_rsqrt_fusion, f32[512]{0:T(512)S(1)} %broadcast_multiply_fusion.4), kind=kOutput, calls=%fused_computation.11 | convolution fusion | flops 5445844992 | bytes 31854592 | tf_op jit(solution)/shard_map/dot_general | solution.py:1019
  429.4 173.1 %attention4.1 = (bf16[512,1152]{1,0:T(8,128)(2,1)}, bf16[512,1152]{1,0:T(8,128)(2,1)}, bf16[512,1152]{1,0:T(8,128)(2,1)}, bf16[144,4608]{1,0:T(8,128)(2,1)}, bf16[4,144,1152]{2,1,0:T(8,128)(2,1)}) custom-call(bf16[512,1152]{1,0:T(8,128)(2,1)} %convolution_convert_fusion.4.refs_0_, bf16[512,1152]{1,0:T(8,128)(2,1)} %convolution_convert_fusion.3.refs_1_, ...), custom_call_target="tpu_custom_call" | custom-call | tf_op jit(solution)/shard_map/attention4/pallas_call | solution.py:990
  602.5 4.1 fusion.91
  606.8 4.2 convolution_add_fusion.3
  612.0 2.6 fusion.69
  614.6 2.7 fusion.13
  619.1 113.7 %scatter5.1 = (bf16[4,144,1152]{2,1,0:T(8,128)(2,1)}, bf16[4,8,192,128]{3,2,1,0:T(8,128)(2,1)}) custom-call(bf16[512,1152]{1,0:T(8,128)(2,1)} %copy-done.19, bf16[512,1152]{1,0:T(8,128)(2,1)} %copy-done.13, bf16[512,1152]{1,0:T(8,128)(2,1)} %get-tuple-element.40.refs_2_, bf16[512,1152]{1,0:T(8,128)(2,1)} %get-tuple-element.41.refs_3_, ...), custom_call_target="tpu_custom_call" | custom-call | tf_op jit(solution)/shard_map/scatter5/pallas_call | solution.py:682
  732.8 2.1 reshape.307
  737.7 1.9 bitcast_convert_fusion.1
  739.6 1.3 convert_bitcast_fusion
  740.9 1.4 copy.120
  746.8 7.8 %exchange7.1 = f32[8,16,128]{2,1,0:T(8,128)} custom-call(f32[16,128]{1,0:T(8,128)} %pad_bitcast_fusion.2.rows_ref), custom_call_target="tpu_custom_call" | custom-call | tf_op jit(solution)/shard_map/exchange7/pallas_call | solution.py:98
  757.3 1.3 multiply_multiply_fusion.3
  763.7 1.8 convert_element_type.209
  765.5 1.8 bitcast_convert_fusion
  767.3 2.6 fusion.42
  (288 shorter events, 41.4 us)
Async XLA Ops:
  0.7 23.8 %copy-start = (bf16[144,36]{0,1:T(8,128)(2,1)S(1)}, bf16[144,36]{0,1:T(8,128)(2,1)}, u32[]{:S(2)}) copy-start(bf16[144,36]{0,1:T(8,128)(2,1)} %param.36) | copy-start | bytes 31108
  0.7 8.1 %copy-start.44 = (f32[2,1152]{1,0:T(2,128)S(1)}, f32[2,1152]{1,0:T(2,128)}, u32[]{:S(2)}) copy-start(f32[2,1152]{1,0:T(2,128)} %param.26) | copy-start | bytes 27652
  0.7 8.1 %copy-start.51 = (f32[1,1152]{1,0:T(1,128)S(1)}, f32[1,1152]{1,0:T(1,128)}, u32[]{:S(2)}) copy-start(f32[1,1152]{1,0:T(1,128)} %param.25) | copy-start | bytes 13828
  0.7 9.9 %copy-start.61 = (bf16[144]{0:T(256)(128)(2,1)S(1)}, bf16[144]{0:T(256)(128)(2,1)}, u32[]{:S(2)}) copy-start(bf16[144]{0:T(256)(128)(2,1)} %param.43) | copy-start | bytes 868
  0.7 9.9 %copy-start.59 = (bf16[576]{0:T(1024)(128)(2,1)S(1)}, bf16[576]{0:T(1024)(128)(2,1)}, u32[]{:S(2)}) copy-start(bf16[576]{0:T(1024)(128)(2,1)} %param.41) | copy-start | bytes 3460
  0.7 9.9 %copy-start.60 = (bf16[144]{0:T(256)(128)(2,1)S(1)}, bf16[144]{0:T(256)(128)(2,1)}, u32[]{:S(2)}) copy-start(bf16[144]{0:T(256)(128)(2,1)} %param.39) | copy-start | bytes 868
  106.0 3.6 copy-start.1
  106.0 3.6 copy-start.6
  106.0 7.1 slice-start.13
  109.6 3.6 copy-start.2
  109.6 5.3 slice-start.14
  109.6 5.9 slice-start.15
  115.5 8.3 %copy-start.19 = (bf16[512,1152]{1,0:T(8,128)(2,1)}, bf16[512,1152]{1,0:T(8,128)(2,1)S(1)}, u32[]{:S(2)}) copy-start(bf16[512,1152]{1,0:T(8,128)(2,1)S(1)} %fusion.18.refs_0_) | copy-start | bytes 3538948
  117.5 6.3 copy-start.25
  285.1 4.0 copy-start.13
  285.1 4.0 copy-start.7
  285.1 4.0 copy-start.10
  285.1 4.0 copy-start.39
  289.0 7.4 slice-start
  289.0 7.4 slice-start.6
  289.1 7.4 slice-start.1
  289.1 8.3 %slice-start.7 = ((s8[7077888]{0:T(1024)(128)(4,1)}), s8[2883584]{0:T(1024)(128)(4,1)S(1)}, s32[]{:S(2)}) async-start(s8[7077888]{0:T(1024)(128)(4,1)} %bitcast.119), calls=%async_computation.7 | async-start | bytes 5767168
  297.3 14.5 %copy-start.27 = (bf16[256,1152]{1,0:T(8,128)(2,1)S(1)}, bf16[256,1152]{1,0:T(8,128)(2,1)}, u32[]{:S(2)}) copy-start(bf16[256,1152]{1,0:T(8,128)(2,1)} %param.45) | copy-start | bytes 1769476
  297.3 14.5 %copy-start.28 = (bf16[1,256,1152]{2,1,0:T(8,128)(2,1)S(1)}, bf16[1,256,1152]{2,1,0:T(8,128)(2,1)}, u32[]{:S(2)}) copy-start(bf16[1,256,1152]{2,1,0:T(8,128)(2,1)} %param.44) | copy-start | bytes 1769476
  297.3 14.5 %copy-start.36 = (f32[512]{0:T(512)S(1)}, f32[512]{0:T(512)}, u32[]{:S(2)}) copy-start(f32[512]{0:T(512)} %add_convert_fusion.1) | copy-start | bytes 6148
  328.5 4.6 copy-start.62
  328.5 4.5 copy-start.63
  337.1 21.5 %slice-start.10 = ((s8[9437184]{0:T(1024)(128)(4,1)}), s8[4194304]{0:T(1024)(128)(4,1)S(1)}, s32[]{:S(2)}) async-start(s8[9437184]{0:T(1024)(128)(4,1)} %bitcast.123), calls=%async_computation.10 | async-start | bytes 8388608
  340.0 18.6 %slice-start.11 = ((s8[9437184]{0:T(1024)(128)(4,1)}), s8[4194304]{0:T(1024)(128)(4,1)S(1)}, s32[]{:S(2)}) async-start(s8[9437184]{0:T(1024)(128)(4,1)} %bitcast.123), calls=%async_computation.11 | async-start | bytes 8388608
  340.0 18.6 %slice-start.12 = ((s8[9437184]{0:T(1024)(128)(4,1)}), s8[1048576]{0:T(1024)(128)(4,1)S(1)}, s32[]{:S(2)}) async-start(s8[9437184]{0:T(1024)(128)(4,1)} %bitcast.123), calls=%async_computation.12 | async-start | bytes 2097152
  371.6 32.4 %slice-start.2 = ((s8[7077888]{0:T(1024)(128)(4,1)}), s8[2883584]{0:T(1024)(128)(4,1)S(1)}, s32[]{:S(2)}) async-start(s8[7077888]{0:T(1024)(128)(4,1)} %bitcast.115), calls=%async_computation.2 | async-start | bytes 5767168
  387.8 16.2 %slice-start.3 = ((s8[7077888]{0:T(1024)(128)(4,1)}), s8[4194304]{0:T(1024)(128)(4,1)S(1)}, s32[]{:S(2)}) async-start(s8[7077888]{0:T(1024)(128)(4,1)} %bitcast.115), calls=%async_computation.3 | async-start | bytes 8388608
  404.0 6.2 copy-start.14
  404.0 6.2 copy-start.26
  404.0 6.2 copy-start.38
  413.2 3.9 copy-start.5
  602.5 8.4 %slice-start.4 = ((s8[7077888]{0:T(1024)(128)(4,1)}), s8[4194304]{0:T(1024)(128)(4,1)S(1)}, s32[]{:S(2)}) async-start(s8[7077888]{0:T(1024)(128)(4,1)} %bitcast.117), calls=%async_computation.4 | async-start | bytes 8388608
  602.5 8.4 %slice-start.8 = ((s8[7077888]{0:T(1024)(128)(4,1)}), s8[4194304]{0:T(1024)(128)(4,1)S(1)}, s32[]{:S(2)}) async-start(s8[7077888]{0:T(1024)(128)(4,1)} %bitcast.121), calls=%async_computation.8 | async-start | bytes 8388608
  606.7 4.3 slice-start.5
  606.7 4.3 slice-start.9
  606.7 4.3 copy-start.8
  606.7 4.3 copy-start.11
  606.7 4.9 copy-start.16
  606.7 5.2 copy-start.20
  606.7 5.2 copy-start.42
  606.8 5.2 copy-start.48
  754.6 8.0 %copy-start.22 = (bf16[512,1152]{1,0:T(8,128)(2,1)S(1)}, bf16[512,1152]{1,0:T(8,128)(2,1)}, u32[]{:S(2)}) copy-start(bf16[512,1152]{1,0:T(8,128)(2,1)} %get-tuple-element.86) | copy-start | bytes 3538948
  760.1 3.6 copy-start.31
  (32 other events, 63.1 us)

commit v5 on v4

--- a/solution.py
+++ b/solution.py
@@ -104,8 +104,13 @@
         compiler_params=pltpu.CompilerParams(
             collective_id=number, has_side_effects=True, vmem_limit_bytes=VMEM_BYTES
         ),
+        cost_estimate=taking(8),
         name=f"exchange{number}",
     )(rows)
+
+
+def taking(microseconds):
+    return pl.CostEstimate(flops=0, transcendentals=0, bytes_accessed=microseconds * 3_000_000)
 
 
 class Place:
@@ -201,8 +206,8 @@
 
 
 class GatherUnit:
-    def __init__(self, at, piece, out, layout, start, count, side_first, send_sem, recv_sem):
-        self.at, self.piece, self.out, self.layout = at, piece, out, layout
+    def __init__(self, at, line, out, layout, start, count, side_first, send_sem, recv_sem):
+        self.at, self.line, self.out, self.layout = at, line, out, layout
         self.rows = pl.ds(start, count)
         self.side_first, self.send_sem, self.recv_sem = side_first, send_sem, recv_sem
         self.sent = []
@@ -227,30 +232,35 @@
         half = self.at.half
         return half, 2 * half, 3 * half, 3 * half + 1
 
-    def begin(self):
+    def block_to(self, step, peer):
         at = self.at
-
-        def own_to(peer):
-            return lambda: (
-                self.piece.at[self.rows], self.view(at.role, at.line, at.side), peer
-            )
-
+        where = (at.role, at.lines[step], at.side)
+        if step < len(self.line):
+            return lambda: (self.line[step].at[self.rows], self.view(*where), peer)
+        return lambda: (self.view(*where), self.view(*where), peer)
+
+    def begin(self, to_side):
         beside, across, _, _ = self.numbers()
-        for step in range(1, at.half):
-            self.send(step, own_to(at.along[step]))
-        self.send(beside, own_to(at.beside))
-        self.send(across, own_to(at.across))
+        for step in range(len(self.line)):
+            if to_side:
+                self.send(beside + step, self.block_to(step, self.at.beside))
+            else:
+                self.send(across + step, self.block_to(step, self.at.across))
+
+    def begin_line(self):
+        if len(self.line) == 1:
+            for step in range(1, self.at.half):
+                self.send(step, self.block_to(0, self.at.along[step]))
+
+    def line_step(self, step):
+        beside, across, _, _ = self.numbers()
+        if step >= len(self.line):
+            self.got(step, self.view(self.at.role, self.at.lines[step], self.at.side))
+            self.send(across + step, self.block_to(step, self.at.across))
+            self.send(beside + step, self.block_to(step, self.at.beside))
 
     def pass_on(self, number, peer, *where):
         self.send(number, lambda: (self.view(*where), self.view(*where), peer))
-
-    def line_step(self, step):
-        at = self.at
-        where = (at.role, at.lines[step], at.side)
-        self.got(step, self.view(*where))
-        beside, across, _, _ = self.numbers()
-        self.pass_on(beside + step, at.beside, *where)
-        self.pass_on(across + step, at.across, *where)
 
     def second(self):
         at, every = self.at, slice(None)
@@ -303,15 +313,16 @@
             self.copy_of(number, make).wait_send()
 
 
-def gather_start(at, layouts, orders, pieces, outs, send_sem, recv_sem, local_sem):
+def gather_start(at, layouts, orders, lines, outs, send_sem, recv_sem, local_sem):
     pairs, local = [], []
     for matrix, layout in enumerate(layouts):
-        rows = pieces[matrix].shape[0]
+        line = lines[matrix]
+        rows = line[0].shape[0]
         pairs.append(
             [
                 GatherUnit(
                     at,
-                    pieces[matrix],
+                    line,
                     outs[matrix],
                     layout,
                     start,
@@ -324,19 +335,23 @@
             ]
         )
 
-        def make(matrix=matrix, layout=layout, rows=rows):
-            target = block_view(outs[matrix], layout, at.role, at.line, at.side, pl.ds(0, rows))
-            return pltpu.make_async_copy(pieces[matrix], target, local_sem.at[matrix])
-
-        make().start()
-        local.append(make)
-    for unit in pairs[0]:
-        unit.begin()
+        def make(step, matrix=matrix, layout=layout, line=line, rows=rows):
+            place = (at.role, at.lines[step], at.side, pl.ds(0, rows))
+            return pltpu.make_async_copy(
+                line[step], block_view(outs[matrix], layout, *place), local_sem.at[matrix, step]
+            )
+
+        for step in range(len(line)):
+            make(step).start()
+            local.append(functools.partial(make, step))
+    for pair in pairs:
+        for unit in pair:
+            unit.begin(False)
     return pairs, local
 
 
 def gather_actions(pairs, local):
-    half, count = pairs[0][0].at.half, len(pairs)
+    count = len(pairs)
     actions = []
 
     def each(pair, name, *given):
@@ -350,13 +365,17 @@
         for make in local:
             make().wait()
 
+    half = pairs[0][0].at.half
+    for pair in pairs:
+        each(pair, "begin_line")
+    for pair in pairs:
+        each(pair, "begin", True)
     actions.append(settle)
     for matrix in range(count + 1):
         if matrix < count:
-            for step in range(1, half):
-                each(pairs[matrix], "line_step", step)
-            if matrix + 1 < count:
-                each(pairs[matrix + 1], "begin")
+            if len(pairs[matrix][0].line) == 1:
+                for step in range(1, half):
+                    each(pairs[matrix], "line_step", step)
             each(pairs[matrix], "second")
         if matrix:
             each(pairs[matrix - 1], "third")
@@ -369,46 +388,73 @@
     return [
         pltpu.SemaphoreType.DMA((2 * count, 3 * half + 5)),
         pltpu.SemaphoreType.DMA((2 * count, 3 * half + 5)),
-        pltpu.SemaphoreType.DMA((count,)),
+        pltpu.SemaphoreType.DMA((count, half)),
     ]
 
 
-def gather_kernel(half, layouts, orders, *refs):
-    count = len(layouts)
+class LineCopies:
+    def __init__(self, at, block, out, send_sem, recv_sem):
+        self.at, self.block, self.out = at, block, out
+        self.send_sem, self.recv_sem = send_sem, recv_sem
+
+    def copy_of(self, step):
+        return remote(
+            self.block,
+            self.out.at[step],
+            self.send_sem.at[step],
+            self.recv_sem.at[step],
+            self.at.along[step],
+        )
+
+    def begin(self):
+        for step in range(1, self.at.half):
+            self.copy_of(step).start()
+
+    def finish(self):
+        for step in range(1, self.at.half):
+            self.copy_of(step).wait_recv()
+            self.copy_of(step).wait_send()
+
+
+def gather_kernel(half, layout, order, *refs):
+    piece, next_piece, rows, whole, line, out = refs[:6]
+    message_sems, line_sems, scratch = refs[6:8], refs[8:10], refs[10:]
     at = Place(half)
-    rows, out = refs[count], refs[2 * count + 1]
-    scratch = refs[2 * count + 2 :]
-    message = Message(at, rows, out, True, *scratch[:2])
+    message = Message(at, rows, out, True, *message_sems)
+    copies = LineCopies(at, next_piece, line, *line_sems)
     at.greet(True)
     message.begin()
-    pairs, local = gather_start(
-        at, layouts, orders, refs[:count], refs[count + 1 : 2 * count + 1], *scratch[2:]
-    )
-    for action in gather_actions(pairs, local):
+    pairs, local = gather_start(at, (layout,), (order,), [[piece]], [whole], *scratch)
+    actions = gather_actions(pairs, local)
+    actions[0]()
+    copies.begin()
+    for action in actions[1:]:
         action()
     message.arrive()
     message.finish()
-
-
-def gather(pieces, layouts, orders, rows, number):
+    copies.finish()
+
+
+def gather(piece, layout, order, next_piece, rows, number):
     half = lax.axis_size("fsdp") // 2
-    count = len(pieces)
     vmem, hbm = pl.BlockSpec(memory_space=pltpu.VMEM), pl.BlockSpec(memory_space=pl.ANY)
     return pl.pallas_call(
-        functools.partial(gather_kernel, half, layouts, orders),
+        functools.partial(gather_kernel, half, layout, order),
         out_shape=[
-            jax.ShapeDtypeStruct(whole_shape(layout, half, *piece.shape), piece.dtype)
-            for piece, layout in zip(pieces, layouts)
-        ]
-        + [jax.ShapeDtypeStruct(rows.shape, rows.dtype)],
-        in_specs=[vmem] * (count + 1),
-        out_specs=[hbm] * count + [vmem],
-        scratch_shapes=message_scratch(half) + gather_scratch(count, half),
+            jax.ShapeDtypeStruct(whole_shape(layout, half, *piece.shape), piece.dtype),
+            jax.ShapeDtypeStruct((half,) + next_piece.shape, next_piece.dtype),
+            jax.ShapeDtypeStruct(rows.shape, rows.dtype),
+        ],
+        in_specs=[vmem] * 3,
+        out_specs=[hbm, vmem, vmem],
+        scratch_shapes=message_scratch(half)
+        + [pltpu.SemaphoreType.DMA((half,)), pltpu.SemaphoreType.DMA((half,))]
+        + gather_scratch(1, half),
         compiler_params=pltpu.CompilerParams(
             collective_id=number, has_side_effects=True, vmem_limit_bytes=VMEM_BYTES
         ),
         name=f"gather{number}",
-    )(*pieces, rows)
+    )(piece, next_piece, rows)
 
 
 def accumulate(target, source):
@@ -429,11 +475,9 @@
         self.rows = pl.ds(start, count)
         self.across_first = across_first
         self.send_sem, self.recv_sem, self.stage_sem = sems
-        self.core_buf, self.first_buf, self.last_buf, self.line_buf, self.stage = buffers
+        self.core_buf, self.first_buf, self.last_buf, self.stage = buffers
         self.sent = []
-        half = at.half
         self.base_first, self.base_last = 4, 6
-        self.base_line, self.base_share = 6 + half, 6 + 2 * half
         self.first_peer = at.across if across_first else at.beside
         self.last_peer = at.beside if across_first else at.across
 
@@ -443,12 +487,6 @@
         return block_view(
             self.terms, self.layout, role, slice(None), self.at.sides[side_step], self.rows
         )
-
-    def out_view(self, role):
-        if self.layout == BY_COLUMN:
-            width = self.out.shape[1] // 4
-            return self.out.at[self.rows, pl.ds(pl.multiple_of(role * width, 128), width)]
-        return self.out.at[role, self.rows]
 
     def send(self, number, make):
         self.sent.append((number, make))
@@ -513,39 +551,9 @@
         block = self.last_buf.at[line]
         self.got(self.base_last + step, block)
         accumulate(block, self.first_buf.at[0, line])
-        if step:
-            self.send(
-                self.base_line + step,
-                lambda: (self.last_buf.at[line], self.line_buf.at[step], self.at.along[step]),
-            )
-
-    def end(self):
-        at = self.at
-        own = self.last_buf.at[at.line]
-        for step in range(1, at.half):
-            self.got(self.base_line + step, self.line_buf.at[step])
-            accumulate(own, self.line_buf.at[step])
-        target = self.out_view(at.role)
-        target[...] = own[...]
-        for step in (2, 1):
-            self.send(
-                self.base_share + step,
-                lambda step=step: (
-                    self.last_buf.at[at.line], self.out_view(at.role), {"dp": at.roles[step]}
-                ),
-            )
+        self.out[line, self.rows] = block[...]
 
     def finish(self):
-        roles = self.at.roles
-        self.got(self.base_share + 2, self.out_view(roles[2]))
-        self.send(
-            self.base_share + 3,
-            lambda: (self.out_view(roles[2]), self.out_view(roles[2]), self.at.core),
-        )
-
-    def close(self):
-        for step in (1, 3):
-            self.got(self.base_share + step, self.out_view(self.at.roles[step]))
         for number, make in self.sent:
             self.copy_of(number, make).wait_send()
 
@@ -558,7 +566,6 @@
         [("paired", 0, 1), ("paired", 0, 0)],
         [("joined", 1), ("joined", 0)],
         [("lined", step) for step in steps],
-        [("end",)],
     ]
     actions = []
 
@@ -574,9 +581,8 @@
             if 0 <= turn - index < len(stages):
                 for call in stages[turn - index]:
                     each(pair, *call)
-    for name in ("finish", "close"):
-        for pair in pairs:
-            each(pair, name)
+    for pair in pairs:
+        each(pair, "finish")
     return actions
 
 
@@ -597,7 +603,7 @@
                     size,
                     orders[matrix][part],
                     [sem.at[unit] for sem in sems],
-                    buffers[5 * unit : 5 * unit + 5],
+                    buffers[4 * unit : 4 * unit + 4],
                 )
             )
         pairs.append(pair)
@@ -608,29 +614,116 @@
 
 
 def scatter_scratch(count, half, rows, columns):
-    scratch = [pltpu.SemaphoreType.DMA((2 * count, 2 * half + 10))] * 2
+    scratch = [pltpu.SemaphoreType.DMA((2 * count, half + 6))] * 2
     scratch += [pltpu.SemaphoreType.DMA((2 * count,))]
     for _ in range(count):
         for _, size in cut(rows):
-            for lead in ((2, 2, half), (2, half), (half,), (half,), (half,)):
+            for lead in ((2, 2, half), (2, half), (half,), (half,)):
                 scratch.append(pltpu.VMEM(lead + (size, columns), jnp.bfloat16))
     return scratch
 
 
-def scatter_outs(layouts, rows, columns):
-    return [
-        jax.ShapeDtypeStruct(
-            (rows, 4 * columns) if layout == BY_COLUMN else (4, rows, columns), jnp.bfloat16
+def scatter_outs(count, half, rows, columns):
+    return [jax.ShapeDtypeStruct((half, rows, columns), jnp.bfloat16)] * count
+
+
+def swap(value, axis, mask):
+    size = lax.axis_size(axis)
+    return lax.ppermute(value, axis, [(source, source ^ mask) for source in range(size)])
+
+
+def along_line(near, later):
+    line = lax.axis_index("fsdp") // 2
+
+    def at(sums, index):
+        return lax.dynamic_index_in_dim(sums, index, 0, keepdims=False)
+
+    return [at(near, line)] + [
+        swap(at(near if mask == 2 else later, line ^ (mask // 2)), "fsdp", mask)
+        for mask in range(2, lax.axis_size("fsdp"), 2)
+    ]
+
+
+def four_roles(terms):
+    role = lax.axis_index("dp")
+    total = sum(term.astype(jnp.float32) for term in terms).astype(jnp.bfloat16)
+    across = swap(total, "dp", 2)
+    blocks = [total, swap(total, "dp", 1), across, swap(across, "dp", 1)]
+    whole = jnp.zeros((4,) + total.shape, jnp.float32)
+    for step, block in enumerate(blocks):
+        whole = lax.dynamic_update_slice(
+            whole, block[None].astype(jnp.float32), (role ^ step, 0, 0)
         )
-        for layout in layouts
+    return whole
+
+
+class LineSum:
+    def __init__(self, at, near, out, buffer, send_sem, recv_sem, local_sem):
+        self.at, self.near, self.out, self.buffer = at, near, out, buffer
+        self.send_sem, self.recv_sem, self.local_sem = send_sem, recv_sem, local_sem
+        self.sent = []
+
+    def send(self, number, source, target, peer):
+        copy = remote(source, target, self.send_sem.at[number], self.recv_sem.at[number], peer)
+        copy.start()
+        self.sent.append(copy)
+
+    def got(self, number, target):
+        remote(
+            target, target, self.send_sem.at[number], self.recv_sem.at[number], self.at.core
+        ).wait_recv()
+
+    def begin(self):
+        at = self.at
+        for step in range(1, at.half):
+            self.send(step, self.near.at[at.lines[step]], self.buffer.at[step], at.along[step])
+        self.local = pltpu.make_async_copy(
+            self.near.at[at.line], self.buffer.at[0], self.local_sem
+        )
+        self.local.start()
+
+    def total(self):
+        at, own = self.at, self.buffer.at[0]
+        self.local.wait()
+        for step in range(1, at.half):
+            self.got(step, self.buffer.at[step])
+            accumulate(own, self.buffer.at[step])
+        self.out[at.role] = own[...]
+        self.send(at.half, own, self.out.at[at.role], at.across)
+        self.send(at.half + 1, own, self.out.at[at.role], at.core)
+
+    def share(self):
+        at = self.at
+        far = self.out.at[at.roles[2]]
+        self.got(at.half, far)
+        self.send(at.half + 2, far, far, at.core)
+
+    def finish(self):
+        at = self.at
+        self.got(at.half + 1, self.out.at[at.roles[1]])
+        self.got(at.half + 2, self.out.at[at.roles[3]])
+        for copy in self.sent:
+            copy.wait_send()
+
+
+def roles_kernel(half, order, *refs):
+    ins, rows, nears = refs[:6], refs[6], refs[7:9]
+    out, rows_out, sums = refs[9], refs[10], refs[11:13]
+    left, right, terms, local_sem, line_buf, line_send, line_recv, line_local = refs[13:21]
+    scratch = refs[21:]
+    at = Place(half)
+    lines = [
+        LineSum(
+            at,
+            nears[index],
+            sums[index],
+            line_buf.at[index],
+            line_send.at[index],
+            line_recv.at[index],
+            line_local.at[index],
+        )
+        for index in range(2)
     ]
-
-
-def roles_kernel(half, order, *refs):
-    ins, rows, out, rows_out = refs[:6], refs[6], refs[7], refs[8]
-    left, right, terms, local_sem = refs[9:13]
-    scratch = refs[13:]
-    at = Place(half)
     local = []
     for index in range(6):
         target = left.at[index] if index < 2 else right.at[index - 2]
@@ -640,6 +733,8 @@
     message = Message(at, rows, rows_out, False, *scratch[:2])
     at.greet(True)
     message.begin()
+    for line in lines:
+        line.begin()
     for copy in local:
         copy.wait()
     shard_rows, columns = terms.shape[3:]
@@ -666,38 +761,52 @@
     pairs = scatter_start(at, (BY_ROLE,), (order,), [terms], [out], scratch[2:])
     two_roles(at.roles[2], at.roles[0])
     actions = scatter_actions(pairs)
-    for action in actions[:5]:
+    for action in actions[:4]:
         action()
     message.arrive()
-    for action in actions[5:]:
+    for action in actions[4:6]:
         action()
+    lines[0].total()
+    for action in actions[6:]:
+        action()
+    lines[0].share()
+    lines[1].total()
     message.finish()
-
-
-def scatter_products(lefts, rights, order, message, number):
+    lines[0].finish()
+    lines[1].share()
+    lines[1].finish()
+
+
+def scatter_products(lefts, rights, order, message, nears, number):
     half = lax.axis_size("fsdp") // 2
     model_width = lefts[0].shape[1]
     rows, columns = model_width // (2 * half), rights[0].shape[1]
     vmem, hbm = pl.BlockSpec(memory_space=pltpu.VMEM), pl.BlockSpec(memory_space=pl.ANY)
     return pl.pallas_call(
         functools.partial(roles_kernel, half, order),
-        out_shape=scatter_outs((BY_ROLE,), rows, columns)
-        + [jax.ShapeDtypeStruct((4, 2 * half) + message.shape, message.dtype)],
-        in_specs=[hbm] * 6 + [vmem],
-        out_specs=[vmem] * 2,
+        out_shape=scatter_outs(1, half, rows, columns)
+        + [jax.ShapeDtypeStruct((4, 2 * half) + message.shape, message.dtype)]
+        + [jax.ShapeDtypeStruct((4, rows, columns), jnp.bfloat16)] * 2,
+        in_specs=[hbm] * 6 + [vmem] + [hbm] * 2,
+        out_specs=[vmem] * 4,
         scratch_shapes=[
             pltpu.VMEM((2,) + lefts[0].shape, jnp.bfloat16),
             pltpu.VMEM((4,) + rights[0].shape, jnp.bfloat16),
             pltpu.VMEM((4, half, 2, rows, columns), jnp.bfloat16),
             pltpu.SemaphoreType.DMA((6,)),
+            pltpu.VMEM((2, half, rows, columns), jnp.bfloat16),
+            pltpu.SemaphoreType.DMA((2, half + 3)),
+            pltpu.SemaphoreType.DMA((2, half + 3)),
+            pltpu.SemaphoreType.DMA((2,)),
         ]
         + message_scratch(half)
         + scatter_scratch(1, half, rows, columns),
         compiler_params=pltpu.CompilerParams(
             collective_id=number, has_side_effects=True, vmem_limit_bytes=VMEM_BYTES
         ),
+        cost_estimate=taking(90),
         name=f"scatter{number}",
-    )(*lefts, *rights, message)
+    )(*lefts, *rights, message, *nears)
 
 
 def head_window(head, width, columns):
@@ -775,10 +884,12 @@
 def forward_kernel(half, layouts, orders, heads, *refs):
     count = len(layouts)
     q_ref, k_ref, v_ref = refs[:3]
-    pieces = refs[3 : 3 + count]
-    o_ref, log_ref, keys, values = refs[3 + count : 7 + count]
-    outs = refs[7 + count : 7 + 2 * count]
-    send_sem, recv_sem = refs[7 + 2 * count : 9 + 2 * count]
+    fc1_piece, fc1_line, fc2_piece = refs[3:6]
+    lines = [[fc1_piece] + [fc1_line.at[step] for step in range(1, half)], [fc2_piece]]
+    refs = refs[6:]
+    o_ref, log_ref, keys, values = refs[:4]
+    outs = refs[4 : 4 + count]
+    send_sem, recv_sem = refs[4 + count : 6 + count]
     at = Place(half)
     width = q_ref.shape[1] // heads
     rows = keys.shape[0] // 4
@@ -804,9 +915,12 @@
     send(1, v_ref.at[own], quarter(values, 2), along)
     send(2, v_ref.at[own], quarter(values, 1), beside)
     send(3, k_ref.at[own], quarter(keys, 2), along)
-    pairs, local = gather_start(
-        at, layouts, orders, pieces, outs, *refs[9 + 2 * count :]
-    )
+    pairs, local = gather_start(at, layouts, orders, lines, outs, *refs[6 + count :])
+    actions = gather_actions(pairs, local)
+    beside_first, settle, second, line_steps = count, 2 * count, 2 * count + 1, 2 * count + 2
+    late = line_steps + half - 1
+    for action in actions[:beside_first]:
+        action()
     quarter(keys, 0)[...] = k_ref[own]
     quarter(values, 0)[...] = v_ref[own]
     o_ref[...] = jnp.zeros_like(o_ref)
@@ -818,8 +932,6 @@
         got(1, quarter(values, 2))
         send(5, quarter(values, 2), quarter(values, 3), beside)
 
-    actions = gather_actions(pairs, local)
-    early = 1 + (half - 1)
     first = pl.ds(0, short)
     run_heads(
         heads,
@@ -832,10 +944,12 @@
             o_ref.at[first],
             log_ref.at[first],
         ),
-        [lambda: None, lambda: None, lambda: None] + actions[:early],
+        [],
     )
     pass_on()
-    for action in actions[early : early + 2]:
+    for action in (
+        actions[beside_first : settle + 1] + actions[line_steps:late] + actions[second:line_steps]
+    ):
         action()
     got(2, quarter(values, 1))
     got(3, quarter(keys, 2))
@@ -846,7 +960,7 @@
         lambda head: attend_head(
             head, width, q_ref.at[own], keys, values, o_ref.at[own], log_ref.at[own]
         ),
-        actions[early + 2 : -count],
+        actions[late:-count],
     )
     for action in actions[-count:]:
         action()
@@ -854,9 +968,9 @@
         copy.wait_send()
 
 
-def attention_forward(q_rows, k_rows, v_rows, pieces, layouts, orders, heads, rows, number):
+def attention_forward(q_rows, k_rows, v_rows, blocks, layouts, orders, heads, rows, number):
     half = lax.axis_size("fsdp") // 2
-    count = len(pieces)
+    count = len(layouts)
     vmem, hbm = pl.BlockSpec(memory_space=pltpu.VMEM), pl.BlockSpec(memory_space=pl.ANY)
     total, columns = q_rows.shape
     outs = [
@@ -865,21 +979,22 @@
         jax.ShapeDtypeStruct((4 * rows, columns), jnp.bfloat16),
         jax.ShapeDtypeStruct((4 * rows, columns), jnp.bfloat16),
     ] + [
-        jax.ShapeDtypeStruct(whole_shape(layout, half, *piece.shape), piece.dtype)
-        for piece, layout in zip(pieces, layouts)
+        jax.ShapeDtypeStruct(whole_shape(layout, half, *blocks[0].shape), blocks[0].dtype)
+        for layout in layouts
     ]
     return pl.pallas_call(
         functools.partial(forward_kernel, half, layouts, orders, heads),
         out_shape=outs,
-        in_specs=[vmem] * (3 + count),
+        in_specs=[vmem] * (3 + len(blocks)),
         out_specs=[vmem] * 4 + [hbm] * count,
         scratch_shapes=[pltpu.SemaphoreType.DMA((6,)), pltpu.SemaphoreType.DMA((6,))]
         + gather_scratch(count, half),
         compiler_params=pltpu.CompilerParams(
             collective_id=number, has_side_effects=True, vmem_limit_bytes=VMEM_BYTES
         ),
+        cost_estimate=taking(120),
         name=f"attention{number}",
-    )(q_rows, k_rows, v_rows, *pieces)
+    )(q_rows, k_rows, v_rows, *blocks)
 
 
 def backward_kernel(half, layouts, orders, heads, *refs):
@@ -915,7 +1030,7 @@
     def quarter(index):
         return pl.ds(index * rows, rows)
 
-    split = 2 * len(actions) // 5
+    split = 2 * count
     run_heads(
         heads,
         lambda head: attend_back_head(
@@ -964,7 +1079,7 @@
     got(1, wide_got.at[pl.ds(2, 2)])
     slim[1] = (dv[quarter(2)] + wide_got[3].astype(jnp.float32)).astype(jnp.bfloat16)
     send(3, slim.at[1], slim_got.at[1], along)
-    for action in actions[split + 2 : -2 * count]:
+    for action in actions[split + 2 : -count]:
         action()
     got(2, slim_got.at[0])
     total = dk[quarter(0)] + wide_got[0].astype(jnp.float32) + slim_got[0].astype(jnp.float32)
@@ -972,7 +1087,7 @@
     got(3, slim_got.at[1])
     total = dv[quarter(0)] + wide_got[2].astype(jnp.float32) + slim_got[1].astype(jnp.float32)
     dv_out[own] = total.astype(jnp.bfloat16)
-    for action in actions[-2 * count :]:
+    for action in actions[-count:]:
         action()
     for copy in sent:
         copy.wait_send()
@@ -989,7 +1104,7 @@
     low_rows = jax.ShapeDtypeStruct((total, model_width), jnp.bfloat16)
     return pl.pallas_call(
         functools.partial(backward_kernel, half, layouts, orders, heads),
-        out_shape=[low_rows] * 3 + scatter_outs(layouts, rows, columns),
+        out_shape=[low_rows] * 3 + scatter_outs(count, half, rows, columns),
         in_specs=[vmem] * 7 + [hbm] * count,
         out_specs=[vmem] * (3 + count),
         scratch_shapes=[
@@ -1007,6 +1122,7 @@
         compiler_params=pltpu.CompilerParams(
             collective_id=number, has_side_effects=True, vmem_limit_bytes=VMEM_BYTES
         ),
+        cost_estimate=taking(150),
         name=f"attention{number}",
     )(*rows_in, keys, values, *gradients)
 
@@ -1028,12 +1144,12 @@
 
 
 def spread(per_slot, short_count, len_short, quarter_rows):
-    width = per_slot.shape[1]
-    short_part = jnp.broadcast_to(
-        per_slot[:short_count, None, :], (short_count, len_short, width)
-    ).reshape(short_count * len_short, width)
-    long_part = jnp.broadcast_to(per_slot[short_count:], (quarter_rows, width))
-    return jnp.concatenate([short_part, long_part], 0)
+    short_rows = short_count * len_short
+    row = lax.broadcasted_iota(jnp.int32, (short_rows + quarter_rows, 1), 0)
+    result = per_slot[short_count][None]
+    for slot in range(short_count):
+        result = jnp.where(row < (short_count - slot) * len_short, per_slot[short_count - 1 - slot][None], result)
+    return result
 
 
 def slot_sum(values, short_count, len_short):
@@ -1110,6 +1226,10 @@
     half = fsdp_count // 2
     shard_rows = w_qkv.shape[0]
     unit_rows = w_fc2.shape[0] // 4
+    mixed_shard = jnp.concatenate([w_qkv, w_proj], 1)
+    attention_piece = lax.dynamic_slice_in_dim(mixed_shard, role * model_width, model_width, 1)
+    fc1_piece = lax.dynamic_slice_in_dim(w_fc1, role * model_width, model_width, 1)
+    fc2_piece = lax.dynamic_slice_in_dim(w_fc2, role * unit_rows, unit_rows, 0)
     short_act = low(jax.nn.silu(short_cond))
     long_act = low(jax.nn.silu(long_cond))
     message = exchange(packed([short_act, b_proj, b_fc1, b_fc2], 16), "fsdp", False, 0)
@@ -1141,12 +1261,11 @@
         [partial[:fsdp_count], jnp.repeat(partial[fsdp_count:], SPLIT, axis=0)], 1
     ).reshape(fsdp_count, -1)
     for_device = low(jnp.pad(for_device, ((0, 0), (0, -for_device.shape[1] % 2048))))
-    mixed_shard = jnp.concatenate([w_qkv, w_proj], 1)
-    attention_piece = lax.dynamic_slice_in_dim(mixed_shard, role * model_width, model_width, 1)
-    attention_full, shares = gather(
-        [attention_piece],
-        (BY_ROLE,),
-        ((True, False),),
+    attention_full, fc1_line, shares = gather(
+        attention_piece,
+        BY_ROLE,
+        (True, False),
+        fc1_piece,
         for_device.reshape(fsdp_count, -1, 128),
         2,
     )
@@ -1177,22 +1296,21 @@
     hidden1 = low(normed1 * (1.0 + scale1) + shift1)
     q_rows, k_rows, v_rows = (low(product(hidden1, attention_full[part])) for part in range(3))
 
-    fc1_piece = lax.dynamic_slice_in_dim(w_fc1, role * model_width, model_width, 1)
-    fc2_piece = lax.dynamic_slice_in_dim(w_fc2, role * unit_rows, unit_rows, 0)
     head_rows, log_rows, keys, values, fc1_full, fc2_full = attention_forward(
         q_rows,
         k_rows,
         v_rows,
-        [fc1_piece, fc2_piece],
+        [fc1_piece, fc1_line, fc2_piece],
         (BY_COLUMN, BY_SHARD),
-        ((True, False), (True, True)),
+        ((True, False), (True, False)),
         head_count,
         quarter_rows,
         3,
     )
-    head_rows = head_rows.reshape(row_count, head_count, head_width)
-    head_gate_rows = spread(head_gate, short_count, len_short, quarter_rows)[:, :, None]
-    attention = low((head_rows * head_gate_rows).reshape(row_count, model_width))
+    head_gate_rows = spread(
+        jnp.repeat(head_gate, head_width, axis=1), short_count, len_short, quarter_rows
+    )
+    attention = low(head_rows * head_gate_rows)
     projected = product(attention, attention_full[3]) + proj_bias
     mixed = x_rows + gate1 * projected
     fc1_full = fc1_full.reshape(model_width, -1)
@@ -1227,16 +1345,15 @@
     d_mixed = gradient + norm_back(d_hidden2 * (1.0 + scale2), normed2, inverse2)
     d_projected = low(d_mixed * gate1)
     slot_gate1 = slot_sum(d_mixed * projected, short_count, len_short)
-    d_attention = product_nt(d_projected, attention_full[3]).reshape(
-        row_count, head_count, head_width
-    )
-    d_head = slot_sum(jnp.sum(d_attention * head_rows, axis=-1), short_count, len_short)
+    d_attention = product_nt(d_projected, attention_full[3])
+    d_head = slot_sum(d_attention * head_rows, short_count, len_short)
+    d_head = jnp.sum(d_head.reshape(slot_count, head_count, head_width), axis=-1)
     d_heads = low(d_attention * head_gate_rows)
     bias_grad = jnp.concatenate(
         [jnp.sum(part, axis=0, dtype=jnp.float32) for part in (d_projected, d_up, d_down)]
     )
-    dq_rows, dk_rows, dv_rows, fc1_sum, fc2_sum = attention_backward(
-        [q_rows, k_rows, v_rows, d_heads.reshape(row_count, model_width), log_rows],
+    dq_rows, dk_rows, dv_rows, fc1_near, fc2_near = attention_backward(
+        [q_rows, k_rows, v_rows, d_heads, log_rows],
         keys,
         values,
         [grad_fc1, grad_fc2],
@@ -1247,8 +1364,6 @@
         model_width,
         4,
     )
-    g_w_fc1 = fc1_sum.astype(jnp.float32)
-    g_w_fc2 = fc2_sum.reshape(-1, model_width).astype(jnp.float32)
     d_hidden1 = (
         product_nt(dq_rows, attention_full[0])
         + product_nt(dk_rows, attention_full[1])
@@ -1275,15 +1390,16 @@
         1,
     )
     message = packed([low(d_conditioned), low(bias_grad), short_act, own_long_act], 16)
-    attention_sum, all_rows = scatter_products(
+    attention_sum, all_rows, fc1_sum, fc2_sum = scatter_products(
         [hidden1, attention],
         [dq_rows, dk_rows, dv_rows, d_projected],
-        (False, False),
+        (True, False),
         message,
+        [fc1_near, fc2_near],
         5,
     )
-    g_w_qkv = attention_sum[:3].transpose(1, 0, 2).reshape(shard_rows, -1).astype(jnp.float32)
-    g_w_proj = attention_sum[3].astype(jnp.float32)
+    g_w_fc1 = fc1_sum.transpose(1, 0, 2).reshape(shard_rows, -1).astype(jnp.float32)
+    g_w_fc2 = fc2_sum.reshape(-1, model_width).astype(jnp.float32)
     all_rows, bias_rows, all_short, all_long = unpacked(
         all_rows, [(2, width), bias_grad.shape, (model_width,), (model_width,)]
     )
@@ -1297,7 +1413,12 @@
         + product_nt(d_items[:, mod_width : mod_width + head_count], w_head_router)
         + product_nt(d_items[:, mod_width + head_count :], w_group_router)
     )
-    d_silu = unpacked(exchange(packed([d_silu], 8), "fsdp", False, 7), [d_silu.shape])[0]
+    gathered = exchange(packed([d_silu], 8), "fsdp", False, 7)
+    gathered, later_sum = lax.optimization_barrier((gathered, attention_sum))
+    attention_grad = four_roles(along_line(attention_sum, later_sum))
+    g_w_qkv = attention_grad[:3].transpose(1, 0, 2).reshape(shard_rows, -1)
+    g_w_proj = attention_grad[3]
+    d_silu = unpacked(gathered, [d_silu.shape])[0]
     d_silu = d_silu.transpose(1, 0, 2).reshape(-1, model_width)
     d_short_cond = lax.dynamic_slice_in_dim(d_silu, fsdp_index, 1, 0) * silu_grad(short_cond)
     d_long_cond = d_silu[fsdp_count:] * silu_grad(long_cond)

time: 775 us -> 699 us (0.902)
  Pallas kernels: 529 us -> 444 us
  waiting for transfers between devices: 0 us -> 14.5 us
    pallas_call x1, Pallas kernels: 173 us -> 128 us  [attention_backward(): pl.pallas_call(functools.partial(backward_kernel, half, layouts, orders,...]
    pallas_call x1, Pallas kernels: 114 us -> 89 us  [scatter_products(): pl.pallas_call(functools.partial(roles_kernel, half, order), out_shape=sc...]
    pallas_call x1, Pallas kernels: 156 us -> 141 us  [attention_forward(): pl.pallas_call(functools.partial(forward_kernel, half, layouts, orders, h...]
    ppermute x0 -> x6, waiting for transfers between devices: none -> 14.5 us  [swap(): lax.ppermute(value, axis, [(source, source ^ mask) for source in range(si...]
    unnamed x165 -> x158, local copies, waits for them, and re-layouts: 16.3 us -> 12.7 us
    reduce_sum x2 -> x3, other arithmetic: 19.1 us -> 15.7 us  [per_device(): jnp.sum(part, axis=0, dtype=jnp.float32)]
  transfers between devices with their start and end apart: 0 -> 6, of which waited for: 0 -> 3; matrix products, arithmetic and copies ran while one was open for 0% -> 3% of each run, Pallas kernels for 0% -> 0%
where the time goes in v5:
time: 699 us; the launch traced here: 694 us
  Pallas kernels  444 us (64%)
  matrix products  122 us (17%)
  other arithmetic  56.6 us (8%)
  local copies, waits for them, and re-layouts  49.7 us (7%)
  waiting for transfers between devices  14.5 us (2%)
    pallas_call x1, Pallas kernels, attention_forward(): pl.pallas_call(functools.partial(forward_kernel, half, layouts, orders, h...  141 us
    pallas_call x1, Pallas kernels, attention_backward(): pl.pallas_call(functools.partial(backward_kernel, half, layouts, orders,...  128 us
    pallas_call x1, Pallas kernels, scatter_products(): pl.pallas_call(functools.partial(roles_kernel, half, order), out_shape=sc...  89 us
    pallas_call x1, Pallas kernels, gather(): pl.pallas_call(functools.partial(gather_kernel, half, layout, order), out...  69.3 us
    dot_general x9, matrix products, product_nt(): lax.dot_general(left, right, (((1,), (1,)), ((), ())), preferred_element_...  47.2 us
    dot_general x9, matrix products, product(): return jnp.dot(left, right, preferred_element_type=jnp.float32)  45.2 us
    dot_general x5, matrix products, product_tn(): lax.dot_general(left, right, (((0,), (0,)), ((), ())), preferred_element_...  29.2 us
    pallas_call x2, Pallas kernels, exchange(): pl.pallas_call(functools.partial(exchange_kernel, axis, size, spread_out)...  17.6 us
  transfers between devices with their start and end apart: 6, of which 3 were waited for; matrix products, arithmetic and copies ran while one was open for 3% of the time, Pallas kernels for 0%

profile of v5, /device:TPU:0, one launch (start us, length us, event | category | flops | bytes accessed | tf_op | source)
XLA Modules:
  0.0 694.1 jit_solution(8835614708825142408)
XLA Ops:
  1.4 1.9 convert_reduce_fusion.4
  3.9 2.1 concatenate.91
  6.6 9.8 %exchange0.1 = bf16[8,16,128]{2,1,0:T(8,128)(2,1)} custom-call(bf16[16,128]{1,0:T(8,128)(2,1)} %pad_bitcast_fusion.3.rows_ref), custom_call_target="tpu_custom_call" | custom-call | bytes 24000000 | tf_op jit(solution)/shard_map/exchange0/pallas_call | solution.py:98
  19.0 2.0 convolution_add_fusion
  23.7 1.9 fusion.37
  25.6 69.3 %gather2.1 = (bf16[4,4,2,144,1152]{4,3,2,1,0:T(8,128)(2,1)}, bf16[4,144,1152]{2,1,0:T(8,128)(2,1)}, bf16[8,112,128]{2,1,0:T(8,128)(2,1)}) custom-call(bf16[144,1152]{1,0:T(8,128)(2,1)} %get-tuple-element.129.refs_0_, bf16[144,1152]{1,0:T(8,128)(2,1)} %get-tuple-element.130.refs_1_.refs_3_, bf16[8,112,128]{2,1,0:T(8,128)(2,1)} %bitcast.160), custom_call_target="tpu_custom_call" | custom-call | tf_op jit(solution)/shard_map/gather2/pallas_call | solution.py:441
  99.0 1.7 fusion.22
  100.8 6.0 fusion.70
  109.6 3.7 convolution_convert_fusion.4.refs_0_
  114.7 2.9 convolution_convert_fusion.3.refs_1_
  117.6 2.9 convolution_convert_fusion.2.refs_2_
  122.1 1.7 constant_dynamic-slice_fusion.4.refs_5_
  123.8 140.6 %attention3.1 = (f32[512,1152]{1,0:T(8,128)}, f32[512,128]{1,0:T(8,128)}, bf16[1024,1152]{1,0:T(8,128)(2,1)}, bf16[1024,1152]{1,0:T(8,128)(2,1)}, bf16[4,2,144,4...) custom-call(bf16[512,1152]{1,0:T(8,128)(2,1)} %convolution_convert_fusion.4.refs_0_, ...), custom_call_target="tpu_custom_call" | custom-call | bytes 360000000 | tf_op jit(solution)/shard_map/attention3/pallas_call | solution.py:985
  264.5 2.0 fusion.23.refs_1_
  266.5 6.3 fusion.69
  273.6 4.0 fusion.28
  277.7 11.6 %fusion.79 = f32[512,4608]{1,0:T(8,128)} fusion(bf16[512,1152]{1,0:T(8,128)(2,1)} %fusion.28, bf16[1152,4608]{1,0:T(8,128)(2,1)} %bitcast.171), kind=kOutput, calls=%fused_computation.212 | convolution fusion | flops 5435817984 | bytes 21233664 | tf_op jit(solution)/shard_map/dot_general | solution.py:1131
  289.4 2.1 fusion.64
  291.5 16.7 %fusion.8 = (f32[512,4608]{1,0:T(8,128)}, f32[512,4608]{1,0:T(8,128)}) fusion(f32[512,4608]{1,0:T(8,128)} %fusion.79, f32[4608]{0:T(1024)S(1)} %reshape.313, bf16[512,1152]{1,0:T(8,128)(2,1)S(1)} %get-tuple-element.82, bf16[4608,1152]{1,0:T(8,128)(2,1)} %bitcast.173), kind=kOutput, calls=%fused_computation.31 | convolution fusion | flops 5459410944 | bytes 40126464 | tf_op jit(solution)/shard_map/dot_general | solution.py:1141
  308.2 4.3 slice_reduce_fusion.1
  314.2 14.6 %convolution_convert_fusion = bf16[4608,1152]{1,0:T(8,128)(2,1)} fusion(bf16[512,1152]{1,0:T(8,128)(2,1)} %copy-done.35, f32[4608]{0:T(1024)S(1)} %broadcast_bitcast_fusion, f32[4608]{0:T(1024)S(1)} %broadcast_bitcast_fusion.1, pred[512]{0:T(512)(128)(4,1)S(1)} %copy-done.59, f32[512,4608]{1,0:T(8,128)} %fusion.79, f32[4608]{0:T(1024)S(1)} %reshape.313), kind=kOutput, calls=%fused_computation | convolution fusion | flops 5469437952 | bytes 21289472 | tf_op jit(solution)/shard_map/dot_general | solution.py:1135
  328.8 14.7 %convolution_add_fusion.1 = f32[512,1152]{1,0:T(8,128)} fusion(bf16[4608,1152]{1,0:T(8,128)(2,1)} %bitcast.174, f32[1152]{0:T(1024)S(1)} %reshape.314, f32[4608]{0:T(1024)S(1)} %broadcast_bitcast_fusion, f32[4608]{0:T(1024)S(1)} %broadcast_bitcast_fusion.1, pred[512]{0:T(512)(128)(4,1)S(1)} %copy-done.59, f32[512,4608]{1,0:T(8,128)} %fusion.79, ...), kind=kOutput, calls=%fused_computation.27 | convolution fusion | flops 5464719360 | bytes 22473728 | tf_op jit(solution)/shard_map/dot_general | solution.py:1131
  343.6 9.0 %fusion.66 = (bf16[4608]{0:T(1024)(128)(2,1)S(1)}, bf16[512,4608]{1,0:T(8,128)(2,1)}) fusion(f32[512,4608]{1,0:T(8,128)S(1)} %bitcast.141, f32[4608]{0:T(1024)S(1)} %reshape.313, f32[512,4608]{1,0:T(8,128)S(1)} %bitcast.143, f32[4608]{0:T(1024)S(1)} %broadcast_bitcast_fusion, f32[4608]{0:T(1024)S(1)} %broadcast_bitcast_fusion.1, pred[512]{0:T(512)(128)(4,1)S(1)} %copy-done.59), kind=kLoop, calls=%fused_computation.200 | loop fusion | flops 56618496 | bytes 23657984 | tf_op jit(solution)/shard_map/reduce_sum | solution.py:1353
  352.6 10.4 %convolution_convert_fusion.1 = bf16[1152,4608]{1,0:T(8,128)(2,1)} fusion(bf16[512,1152]{1,0:T(8,128)(2,1)S(1)} %copy-done.34, bf16[512,4608]{1,0:T(8,128)(2,1)} %get-tuple-element.84), kind=kOutput, calls=%fused_computation.1 | convolution fusion | flops 5441126400 | bytes 16515072 | tf_op jit(solution)/shard_map/dot_general | solution.py:1135
  362.9 15.5 %fusion.59 = (f32[512]{0:T(512)S(1)}, f32[512]{0:T(512)S(1)}, bf16[512,1152]{1,0:T(8,128)(2,1)}, f32[512,1152]{1,0:T(8,128)}, f32[512,1152]{1,0:T(8,128)}, /*index=5*/f32[512,1152]{1,0:T(8,128)}) fusion(f32[512,6912]{1,0:T(8,128)} %copy-done.1, f32[512]{0:T(512)S(1)} %add_rsqrt_fusion, f32[512,1152]{1,0:T(8,128)S(1)} %get-tuple-element.89, ...), kind=kOutput, calls=%fused_computation.197 | convolution fusion | flops 5446433792 | bytes 34220032 | tf_op jit(solution)/shard_map/dot_general | solution.py:1141
  378.4 2.5 slice_reduce_fusion.9
  381.0 4.6 fusion.68
  385.6 3.8 fusion.71
  389.4 127.9 %attention4.1 = (bf16[512,1152]{1,0:T(8,128)(2,1)}, bf16[512,1152]{1,0:T(8,128)(2,1)}, bf16[512,1152]{1,0:T(8,128)(2,1)}, bf16[4,144,1152]{2,1,0:T(8,128)(2,1)}, bf16[4,144,1152]{2,1,0:T(8,128)(2,1)}) custom-call(bf16[512,1152]{1,0:T(8,128)(2,1)} %convolution_convert_fusion.4.refs_0_, bf16[512,1152]{1,0:T(8,128)(2,1)} %convolution_convert_fusion.3.refs_1_, ...), custom_call_target="tpu_custom_call" | custom-call | bytes 450000000 | tf_op jit(solution)/shard_map/attention4/pallas_call | solution.py:1105
  517.3 4.1 fusion.80
  521.5 1.9 convolution_add_fusion.3
  523.9 4.2 fusion.60
  529.8 3.6 fusion.11
  539.2 89.0 %scatter5.1 = (bf16[4,144,1152]{2,1,0:T(8,128)(2,1)}, bf16[4,8,192,128]{3,2,1,0:T(8,128)(2,1)}, bf16[4,144,1152]{2,1,0:T(8,128)(2,1)}, bf16[4,144,1152]{2,1,0:T(8,128)(2,1)}) custom-call(bf16[512,1152]{1,0:T(8,128)(2,1)} %copy-done.14, bf16[512,1152]{1,0:T(8,128)(2,1)} %copy-done.15, bf16[512,1152]{1,0:T(8,128)(2,1)} %get-tuple-element.46.refs_2_, ...), custom_call_target="tpu_custom_call" | custom-call | bytes 270000000 | tf_op jit(solution)/shard_map/scatter5/pallas_call | solution.py:785
  628.3 2.1 reshape.302
  637.1 7.8 %exchange7.1 = f32[8,16,128]{2,1,0:T(8,128)} custom-call(f32[16,128]{1,0:T(8,128)} %pad_bitcast_fusion.2.rows_ref), custom_call_target="tpu_custom_call" | custom-call | bytes 24000000 | tf_op jit(solution)/shard_map/exchange7/pallas_call | solution.py:98
  645.0 1.9 dynamic-slice_bitcast_fusion.1
  646.9 2.7 collective-permute-start.2
  650.7 1.7 collective-permute-start
  653.5 1.8 fusion.72
  656.6 2.3 fusion.74
  663.9 1.5 convert_bitcast_fusion
  665.4 1.8 copy.68
  667.2 1.8 bitcast_convert_fusion
  671.8 6.0 collective-permute-done.1
  680.1 2.6 fusion.35
  682.8 7.0 %collective-permute-done.4 = bf16[144,1152]{1,0:T(8,128)(2,1)S(1)} collective-permute-done((bf16[144,1152]{1,0:T(8,128)(2,1)S(1)}, bf16[144,1152]{1,0:T(8,128)(2,1)S(1)}, u32[]{:S(2)}, u32[]{:S(2)}) %collective-permute-start.4) | collective-permute-done | bytes 331808 | tf_op jit(solution)/shard_map/ppermute | solution.py:632
  689.8 1.5 collective-permute-done.5
  (295 shorter events, 49.9 us)
Async XLA Ops:
  0.7 17.5 %copy-start = (bf16[144,36]{0,1:T(8,128)(2,1)S(1)}, bf16[144,36]{0,1:T(8,128)(2,1)}, u32[]{:S(2)}) copy-start(bf16[144,36]{0,1:T(8,128)(2,1)} %param.36) | copy-start | bytes 31108
  19.0 4.7 copy-start.38
  19.0 4.7 copy-start.39
  96.0 24.5 %copy-start.40 = (f32[2,6964]{1,0:T(2,128)}, f32[2,6964]{1,0:T(2,128)S(1)}, u32[]{:S(2)}) copy-start(f32[2,6964]{1,0:T(2,128)S(1)} %reshape.294) | copy-start | bytes 167140
  99.0 9.3 %copy-start.44 = (f32[512]{0:T(512)}, f32[512]{0:T(512)S(1)}, u32[]{:S(2)}) copy-start(f32[512]{0:T(512)S(1)} %broadcast_multiply_fusion.5) | copy-start | bytes 6148
  100.8 7.6 %copy-start.50 = (f32[512]{0:T(512)}, f32[512]{0:T(512)S(1)}, u32[]{:S(2)}) copy-start(f32[512]{0:T(512)S(1)} %add_rsqrt_fusion.1) | copy-start | bytes 6148
  100.8 6.0 copy-start.58
  106.8 2.8 copy-start.22
  106.8 7.9 %copy-start.20 = (bf16[1,4,2,144,1152]{4,3,2,1,0:T(8,128)(2,1)}, bf16[1,4,2,144,1152]{4,3,2,1,0:T(8,128)(2,1)S(1)}, u32[]{:S(2)}) copy-start(bf16[1,4,2,144,1152]{4,3,2,1,0:T(8,128)(2,1)S(1)} %get-tuple-element.95) | copy-start | bytes 7962628
  106.8 10.8 %copy-start.18 = (bf16[1,4,2,144,1152]{4,3,2,1,0:T(8,128)(2,1)}, bf16[1,4,2,144,1152]{4,3,2,1,0:T(8,128)(2,1)S(1)}, u32[]{:S(2)}) copy-start(bf16[1,4,2,144,1152]{4,3,2,1,0:T(8,128)(2,1)S(1)} %get-tuple-element.94) | copy-start | bytes 7962628
  108.9 5.8 copy-start.1
  109.5 8.1 %copy-start.14 = (bf16[512,1152]{1,0:T(8,128)(2,1)}, bf16[512,1152]{1,0:T(8,128)(2,1)S(1)}, u32[]{:S(2)}) copy-start(bf16[512,1152]{1,0:T(8,128)(2,1)S(1)} %fusion.16.refs_0_) | copy-start | bytes 3538948
  117.6 2.9 copy-start.68
  117.6 2.9 copy-start.61
  266.5 6.3 copy-start.15
  277.7 11.6 %copy-start.65 = (s32[256]{0:T(256)S(1)}, s32[256]{0:T(256)}, u32[]{:S(2)}) copy-start(s32[256]{0:T(256)} %param.32) | copy-start | bytes 3076
  277.7 11.6 %copy-start.66 = (s32[1,256]{1,0:T(1,128)S(1)}, s32[1,256]{1,0:T(1,128)}, u32[]{:S(2)}) copy-start(s32[1,256]{1,0:T(1,128)} %param.31) | copy-start | bytes 3076
  277.7 11.7 %copy-start.24 = (bf16[256,1152]{1,0:T(8,128)(2,1)S(1)}, bf16[256,1152]{1,0:T(8,128)(2,1)}, u32[]{:S(2)}) copy-start(bf16[256,1152]{1,0:T(8,128)(2,1)} %param.45) | copy-start | bytes 1769476
  277.7 11.7 %copy-start.25 = (bf16[1,256,1152]{2,1,0:T(8,128)(2,1)S(1)}, bf16[1,256,1152]{2,1,0:T(8,128)(2,1)}, u32[]{:S(2)}) copy-start(bf16[1,256,1152]{2,1,0:T(8,128)(2,1)} %param.44) | copy-start | bytes 1769476
  291.5 16.7 %copy-start.35 = (bf16[512,1152]{1,0:T(8,128)(2,1)}, bf16[512,1152]{1,0:T(8,128)(2,1)S(1)}, u32[]{:S(2)}) copy-start(bf16[512,1152]{1,0:T(8,128)(2,1)S(1)} %get-tuple-element.82) | copy-start | bytes 3538948
  308.2 4.6 copy-start.69
  308.2 4.6 copy-start.67
  308.2 6.0 copy-start.59
  314.2 29.3 %slice-start = ((s8[9437184]{0:T(1024)(128)(4,1)}), s8[1048576]{0:T(1024)(128)(4,1)S(1)}, s32[]{:S(2)}) async-start(s8[9437184]{0:T(1024)(128)(4,1)} %bitcast.140), calls=%async_computation | async-start | bytes 2097152
  314.2 29.3 %slice-start.1 = ((s8[9437184]{0:T(1024)(128)(4,1)}), s8[4194304]{0:T(1024)(128)(4,1)S(1)}, s32[]{:S(2)}) async-start(s8[9437184]{0:T(1024)(128)(4,1)} %bitcast.140), calls=%async_computation.1 | async-start | bytes 8388608
  314.2 29.3 %slice-start.3 = ((s8[9437184]{0:T(1024)(128)(4,1)}), s8[4194304]{0:T(1024)(128)(4,1)S(1)}, s32[]{:S(2)}) async-start(s8[9437184]{0:T(1024)(128)(4,1)} %bitcast.142), calls=%async_computation.3 | async-start | bytes 8388608
  314.2 29.3 %slice-start.4 = ((s8[9437184]{0:T(1024)(128)(4,1)}), s8[4194304]{0:T(1024)(128)(4,1)S(1)}, s32[]{:S(2)}) async-start(s8[9437184]{0:T(1024)(128)(4,1)} %bitcast.142), calls=%async_computation.4 | async-start | bytes 8388608
  328.8 14.8 %slice-start.2 = ((s8[9437184]{0:T(1024)(128)(4,1)}), s8[4194304]{0:T(1024)(128)(4,1)S(1)}, s32[]{:S(2)}) async-start(s8[9437184]{0:T(1024)(128)(4,1)} %bitcast.140), calls=%async_computation.2 | async-start | bytes 8388608
  328.8 14.8 %slice-start.5 = ((s8[9437184]{0:T(1024)(128)(4,1)}), s8[1048576]{0:T(1024)(128)(4,1)S(1)}, s32[]{:S(2)}) async-start(s8[9437184]{0:T(1024)(128)(4,1)} %bitcast.142), calls=%async_computation.5 | async-start | bytes 2097152
  343.6 9.0 %copy-start.34 = (bf16[512,1152]{1,0:T(8,128)(2,1)S(1)}, bf16[512,1152]{1,0:T(8,128)(2,1)}, u32[]{:S(2)}) copy-start(bf16[512,1152]{1,0:T(8,128)(2,1)} %fusion.28) | copy-start | bytes 3538948
  380.9 4.6 copy-start.23
  380.9 4.6 copy-start.30
  380.9 4.6 copy-start.46
  380.9 4.6 copy-start.47
  385.6 3.8 copy-start.12
  517.3 4.2 copy-start.21
  517.3 4.2 copy-start.32
  523.9 4.4 copy-start.26
  645.0 10.2 %copy-start.17 = (bf16[4,8,1,6964]{3,1,2,0:T(8,128)(2,1)S(1)}, bf16[4,8,1,6964]{3,1,2,0:T(8,128)(2,1)}, u32[]{:S(2)}) copy-start(bf16[4,8,1,6964]{3,1,2,0:T(8,128)(2,1)} %copy-done.16) | copy-start | bytes 1337092
  645.0 10.2 %copy-start.37 = (bf16[4,2,6964]{2,1,0:T(2,128)(2,1)S(1)}, bf16[4,2,6964]{2,1,0:T(2,128)(2,1)}, u32[]{:S(2)}) copy-start(bf16[4,2,6964]{2,1,0:T(2,128)(2,1)} %copy-done.36) | copy-start | bytes 334276
  646.9 24.9 %collective-permute-start.2 = (bf16[144,1152]{1,0:T(8,128)(2,1)}, bf16[144,1152]{1,0:T(8,128)(2,1)}, u32[]{:S(2)}, u32[]{:S(2)}) collective-permute-start(bf16[144,1152]{1,0:T(8,128)(2,1)} %get-tuple-element.107), channel_id=1, source_target_pairs={{0,6},{1,7},{2,4},{3,5},{4,2},{5,3},{6,0},{7,1},{8,14},{9,15},{10,... | collective-permute-start | bytes 995336 | tf_op jit(solution)/shard_map/ppermute | solution.py:632
  649.6 28.2 %collective-permute-start.1 = (bf16[144,1152]{1,0:T(8,128)(2,1)S(1)}, bf16[144,1152]{1,0:T(8,128)(2,1)}, u32[]{:S(2)}, u32[]{:S(2)}) collective-permute-start(bf16[144,1152]{1,0:T(8,128)(2,1)S(1)} %get-tuple-element.106), channel_id=1, source_target_pairs={{0,4},{1,5},{2,6},{3,7},{4,0},{5,1},{6,2},{7,3},{8,12},{9,13},{10,... | collective-permute-start | bytes 995336 | tf_op jit(solution)/shard_map/ppermute | solution.py:632
  650.7 27.1 %collective-permute-start = (bf16[144,1152]{1,0:T(8,128)(2,1)S(1)}, bf16[144,1152]{1,0:T(8,128)(2,1)}, u32[]{:S(2)}, u32[]{:S(2)}) collective-permute-start(bf16[144,1152]{1,0:T(8,128)(2,1)S(1)} %dynamic-slice_bitcast_fusion.2), channel_id=1, source_target_pairs={{0,2},{1,3},{2,0},{3,1},{4,6},{5,7},{6,4},{7,5},{8,10},{9,11},{10,... | collective-permute-start | bytes 995336 | tf_op jit(solution)/shard_map/ppermute | solution.py:632
  653.4 5.5 copy-start.13
  656.6 3.7 copy-start.41
  679.4 10.3 %collective-permute-start.3 = (bf16[144,1152]{1,0:T(8,128)(2,1)S(1)}, bf16[144,1152]{1,0:T(8,128)(2,1)S(1)}, u32[]{:S(2)}, u32[]{:S(2)}) collective-permute-start(bf16[144,1152]{1,0:T(8,128)(2,1)S(1)} %get-tuple-element.80), channel_id=1, source_target_pairs={{0,8},{8,0},{16,24},{24,16},{1,9},{9,1},{17,25},{25,17},{2,10},{10... | collective-permute-start | bytes 995336 | tf_op jit(solution)/shard_map/ppermute | solution.py:632
  679.5 10.2 %collective-permute-start.4 = (bf16[144,1152]{1,0:T(8,128)(2,1)S(1)}, bf16[144,1152]{1,0:T(8,128)(2,1)S(1)}, u32[]{:S(2)}, u32[]{:S(2)}) collective-permute-start(bf16[144,1152]{1,0:T(8,128)(2,1)S(1)} %get-tuple-element.80), channel_id=1, source_target_pairs={{0,16},{8,24},{16,0},{24,8},{1,17},{9,25},{17,1},{25,9},{2,18},{10... | collective-permute-start | bytes 995336 | tf_op jit(solution)/shard_map/ppermute | solution.py:632
  689.7 1.6 collective-permute-start.5
  (34 other events, 64.1 us)

commit v6 on v5

--- a/solution.py
+++ b/solution.py
@@ -881,15 +881,41 @@
     lax.fori_loop(0, head_count, step, 0)
 
 
+def mix_rows(
+    x_ref, start, length, first_slot, o_ref, slot_values, weights, attention, projected, mixed, hidden
+):
+    size = 128 if length % 128 == 0 else length
+
+    def step(index, carry):
+        own = pl.ds(pl.multiple_of(index * size, size), size)
+        place = pl.ds(pl.multiple_of(start + index * size, size), size)
+        values = slot_values[first_slot + index * size // length]
+        head_gate, gate1, shift2, scale2, bias = (values[row : row + 1] for row in range(5))
+        gated = (o_ref[place] * head_gate).astype(jnp.bfloat16)
+        attention[place] = gated
+        result = jnp.dot(gated, weights[...], preferred_element_type=jnp.float32) + bias
+        projected[place] = result
+        total = x_ref[own].astype(jnp.float32) + gate1 * result
+        mixed[place] = total
+        centred = total - jnp.mean(total, axis=-1, keepdims=True)
+        variance = jnp.mean(centred * centred, axis=-1, keepdims=True)
+        normed = centred * lax.rsqrt(variance + epsilon)
+        hidden[place] = (normed * (1.0 + scale2) + shift2).astype(jnp.bfloat16)
+        return carry
+
+    lax.fori_loop(0, x_ref.shape[0] // size, step, 0)
+
+
 def forward_kernel(half, layouts, orders, heads, *refs):
     count = len(layouts)
     q_ref, k_ref, v_ref = refs[:3]
     fc1_piece, fc1_line, fc2_piece = refs[3:6]
     lines = [[fc1_piece] + [fc1_line.at[step] for step in range(1, half)], [fc2_piece]]
-    refs = refs[6:]
-    o_ref, log_ref, keys, values = refs[:4]
-    outs = refs[4 : 4 + count]
-    send_sem, recv_sem = refs[4 + count : 6 + count]
+    x_short, x_long, slot_values, weights = refs[6:10]
+    refs = refs[10:]
+    o_ref, log_ref, keys, values, *mixing = refs[:8]
+    outs = refs[8 : 8 + count]
+    send_sem, recv_sem, projection, projection_sem = refs[8 + count : 12 + count]
     at = Place(half)
     width = q_ref.shape[1] // heads
     rows = keys.shape[0] // 4
@@ -915,7 +941,9 @@
     send(1, v_ref.at[own], quarter(values, 2), along)
     send(2, v_ref.at[own], quarter(values, 1), beside)
     send(3, k_ref.at[own], quarter(keys, 2), along)
-    pairs, local = gather_start(at, layouts, orders, lines, outs, *refs[6 + count :])
+    pairs, local = gather_start(at, layouts, orders, lines, outs, *refs[12 + count :])
+    load = pltpu.make_async_copy(weights.at[3], projection, projection_sem)
+    load.start()
     actions = gather_actions(pairs, local)
     beside_first, settle, second, line_steps = count, 2 * count, 2 * count + 1, 2 * count + 2
     late = line_steps + half - 1
@@ -960,15 +988,21 @@
         lambda head: attend_head(
             head, width, q_ref.at[own], keys, values, o_ref.at[own], log_ref.at[own]
         ),
-        actions[late:-count],
-    )
+        actions[late : late + 2],
+    )
+    for action in actions[late + 2 : -count]:
+        action()
+    load.wait()
+    slots = slot_values.shape[0]
+    mix_rows(x_short, 0, short // (slots - 1), 0, o_ref, slot_values, projection, *mixing)
+    mix_rows(x_long, short, rows, slots - 1, o_ref, slot_values, projection, *mixing)
     for action in actions[-count:]:
         action()
     for copy in sent:
         copy.wait_send()
 
 
-def attention_forward(q_rows, k_rows, v_rows, blocks, layouts, orders, heads, rows, number):
+def attention_forward(q_rows, k_rows, v_rows, blocks, mixing, layouts, orders, heads, rows, number):
     half = lax.axis_size("fsdp") // 2
     count = len(layouts)
     vmem, hbm = pl.BlockSpec(memory_space=pltpu.VMEM), pl.BlockSpec(memory_space=pl.ANY)
@@ -978,6 +1012,10 @@
         jax.ShapeDtypeStruct((total, 128), jnp.float32),
         jax.ShapeDtypeStruct((4 * rows, columns), jnp.bfloat16),
         jax.ShapeDtypeStruct((4 * rows, columns), jnp.bfloat16),
+        jax.ShapeDtypeStruct((total, columns), jnp.bfloat16),
+        jax.ShapeDtypeStruct((total, columns), jnp.float32),
+        jax.ShapeDtypeStruct((total, columns), jnp.float32),
+        jax.ShapeDtypeStruct((total, columns), jnp.bfloat16),
     ] + [
         jax.ShapeDtypeStruct(whole_shape(layout, half, *blocks[0].shape), blocks[0].dtype)
         for layout in layouts
@@ -985,16 +1023,21 @@
     return pl.pallas_call(
         functools.partial(forward_kernel, half, layouts, orders, heads),
         out_shape=outs,
-        in_specs=[vmem] * (3 + len(blocks)),
-        out_specs=[vmem] * 4 + [hbm] * count,
-        scratch_shapes=[pltpu.SemaphoreType.DMA((6,)), pltpu.SemaphoreType.DMA((6,))]
+        in_specs=[vmem] * (6 + len(blocks)) + [hbm],
+        out_specs=[vmem] * 8 + [hbm] * count,
+        scratch_shapes=[
+            pltpu.SemaphoreType.DMA((6,)),
+            pltpu.SemaphoreType.DMA((6,)),
+            pltpu.VMEM((columns, columns), jnp.bfloat16),
+            pltpu.SemaphoreType.DMA,
+        ]
         + gather_scratch(count, half),
         compiler_params=pltpu.CompilerParams(
             collective_id=number, has_side_effects=True, vmem_limit_bytes=VMEM_BYTES
         ),
         cost_estimate=taking(120),
         name=f"attention{number}",
-    )(q_rows, k_rows, v_rows, *blocks)
+    )(q_rows, k_rows, v_rows, *blocks, *mixing)
 
 
 def backward_kernel(half, layouts, orders, heads, *refs):
@@ -1296,27 +1339,46 @@
     hidden1 = low(normed1 * (1.0 + scale1) + shift1)
     q_rows, k_rows, v_rows = (low(product(hidden1, attention_full[part])) for part in range(3))
 
-    head_rows, log_rows, keys, values, fc1_full, fc2_full = attention_forward(
+    head_columns = jnp.repeat(head_gate, head_width, axis=1)
+    pieces = modulation.reshape(slot_count, 6, model_width)
+    slot_values = jnp.stack(
+        [
+            head_columns,
+            pieces[:, 2],
+            pieces[:, 3],
+            pieces[:, 4],
+            jnp.broadcast_to(proj_bias, (slot_count, model_width)),
+        ],
+        1,
+    )
+    slot_values = jnp.pad(slot_values, ((0, 0), (0, 3), (0, 0)))
+    (
+        head_rows,
+        log_rows,
+        keys,
+        values,
+        attention,
+        projected,
+        mixed,
+        hidden2,
+        fc1_full,
+        fc2_full,
+    ) = attention_forward(
         q_rows,
         k_rows,
         v_rows,
         [fc1_piece, fc1_line, fc2_piece],
+        [x_short.reshape(short_rows, model_width), x_long, slot_values, attention_full],
         (BY_COLUMN, BY_SHARD),
         ((True, False), (True, False)),
         head_count,
         quarter_rows,
         3,
     )
-    head_gate_rows = spread(
-        jnp.repeat(head_gate, head_width, axis=1), short_count, len_short, quarter_rows
-    )
-    attention = low(head_rows * head_gate_rows)
-    projected = product(attention, attention_full[3]) + proj_bias
-    mixed = x_rows + gate1 * projected
+    head_gate_rows = spread(head_columns, short_count, len_short, quarter_rows)
     fc1_full = fc1_full.reshape(model_width, -1)
     fc2_full = fc2_full.reshape(-1, model_width)
     normed2, inverse2 = norm_parts(mixed)
-    hidden2 = low(normed2 * (1.0 + scale2) + shift2)
     channel_gate = spread(
         jnp.repeat(group_gate, CHAN, axis=1), short_count, len_short, quarter_rows
     )

time: 699 us -> 691 us (0.989)
  matrix products: 122 us -> 113 us
    dot_general x9 -> x8, matrix products: 45.2 us -> 39.1 us  [product(): return jnp.dot(left, right, preferred_element_type=jnp.float32)]
  transfers between devices with their start and end apart: 6 -> 6, of which waited for: 3 -> 4; matrix products, arithmetic and copies ran while one was open for 3% -> 3% of each run, Pallas kernels for 0% -> 0%
where the time goes in v6:
time: 691 us; the launch traced here: 683 us
  Pallas kernels  444 us (64%)
  matrix products  113 us (16%)
  other arithmetic  58.3 us (8%)
  local copies, waits for them, and re-layouts  46.4 us (7%)
  waiting for transfers between devices  15 us (2%)
    pallas_call x1, Pallas kernels, attention_forward(): pl.pallas_call(functools.partial(forward_kernel, half, layouts, orders, h...  140 us
    pallas_call x1, Pallas kernels, attention_backward(): pl.pallas_call(functools.partial(backward_kernel, half, layouts, orders,...  128 us
    pallas_call x1, Pallas kernels, scatter_products(): pl.pallas_call(functools.partial(roles_kernel, half, order), out_shape=sc...  89.2 us
    pallas_call x1, Pallas kernels, gather(): pl.pallas_call(functools.partial(gather_kernel, half, layout, order), out...  69.2 us
    dot_general x9, matrix products, product_nt(): lax.dot_general(left, right, (((1,), (1,)), ((), ())), preferred_element_...  45.5 us
    dot_general x8, matrix products, product(): return jnp.dot(left, right, preferred_element_type=jnp.float32)  39.1 us
    dot_general x5, matrix products, product_tn(): lax.dot_general(left, right, (((0,), (0,)), ((), ())), preferred_element_...  28.3 us
    reduce_sum x3, other arithmetic, per_device(): jnp.sum(part, axis=0, dtype=jnp.float32)  19.7 us
  transfers between devices with their start and end apart: 6, of which 4 were waited for; matrix products, arithmetic and copies ran while one was open for 3% of the time, Pallas kernels for 0%

profile of v6, /device:TPU:0, one launch (start us, length us, event | category | flops | bytes accessed | tf_op | source)
XLA Modules:
  0.0 683.4 jit_solution(1337512918788632790)
XLA Ops:
  1.4 1.9 convert_reduce_fusion.4
  3.9 2.1 concatenate.91
  6.6 9.8 %exchange0.1 = bf16[8,16,128]{2,1,0:T(8,128)(2,1)} custom-call(bf16[16,128]{1,0:T(8,128)(2,1)} %pad_bitcast_fusion.3.rows_ref), custom_call_target="tpu_custom_call" | custom-call | bytes 24000000 | tf_op jit(solution)/shard_map/exchange0/pallas_call | solution.py:98
  19.6 2.0 convolution_add_fusion
  23.1 1.9 fusion.35
  25.0 69.2 %gather2.1 = (bf16[4,4,2,144,1152]{4,3,2,1,0:T(8,128)(2,1)}, bf16[4,144,1152]{2,1,0:T(8,128)(2,1)}, bf16[8,112,128]{2,1,0:T(8,128)(2,1)}) custom-call(bf16[144,1152]{1,0:T(8,128)(2,1)} %get-tuple-element.134.refs_0_, bf16[144,1152]{1,0:T(8,128)(2,1)} %get-tuple-element.135.refs_1_.refs_3_, bf16[8,112,128]{2,1,0:T(8,128)(2,1)} %bitcast.157), custom_call_target="tpu_custom_call" | custom-call | tf_op jit(solution)/shard_map/gather2/pallas_call | solution.py:441
  97.6 1.5 convert_reduce_fusion
  99.1 1.7 fusion.22
  100.8 6.1 fusion.68
  107.0 1.5 broadcast_select_fusion
  109.7 3.6 convolution_convert_fusion.2.refs_2_
  113.4 1.5 copy-done.1
  114.9 2.9 convolution_convert_fusion.3.refs_1_
  117.8 2.9 convolution_convert_fusion.4.refs_0_
  121.7 1.7 constant_dynamic-slice_fusion.4.refs_5_
  124.1 140.3 %attention3.1 = (f32[512,1152]{1,0:T(8,128)}, f32[512,128]{1,0:T(8,128)}, bf16[1024,1152]{1,0:T(8,128)(2,1)}, bf16[1024,1152]{1,0:T(8,128)(2,1)}, bf16[512,1152]...) custom-call(bf16[512,1152]{1,0:T(8,128)(2,1)} %convolution_convert_f, ...), custom_call_target="tpu_custom_call" | custom-call | bytes 360000000 | tf_op jit(solution)/shard_map/attention3/pallas_call | solution.py:1023
  264.4 12.0 %fusion.77 = f32[512,4608]{1,0:T(8,128)} fusion(bf16[512,1152]{1,0:T(8,128)(2,1)} %get-tuple-element.45, bf16[1152,4608]{1,0:T(8,128)(2,1)} %bitcast.168), kind=kOutput, calls=%fused_computation.208 | convolution fusion | flops 5435817984 | bytes 21233664 | tf_op jit(solution)/shard_map/dot_general | solution.py:1174
  276.5 2.7 fusion.62
  279.1 16.0 %fusion.8 = (f32[512,4608]{1,0:T(8,128)}, f32[512,4608]{1,0:T(8,128)}) fusion(f32[512,4608]{1,0:T(8,128)} %fusion.77, f32[4608]{0:T(1024)S(1)} %reshape.316, bf16[512,1152]{1,0:T(8,128)(2,1)S(1)} %get-tuple-element.90, bf16[4608,1152]{1,0:T(8,128)(2,1)} %bitcast.170), kind=kOutput, calls=%fused_computation.25 | convolution fusion | flops 5459410944 | bytes 40126464 | tf_op jit(solution)/shard_map/dot_general | solution.py:1184
  295.1 4.3 slice_reduce_fusion.1
  301.2 13.8 %convolution_convert_fusion = bf16[4608,1152]{1,0:T(8,128)(2,1)} fusion(bf16[512,1152]{1,0:T(8,128)(2,1)S(1)} %get-tuple-element.90, f32[4608]{0:T(1024)S(1)} %broadcast_bitcast_fusion, f32[4608]{0:T(1024)S(1)} %broadcast_bitcast_fusion.1, pred[512]{0:T(512)(128)(4,1)S(1)} %copy-done.55, f32[512,4608]{1,0:T(8,128)} %fusion.77, f32[4608]{0:T(1024)S(1)} %reshape.316), kind=kOutput, calls=%fused_computation | convolution fusion | flops 5469437952 | bytes 21289472 | tf_op jit(solution)/shard_map/dot_general | solution.py:1178
  315.0 12.2 %fusion.64 = (bf16[4608]{0:T(1024)(128)(2,1)}, bf16[512,4608]{1,0:T(8,128)(2,1)}) fusion(f32[512,4608]{1,0:T(8,128)S(1)} %bitcast.141, f32[4608]{0:T(1024)S(1)} %reshape.316, f32[512,4608]{1,0:T(8,128)} %get-tuple-element.131, f32[4608]{0:T(1024)S(1)} %broadcast_bitcast_fusion, f32[4608]{0:T(1024)S(1)} %broadcast_bitcast_fusion.1, ...), kind=kLoop, calls=%fused_computation.197 | loop fusion | flops 56618496 | bytes 23657984 | tf_op jit(solution)/shard_map/reduce_sum | solution.py:1415
  327.3 14.8 %convolution_add_fusion.1 = f32[512,1152]{1,0:T(8,128)} fusion(bf16[4608,1152]{1,0:T(8,128)(2,1)} %bitcast.171, f32[1152]{0:T(1024)S(1)} %reshape.317, f32[4608]{0:T(1024)S(1)} %broadcast_bitcast_fusion, f32[4608]{0:T(1024)S(1)} %broadcast_bitcast_fusion.1, pred[512]{0:T(512)(128)(4,1)S(1)} %copy-done.55, f32[512,4608]{1,0:T(8,128)} %fusion.77, ...), kind=kOutput, calls=%fused_computation.22 | convolution fusion | flops 5464719360 | bytes 22473728 | tf_op jit(solution)/shard_map/dot_general | solution.py:1174
  343.5 10.2 %convolution_convert_fusion.1 = bf16[1152,4608]{1,0:T(8,128)(2,1)} fusion(bf16[512,1152]{1,0:T(8,128)(2,1)S(1)} %copy-done.68, bf16[512,4608]{1,0:T(8,128)(2,1)} %get-tuple-element.92), kind=kOutput, calls=%fused_computation.1 | convolution fusion | flops 5441126400 | bytes 16515072 | tf_op jit(solution)/shard_map/dot_general | solution.py:1178
  353.7 15.5 %fusion.58 = (f32[512]{0:T(512)S(1)}, f32[512]{0:T(512)S(1)}, bf16[512,1152]{1,0:T(8,128)(2,1)}, f32[512,1152]{1,0:T(8,128)}, f32[512,1152]{1,0:T(8,128)}, /*index=5*/f32[512,1152]{1,0:T(8,128)}) fusion(f32[512,6912]{1,0:T(8,128)} %copy-done.1, f32[512]{0:T(512)S(1)} %add_rsqrt_fusion, f32[512,1152]{1,0:T(8,128)S(1)} %copy-done.2, ...), kind=kOutput, calls=%fused_computation.195 | convolution fusion | flops 5446433792 | bytes 34220032 | tf_op jit(solution)/shard_map/dot_general | solution.py:1184
  369.5 1.9 slice_reduce_fusion.9
  371.9 4.8 fusion.66
  376.7 2.9 fusion.69
  381.6 1.8 slice_reduce_fusion.5
  385.9 128.2 %attention4.1 = (bf16[512,1152]{1,0:T(8,128)(2,1)}, bf16[512,1152]{1,0:T(8,128)(2,1)}, bf16[512,1152]{1,0:T(8,128)(2,1)}, bf16[4,144,1152]{2,1,0:T(8,128)(2,1)}, bf16[4,144,1152]{2,1,0:T(8,128)(2,1)}) custom-call(bf16[512,1152]{1,0:T(8,128)(2,1)} %convolution_convert_fusion.4.refs_0_, bf16[512,1152]{1,0:T(8,128)(2,1)} %convolution_convert_fusion.3.refs_1_, ...), custom_call_target="tpu_custom_call" | custom-call | bytes 450000000 | tf_op jit(solution)/shard_map/attention4/pallas_call | solution.py:1148
  514.1 4.1 fusion.78
  518.3 1.9 convolution_add_fusion.3
  520.7 4.2 fusion.57
  525.1 1.5 copy-done.7
  526.6 3.6 fusion.11
  532.2 89.2 %scatter5.1 = (bf16[4,144,1152]{2,1,0:T(8,128)(2,1)}, bf16[4,8,192,128]{3,2,1,0:T(8,128)(2,1)}, bf16[4,144,1152]{2,1,0:T(8,128)(2,1)}, bf16[4,144,1152]{2,1,0:T(8,128)(2,1)}) custom-call(bf16[512,1152]{1,0:T(8,128)(2,1)} %copy-done.13, bf16[512,1152]{1,0:T(8,128)(2,1)} %get-tuple-element.54.refs_1_, bf16[512,1152]{1,0:T(8,128)(2,1)} %get-tuple-element.51.refs_2_, ...), custom_call_target="tpu_custom_call" | custom-call | bytes 270000000 | tf_op jit(solution)/shard_map/scatter5/pallas_call | solution.py:785
  621.3 2.0 reshape.305
  630.7 7.8 %exchange7.1 = f32[8,16,128]{2,1,0:T(8,128)} custom-call(f32[16,128]{1,0:T(8,128)} %pad_bitcast_fusion.2.rows_ref), custom_call_target="tpu_custom_call" | custom-call | bytes 24000000 | tf_op jit(solution)/shard_map/exchange7/pallas_call | solution.py:98
  638.5 2.0 dynamic-slice_bitcast_fusion.1
  640.5 1.6 collective-permute-start.1
  652.1 1.8 copy.68
  653.9 1.8 bitcast_convert_fusion
  660.6 4.7 collective-permute-done.1
  665.3 1.9 collective-permute-done
  667.3 1.5 convert_dynamic-update-slice_fusion.3
  669.5 2.6 fusion.33
  672.2 6.9 %collective-permute-done.4 = bf16[144,1152]{1,0:T(8,128)(2,1)S(1)} collective-permute-done((bf16[144,1152]{1,0:T(8,128)(2,1)S(1)}, bf16[144,1152]{1,0:T(8,128)(2,1)S(1)}, u32[]{:S(2)}, u32[]{:S(2)}) %collective-permute-start.4) | collective-permute-done | bytes 331808 | tf_op jit(solution)/shard_map/ppermute | solution.py:632
  679.2 1.5 collective-permute-done.5
  (295 shorter events, 49.0 us)
Async XLA Ops:
  0.7 18.1 %copy-start = (bf16[144,36]{0,1:T(8,128)(2,1)S(1)}, bf16[144,36]{0,1:T(8,128)(2,1)}, u32[]{:S(2)}) copy-start(bf16[144,36]{0,1:T(8,128)(2,1)} %param.36) | copy-start | bytes 31108
  19.6 3.5 copy-start.31
  19.6 3.5 copy-start.33
  21.8 85.1 %copy-start.54 = (pred[512]{0:T(512)(128)(4,1)}, pred[512]{0:T(512)(128)(4,1)S(1)}, u32[]{:S(2)}) copy-start(pred[512]{0:T(512)(128)(4,1)S(1)} %iota_compare_fusion.1) | copy-start | bytes 1540
  95.3 25.3 %copy-start.32 = (f32[2,6964]{1,0:T(2,128)}, f32[2,6964]{1,0:T(2,128)S(1)}, u32[]{:S(2)}) copy-start(f32[2,6964]{1,0:T(2,128)S(1)} %reshape.295) | copy-start | bytes 167140
  99.1 9.4 %copy-start.40 = (f32[512]{0:T(512)}, f32[512]{0:T(512)S(1)}, u32[]{:S(2)}) copy-start(f32[512]{0:T(512)S(1)} %broadcast_multiply_fusion.5) | copy-start | bytes 6148
  100.8 7.7 %copy-start.44 = (f32[512]{0:T(512)}, f32[512]{0:T(512)S(1)}, u32[]{:S(2)}) copy-start(f32[512]{0:T(512)S(1)} %add_rsqrt_fusion.1) | copy-start | bytes 6148
  107.0 2.8 copy-start.15
  107.0 7.9 %copy-start.17 = (bf16[1,4,2,144,1152]{4,3,2,1,0:T(8,128)(2,1)}, bf16[1,4,2,144,1152]{4,3,2,1,0:T(8,128)(2,1)S(1)}, u32[]{:S(2)}) copy-start(bf16[1,4,2,144,1152]{4,3,2,1,0:T(8,128)(2,1)S(1)} %get-tuple-element.101) | copy-start | bytes 7962628
  107.0 10.8 %copy-start.19 = (bf16[1,4,2,144,1152]{4,3,2,1,0:T(8,128)(2,1)}, bf16[1,4,2,144,1152]{4,3,2,1,0:T(8,128)(2,1)S(1)}, u32[]{:S(2)}) copy-start(bf16[1,4,2,144,1152]{4,3,2,1,0:T(8,128)(2,1)S(1)} %get-tuple-element.102) | copy-start | bytes 7962628
  109.1 5.8 copy-start.1
  109.7 8.0 %copy-start.13 = (bf16[512,1152]{1,0:T(8,128)(2,1)}, bf16[512,1152]{1,0:T(8,128)(2,1)S(1)}, u32[]{:S(2)}) copy-start(bf16[512,1152]{1,0:T(8,128)(2,1)S(1)} %fusion.16.refs_0_) | copy-start | bytes 3538948
  117.8 2.9 copy-start.69
  117.8 2.9 copy-start.58
  264.3 12.1 %copy-start.64 = (s32[256]{0:T(256)S(1)}, s32[256]{0:T(256)}, u32[]{:S(2)}) copy-start(s32[256]{0:T(256)} %param.32) | copy-start | bytes 3076
  264.4 12.1 %copy-start.65 = (s32[1,256]{1,0:T(1,128)S(1)}, s32[1,256]{1,0:T(1,128)}, u32[]{:S(2)}) copy-start(s32[1,256]{1,0:T(1,128)} %param.31) | copy-start | bytes 3076
  264.4 12.1 %copy-start.21 = (bf16[256,1152]{1,0:T(8,128)(2,1)S(1)}, bf16[256,1152]{1,0:T(8,128)(2,1)}, u32[]{:S(2)}) copy-start(bf16[256,1152]{1,0:T(8,128)(2,1)} %param.45) | copy-start | bytes 1769476
  264.4 12.1 %copy-start.22 = (bf16[1,256,1152]{2,1,0:T(8,128)(2,1)S(1)}, bf16[1,256,1152]{2,1,0:T(8,128)(2,1)}, u32[]{:S(2)}) copy-start(bf16[1,256,1152]{2,1,0:T(8,128)(2,1)} %param.44) | copy-start | bytes 1769476
  295.1 4.6 copy-start.70
  295.1 4.6 copy-start.66
  295.1 6.1 copy-start.55
  295.1 19.8 %slice-start = ((s8[9437184]{0:T(1024)(128)(4,1)}), s8[1048576]{0:T(1024)(128)(4,1)S(1)}, s32[]{:S(2)}) async-start(s8[9437184]{0:T(1024)(128)(4,1)} %bitcast.140), calls=%async_computation | async-start | bytes 2097152
  301.2 13.8 %slice-start.1 = ((s8[9437184]{0:T(1024)(128)(4,1)}), s8[4194304]{0:T(1024)(128)(4,1)S(1)}, s32[]{:S(2)}) async-start(s8[9437184]{0:T(1024)(128)(4,1)} %bitcast.140), calls=%async_computation.1 | async-start | bytes 8388608
  301.2 13.8 %slice-start.2 = ((s8[9437184]{0:T(1024)(128)(4,1)}), s8[4194304]{0:T(1024)(128)(4,1)S(1)}, s32[]{:S(2)}) async-start(s8[9437184]{0:T(1024)(128)(4,1)} %bitcast.140), calls=%async_computation.2 | async-start | bytes 8388608
  315.0 12.2 %copy-start.42 = (f32[8,144]{1,0:T(8,128)S(1)}, f32[8,144]{1,0:T(8,128)}, u32[]{:S(2)}) copy-start(f32[8,144]{1,0:T(8,128)} %get-tuple-element.122) | copy-start | bytes 13828
  327.3 14.8 %copy-start.2 = (f32[512,1152]{1,0:T(8,128)S(1)}, f32[512,1152]{1,0:T(8,128)}, u32[]{:S(2)}) copy-start(f32[512,1152]{1,0:T(8,128)} %get-tuple-element.44) | copy-start | bytes 7077892
  353.7 15.5 %copy-start.63 = (f32[16]{0:T(128)S(1)}, f32[16]{0:T(128)}, u32[]{:S(2)}) copy-start(f32[16]{0:T(128)} %get-tuple-element.126) | copy-start | bytes 196
  353.7 15.7 %copy-start.62 = (f32[16]{0:T(128)S(1)}, f32[16]{0:T(128)}, u32[]{:S(2)}) copy-start(f32[16]{0:T(128)} %get-tuple-element.127) | copy-start | bytes 196
  371.9 4.8 copy-start.20
  371.9 4.8 copy-start.67
  376.7 3.0 copy-start.11
  379.7 3.7 copy-start.24
  514.1 4.2 copy-start.18
  514.1 4.2 copy-start.27
  518.3 2.4 copy-start.28
  520.7 4.4 copy-start.23
  638.5 8.9 %copy-start.34 = (f32[8,16,128]{2,1,0:T(8,128)S(1)}, f32[8,16,128]{2,1,0:T(8,128)}, u32[]{:S(2)}) copy-start(f32[8,16,128]{2,1,0:T(8,128)} %exchange7.1) | copy-start | bytes 196612
  640.5 24.8 %collective-permute-start.1 = (bf16[144,1152]{1,0:T(8,128)(2,1)}, bf16[144,1152]{1,0:T(8,128)(2,1)}, u32[]{:S(2)}, u32[]{:S(2)}) collective-permute-start(bf16[144,1152]{1,0:T(8,128)(2,1)} %get-tuple-element.112), channel_id=1, source_target_pairs={{0,4},{1,5},{2,6},{3,7},{4,0},{5,1},{6,2},{7,3},{8,12},{9,13},{10,... | collective-permute-start | bytes 995336 | tf_op jit(solution)/shard_map/ppermute | solution.py:632
  642.2 23.1 %collective-permute-start.2 = (bf16[144,1152]{1,0:T(8,128)(2,1)}, bf16[144,1152]{1,0:T(8,128)(2,1)}, u32[]{:S(2)}, u32[]{:S(2)}) collective-permute-start(bf16[144,1152]{1,0:T(8,128)(2,1)} %get-tuple-element.113), channel_id=1, source_target_pairs={{0,6},{1,7},{2,4},{3,5},{4,2},{5,3},{6,0},{7,1},{8,14},{9,15},{10,... | collective-permute-start | bytes 995336 | tf_op jit(solution)/shard_map/ppermute | solution.py:632
  644.6 22.5 %collective-permute-start = (bf16[144,1152]{1,0:T(8,128)(2,1)S(1)}, bf16[144,1152]{1,0:T(8,128)(2,1)}, u32[]{:S(2)}, u32[]{:S(2)}) collective-permute-start(bf16[144,1152]{1,0:T(8,128)(2,1)S(1)} %dynamic-slice_bitcast_fusion.2), channel_id=1, source_target_pairs={{0,2},{1,3},{2,0},{3,1},{4,6},{5,7},{6,4},{7,5},{8,10},{9,11},{10,... | collective-permute-start | bytes 995336 | tf_op jit(solution)/shard_map/ppermute | solution.py:632
  645.1 6.1 copy-start.37
  646.3 5.6 copy-start.26
  653.9 2.9 copy-start.29
  655.6 2.9 copy-start.50
  655.6 2.9 copy-start.51
  668.8 10.3 %collective-permute-start.3 = (bf16[144,1152]{1,0:T(8,128)(2,1)S(1)}, bf16[144,1152]{1,0:T(8,128)(2,1)S(1)}, u32[]{:S(2)}, u32[]{:S(2)}) collective-permute-start(bf16[144,1152]{1,0:T(8,128)(2,1)S(1)} %get-tuple-element.88), channel_id=1, source_target_pairs={{0,8},{8,0},{16,24},{24,16},{1,9},{9,1},{17,25},{25,17},{2,10},{10... | collective-permute-start | bytes 995336 | tf_op jit(solution)/shard_map/ppermute | solution.py:632
  668.9 10.2 %collective-permute-start.4 = (bf16[144,1152]{1,0:T(8,128)(2,1)S(1)}, bf16[144,1152]{1,0:T(8,128)(2,1)S(1)}, u32[]{:S(2)}, u32[]{:S(2)}) collective-permute-start(bf16[144,1152]{1,0:T(8,128)(2,1)S(1)} %get-tuple-element.88), channel_id=1, source_target_pairs={{0,16},{8,24},{16,0},{24,8},{1,17},{9,25},{17,1},{25,9},{2,18},{10... | collective-permute-start | bytes 995336 | tf_op jit(solution)/shard_map/ppermute | solution.py:632
  679.1 1.6 collective-permute-start.5
  (32 other events, 42.5 us)
